TPU v7x, 768 devices: a whole 4x8x12 slice. The times are simulated.
768 devices in a mesh: dp: 24 (over x, z_lo), space: 32 (over z_hi, y, core).
Axes of the slice: x: 4, y: 8, z: 12 (z_hi: 2, z_lo: 6; z = z_hi * 6 + z_lo), core: 2. Of those that a mesh axis runs over, the one named last changes fastest.
Arguments:
- image: bfloat16 [24, 256, 10240], P('dp', 'space'), may hold values from -6 to 6
- cotangent: bfloat16 [24, 128, 5120], P('dp', 'space'), may hold values from -6 to 6
- weight: float32 [1440, 160], P('dp'), may hold values from -0.15625 to 0.15625
- moment_one: float32 [1440, 160], P('dp'), may hold values from -0.046875 to 0.046875
- moment_two: float32 [1440, 160], P('dp'), may hold values from 2.5431316e-06 to 4.0690105e-05
Outputs:
- output: bfloat16 [24, 128, 5120], P('dp', 'space')
- grad_image: bfloat16 [24, 256, 10240], P('dp', 'space')
- new_weight: float32 [1440, 160], P('dp')
- new_moment_one: float32 [1440, 160], P('dp')
- new_moment_two: float32 [1440, 160], P('dp')
All inputs are finite; a program needn't handle non-finite values.
Results may differ from a plain program's by a relative error of at most 0.0049.
Values may be sent and summed in bfloat16 or wider, within the bound.
No kernel may reach another device: no remote copies, remote signals or barrier semaphores. Data moves between devices by JAX's collectives and lax.ppermute only.
A program may use at most 32 MiB of HBM per device.

v0:
```python
import jax
import jax.numpy as jnp
from jax import lax
from jax.sharding import PartitionSpec as P

beta_one = 0.9
beta_two = 0.999
learn_rate = 0.01
decay_rate = 0.01
epsilon = 1e-08
adam_step = 10


def from_behind(block, axis, distance):
    devices = range(lax.axis_size(axis))
    route = [(i - distance, i) for i in devices if i - distance in devices]
    return lax.ppermute(block, axis, route)


def body(image, cotangent, weight, moment_one, moment_two):
    channels = weight.shape[1]
    samples, rows_here, merged = image.shape
    cols_here = merged // channels
    out_rows = rows_here // 2
    out_cols = cols_here // 2
    positions = samples * out_rows * out_cols
    above_flat = from_behind(image[:, rows_here - 1 : rows_here], "space", 1)
    above_row = above_flat.reshape(samples, 1, cols_here, channels)
    image_four = image.reshape(samples, rows_here, cols_here, channels)
    padded = jnp.concatenate([above_row, image_four], axis=1)
    padded = jnp.pad(padded, ((0, 0), (0, 0), (1, 1), (0, 0)))
    pieces = [
        padded[
            :, row_tap : row_tap + 2 * out_rows - 1 : 2, col_tap : col_tap + 2 * out_cols - 1 : 2, :
        ]
        for row_tap in range(3)
        for col_tap in range(3)
    ]
    patches = jnp.concatenate(pieces, axis=3).reshape(positions, 9 * channels)
    kernel_half = weight.astype(jnp.bfloat16)
    columns = patches
    forward = jnp.dot(
        columns,
        lax.all_gather(kernel_half, "dp", axis=0, tiled=True),
        preferred_element_type=jnp.float32,
    )
    output = forward.astype(jnp.bfloat16).reshape(samples, out_rows, out_cols * channels)
    used_rows = cotangent.shape[1]
    cotan_flat = cotangent.reshape(samples * used_rows * out_cols, channels)
    patch_grads = lax.dot_general(
        cotan_flat,
        lax.all_gather(kernel_half, "dp", axis=0, tiled=True),
        (((1,), (1,)), ((), ())),
        preferred_element_type=jnp.float32,
    )
    patch_grads = patch_grads.reshape(samples, used_rows, out_cols, 3, 3, channels)
    even_cols = patch_grads[:, :, :, :, 1, :]
    left_taps = patch_grads[:, :, :, :, 0, :]
    left_next = jnp.concatenate([left_taps[:, :, 1:], jnp.zeros_like(left_taps[:, :, 0:1])], axis=2)
    odd_cols = patch_grads[:, :, :, :, 2, :] + left_next
    by_column = jnp.stack([even_cols, odd_cols], axis=3).reshape(
        samples, used_rows, cols_here, 3, channels
    )
    even_rows = by_column[:, 0:out_rows, :, 1, :]
    upper_taps = by_column[:, :, :, 0, :]
    upper_next = jnp.concatenate(
        [upper_taps[:, 1:out_rows], jnp.zeros_like(upper_taps[:, 0:1])], axis=1
    )
    odd_rows = by_column[:, 0:out_rows, :, 2, :] + upper_next
    edge_flat = upper_taps[:, 0:1].reshape(samples, 1, cols_here * channels)
    sent_edge = from_behind(edge_flat, "space", -1)
    odd_rows = odd_rows.at[:, out_rows - 1 : out_rows].add(
        sent_edge.reshape(samples, 1, cols_here, channels)
    )
    grad_image = (
        jnp.stack([even_rows, odd_rows], axis=2)
        .reshape(samples, rows_here, cols_here * channels)
        .astype(jnp.bfloat16)
    )
    grad_flat = cotangent.reshape(positions, channels)
    columns = patches
    grad_shard = lax.psum_scatter(
        lax.dot_general(
            columns, grad_flat, (((0,), (0,)), ((), ())), preferred_element_type=jnp.float32
        ).astype(jnp.bfloat16),
        "dp",
        scatter_dimension=0,
        tiled=True,
    ).astype(jnp.float32)
    grad_shard = lax.psum(grad_shard.astype(jnp.bfloat16), "space").astype(jnp.float32)
    total_count = positions * lax.axis_size("dp") * lax.axis_size("space")
    gradient = grad_shard / float(total_count)
    new_moment_one = beta_one * moment_one + (1.0 - beta_one) * gradient
    new_moment_two = beta_two * moment_two + (1.0 - beta_two) * gradient * gradient
    first_hat = new_moment_one / (1.0 - beta_one**adam_step)
    second_hat = new_moment_two / (1.0 - beta_two**adam_step)
    new_weight = weight - learn_rate * (
        first_hat / (jnp.sqrt(second_hat) + epsilon) + decay_rate * weight
    )
    return (output, grad_image, new_weight, new_moment_one, new_moment_two)


def solution(mesh):
    in_specs = (
        P("dp", "space", None),
        P("dp", "space", None),
        P("dp", None),
        P("dp", None),
        P("dp", None),
    )
    out_specs = (
        P("dp", "space", None),
        P("dp", "space", None),
        P("dp", None),
        P("dp", None),
        P("dp", None),
    )
    return jax.shard_map(body, mesh=mesh, in_specs=in_specs, out_specs=out_specs, check_vma=False)
```

profile of v0, /device:TPU:57, one launch (start us, length us, event | category | flops | bytes accessed | tf_op | source)
XLA Modules:
  0.0 426.3 jit_solution(13313492466477628474)
XLA Ops:
  0.6 1.0 slice.87
  1.6 14.6 %collective-permute-start = (bf16[1,1,10240]{2,1,0:T(2,128)(2,1)S(1)}, bf16[1,1,10240]{2,1,0:T(2,128)(2,1)S(1)}, u32[]{:S(2)}, u32[]{:S(2)}) collective-permute-start(bf16[1,1,10240]{2,1,0:T(2,128)(2,1)S(1)} %slice.87), channel_id=1, source_target_pairs={{0,1},{1,2},{2,3},{3,4},{4,5},{5,6},{6,7},{7,8},{8,9},{9,10},{10,1... | collective-permute-start | bytes 61448 | tf_op jit(solution)/shard_map/ppermute | solution.py:17
  16.2 1.2 reshape.97
  17.5 0.9 reshape.104
  19.1 0.2 slice.90
  19.7 0.2 slice.93
  19.9 0.2 slice.94
  20.1 0.2 slice.95
  20.4 0.3 slice.96
  20.7 0.2 concatenate.15
  21.0 0.4 convolution_convert_fusion
  21.4 80.2 %fusion = bf16[64,160]{1,0:T(8,128)(2,1)S(1)} fusion(bf16[1440,160]{1,0:T(8,128)(2,1)S(1)} %convolution_convert_fusion), kind=kCustom, calls=%all-reduce-scatter | all-reduce-scatter fusion | flops 245761 | bytes 485376
  101.6 1.3 collective-permute-start.2
  103.0 1.3 collective-permute-start.3
  104.4 1.3 dynamic-slice.11
  106.3 0.4 concatenate.18
  106.8 214.9 %psum.7 = bf16[60,160]{1,0:T(8,128)(2,1)S(1)} all-reduce(bf16[60,160]{1,0:T(8,128)(2,1)S(1)} %constant_dynamic-slice_fusion), channel_id=1, replica_groups=mesh['dp'=24,'space'=32] {'space'}, use_global_device_ids=true, to_apply=%region_1.2 | all-reduce | flops 9600 | bytes 38400 | tf_op jit(solution)/shard_map/psum | solution.py:90
  321.6 0.7 multiply_subtract_fusion
  322.3 71.4 %all-gather = bf16[24,60,160]{2,1,0:T(8,128)(2,1)S(1)} all-gather(bf16[1,60,160]{2,1,0:T(8,128)(2,1)S(1)} %get-tuple-element.24), channel_id=1, replica_groups=mesh['dp'=24,'space'=32] {'dp'}, dimensions={0}, use_global_device_ids=true | all-gather | bytes 480000 | tf_op jit(solution)/shard_map/all_gather | solution.py:44
  393.8 0.3 reshape.110
  394.1 0.3 reshape.109
  394.4 0.4 convolution_bitcast_fusion
  395.0 0.5 copy.33
  395.8 0.4 convolution_convert_fusion.1
  396.4 5.0 %collective-permute-start.1 = (f32[1,1,10240]{2,1,0:T(1,128)S(1)}, f32[1,1,10240]{2,1,0:T(1,128)S(1)}, u32[]{:S(2)}, u32[]{:S(2)}) collective-permute-start(f32[1,1,10240]{2,1,0:T(1,128)S(1)} %reshape.102), channel_id=1, source_target_pairs={{1,0},{2,1},{3,2},{4,3},{5,4},{6,5},{7,6},{8,7},{9,8},{10,9},{11,1... | collective-permute-start | bytes 122888 | tf_op jit(solution)/shard_map/ppermute | solution.py:17
  401.7 0.8 reshape.99
  402.4 20.1 %collective-permute-done.1 = f32[1,1,10240]{2,1,0:T(1,128)S(1)} collective-permute-done((f32[1,1,10240]{2,1,0:T(1,128)S(1)}, f32[1,1,10240]{2,1,0:T(1,128)S(1)}, u32[]{:S(2)}, u32[]{:S(2)}) %collective-permute-start.1) | collective-permute-done | bytes 40992 | tf_op jit(solution)/shard_map/ppermute | solution.py:17
  422.5 0.5 broadcast.49
  423.0 0.7 reduce.8
  424.0 1.0 scatter-add.4
  425.1 0.2 pad_maximum_fusion.1
  425.3 1.0 convert_element_type.30
  (36 shorter events, 2.4 us)
Async XLA Ops:
  1.6 16.8 %collective-permute-start = (bf16[1,1,10240]{2,1,0:T(2,128)(2,1)S(1)}, bf16[1,1,10240]{2,1,0:T(2,128)(2,1)S(1)}, u32[]{:S(2)}, u32[]{:S(2)}) collective-permute-start(bf16[1,1,10240]{2,1,0:T(2,128)(2,1)S(1)} %slice.87), channel_id=1, source_target_pairs={{0,1},{1,2},{2,3},{3,4},{4,5},{5,6},{6,7},{7,8},{8,9},{9,10},{10,1... | collective-permute-start | bytes 61448 | tf_op jit(solution)/shard_map/ppermute | solution.py:17
  20.9 83.3 %copy-start = (bf16[1,4,5120]{2,1,0:T(4,128)(2,1)S(1)}, bf16[1,4,5120]{2,1,0:T(4,128)(2,1)}, u32[]{:S(2)}) copy-start(bf16[1,4,5120]{2,1,0:T(4,128)(2,1)} %param.8) | copy-start | bytes 122884
  21.0 300.7 %copy-start.1 = (f32[60,160]{1,0:T(8,128)S(1)}, f32[60,160]{1,0:T(8,128)}, u32[]{:S(2)}) copy-start(f32[60,160]{1,0:T(8,128)} %param.9) | copy-start | bytes 115204
  21.0 300.7 %copy-start.2 = (f32[60,160]{1,0:T(8,128)S(1)}, f32[60,160]{1,0:T(8,128)}, u32[]{:S(2)}) copy-start(f32[60,160]{1,0:T(8,128)} %param.10) | copy-start | bytes 115204
  21.0 300.7 %copy-start.3 = (f32[60,160]{1,0:T(8,128)S(1)}, f32[60,160]{1,0:T(8,128)}, u32[]{:S(2)}) copy-start(f32[60,160]{1,0:T(8,128)} %param.11) | copy-start | bytes 115204
  101.6 4.7 %collective-permute-start.2 = (bf16[64,160]{1,0:T(8,128)(2,1)S(1)}, bf16[64,160]{1,0:T(8,128)(2,1)S(1)}, u32[]{:S(2)}, u32[]{:S(2)}) collective-permute-start(bf16[64,160]{1,0:T(8,128)(2,1)S(1)} %fusion), channel_id=1, source_target_pairs={{0,32},{32,64},{64,96},{96,128},{128,160},{160,192},{192,224},{224... | collective-permute-start | bytes 61448
  103.0 3.4 collective-permute-start.3
  396.4 26.1 %collective-permute-start.1 = (f32[1,1,10240]{2,1,0:T(1,128)S(1)}, f32[1,1,10240]{2,1,0:T(1,128)S(1)}, u32[]{:S(2)}, u32[]{:S(2)}) collective-permute-start(f32[1,1,10240]{2,1,0:T(1,128)S(1)} %reshape.102), channel_id=1, source_target_pairs={{1,0},{2,1},{3,2},{4,3},{5,4},{6,5},{7,6},{8,7},{9,8},{10,9},{11,1... | collective-permute-start | bytes 122888 | tf_op jit(solution)/shard_map/ppermute | solution.py:17
where the time goes:
time: 427 us; the launch traced here: 426 us
  blocking collectives  367 us (86%)
  starting transfers between devices  22.2 us (5%)
  waiting for transfers between devices  20.1 us (5%)
  local copies, waits for them, and re-layouts  12.4 us (3%)
    psum x1, blocking collectives, body(): lax.psum(grad_shard.astype(jnp.bfloat16), 'space').astype(jnp.float32)  215 us
    unnamed x1, blocking collectives  80.2 us
    all_gather x1, blocking collectives, body(): lax.all_gather(kernel_half, 'dp', axis=0, tiled=True)  71.4 us
    ppermute x2, waiting for transfers between devices, from_behind(): return lax.ppermute(block, axis, route)  20.1 us
    ppermute x2, starting transfers between devices, from_behind(): return lax.ppermute(block, axis, route)  19.7 us
  transfers between devices with their start and end apart: 4, of which 1 were waited for; matrix products, arithmetic and copies ran while one was open for 1% of the time, Pallas kernels for 0%

commit v1 on v0

v1 whole, which is shorter than its diff:
```python
import jax
import jax.numpy as jnp
from jax import lax
from jax.experimental import pallas as pl
from jax.experimental.pallas import tpu as pltpu
from jax.sharding import Mesh
from jax.sharding import PartitionSpec as P

beta_one = 0.9
beta_two = 0.999
learn_rate = 0.01
decay_rate = 0.01
epsilon = 1e-08
adam_step = 10

C = 160
COUNT = 98304
F32 = jnp.float32
BF16 = jnp.bfloat16
VM = pl.BlockSpec(memory_space=pltpu.VMEM)
SM = pl.BlockSpec(memory_space=pltpu.SMEM)

PIECE = 40
GRAD_ROWS = 6 * PIECE
SEND_ONE = GRAD_ROWS + 32
SEND_TWO = PIECE + 80


def call(kernel, outs, scratch=(), flops=0, moved=0):
    return pl.pallas_call(
        kernel,
        out_shape=outs,
        scratch_shapes=list(scratch),
        cost_estimate=pl.CostEstimate(flops=flops, bytes_accessed=moved, transcendentals=0),
    )


def tile_rows(piece, wide, groups):
    tiles = []
    for g in range(groups):
        block = piece(wide, g)
        tiles += [block[:, 160 * k : 160 * k + 160] for k in range(4)]
    return tiles


def read_block(ref, g):
    return ref[:, 640 * g : 640 * g + 640].astype(F32)


def pack(rows):
    tail = rows[:, 128:160]
    side = jnp.concatenate([tail[8 * b : 8 * b + 8] for b in range(4)], axis=1)
    return jnp.concatenate([rows[:, 0:128], side], axis=0)


def unpack(piece):
    side = piece[32:40]
    tail = jnp.concatenate([side[:, 32 * b : 32 * b + 32] for b in range(4)], axis=0)
    return jnp.concatenate([piece[0:32], tail], axis=1)


def grad_kernel(
    where_ref, image_ref, cotan_ref, below_ref, weight_ref,
    send_ref, even_ref, odd_ref, taps_ref,
    five_ref, spread_ref, sums_ref, rows_ref,
):
    tiles = tile_rows(read_block, image_ref, 16)
    even = jnp.concatenate(tiles[0::2], axis=0).astype(BF16)
    odd = jnp.concatenate(tiles[1::2], axis=0).astype(BF16)
    even_ref[...] = even
    odd_ref[...] = odd
    five_ref[...] = jnp.zeros_like(five_ref)
    five_ref[0:4] = cotan_ref[...].astype(F32)
    five_ref[4:5] = below_ref[...].astype(F32)
    out_row = lax.broadcasted_iota(jnp.int32, (24, 8), 0)
    in_row = lax.broadcasted_iota(jnp.int32, (24, 8), 1)
    pick = (2 * in_row + out_row // 8 - 1 == out_row % 8).astype(F32).astype(BF16)
    spread_ref[...] = jnp.dot(pick, five_ref[...].astype(BF16), preferred_element_type=F32)
    taps = []
    for r in range(3):
        cols = tile_rows(lambda ref, g: ref[8 * r : 8 * r + 8, 640 * g : 640 * g + 640], spread_ref, 8)
        block = jnp.concatenate(cols, axis=0).astype(BF16)
        taps_ref[r] = block
        taps.append(block)
    zeros = jnp.zeros((8, C), BF16)

    def put(r, s, left, right):
        row = (3 * r + s) * C
        sums_ref[row : row + C] = lax.dot_general(
            left, right, (((0,), (0,)), ((), ())), preferred_element_type=F32
        )

    for r in range(3):
        put(r, 1, even, taps[r])
        put(r, 2, odd, taps[r])
        put(r, 0, odd[0:248], taps[r][8:256])
    sums_ref[1440:1448] = zeros.astype(F32)
    for x in range(4):
        for core in range(2):
            for low in range(6):
                start = 30 * (2 * (6 * x + low) + core)
                piece = pack(sums_ref[start : start + 32])
                send_ref[2 * x + core, PIECE * low : PIECE * low + PIECE] = piece.astype(BF16)
    rows_ref[0:60] = weight_ref[...]
    rows_ref[60:64] = jnp.zeros((4, C), F32)
    quarter = where_ref[0]
    mine = rows_ref[0:16]
    for q in range(1, 4):
        mine = jnp.where(quarter == q, rows_ref[15 * q : 15 * q + 16], mine)
    tail = mine[:, 128:160]
    lane = lax.broadcasted_iota(jnp.int32, (16, 128), 1) // 32
    tail = jnp.where(lane == where_ref[1], jnp.concatenate([tail] * 4, axis=1), 0.0)
    both = jnp.concatenate([mine[:, 0:128], tail], axis=0).astype(BF16)
    for n in range(8):
        send_ref[n, GRAD_ROWS:SEND_ONE] = both


def first_sum_kernel(where_ref, got_ref, send_ref):
    total = got_ref[0, 0:GRAD_ROWS].astype(F32)
    for n in range(1, 8):
        total = total + got_ref[n, 0:GRAD_ROWS].astype(F32)
    total = total.astype(BF16)
    core = where_ref[2]
    heads = [got_ref[2 * x + core, GRAD_ROWS : GRAD_ROWS + 16] for x in range(4)]
    tail = got_ref[core, GRAD_ROWS + 16 : SEND_ONE].astype(F32)
    for x in range(1, 4):
        tail = tail + got_ref[2 * x + core, GRAD_ROWS + 16 : SEND_ONE].astype(F32)
    tail = tail.astype(BF16)
    for low in range(6):
        for high in range(2):
            n = 2 * low + high
            send_ref[n, 0:PIECE] = total[PIECE * low : PIECE * low + PIECE]
            for x in range(4):
                send_ref[n, PIECE + 16 * x : PIECE + 16 * x + 16] = heads[x]
            send_ref[n, PIECE + 64 : SEND_TWO] = tail


def second_sum_kernel(got_ref, send_ref):
    total = got_ref[0, 0:PIECE].astype(F32)
    for n in range(1, 12):
        total = total + got_ref[n, 0:PIECE].astype(F32)
    total = total.astype(BF16)
    for n in range(16):
        send_ref[n] = total


def conv_kernel(
    where_ref, image_ref, above_ref, even_ref, odd_ref, taps_ref, own_ref, other_ref,
    out_ref, grad_ref,
    kernel_ref, shift_ref, roll_ref,
):
    core = where_ref[2]
    for x in range(4):
        for low in range(6):
            for c in range(2):
                for high in range(2):
                    n = 2 * low + high
                    own = own_ref[n, PIECE:SEND_TWO].astype(F32)
                    other = other_ref[n, PIECE:SEND_TWO].astype(F32)
                    block = jnp.where(core == c, own, other)
                    start = 60 * (6 * x + low) + 15 * (2 * c + high)
                    kernel_ref[start : start + 16] = jnp.concatenate(
                        [block[16 * x : 16 * x + 16], block[64:80, 32 * x : 32 * x + 32]], axis=1
                    )

    def tap(r, s):
        row = (3 * r + s) * C
        return kernel_ref[row : row + C].astype(BF16)

    def dot(left, right):
        return jnp.dot(left, right, preferred_element_type=F32)

    def dot_t(left, right):
        return lax.dot_general(left, right, (((1,), (1,)), ((), ())), preferred_element_type=F32)

    zeros = jnp.zeros((8, C), BF16)
    even = even_ref[...]
    odd = odd_ref[...]
    odd_before = jnp.concatenate([zeros, odd[0:248]], axis=0)
    shift_ref[0:1] = above_ref[...].astype(F32)
    shift_ref[1:9] = image_ref[...].astype(F32)
    tiles = tile_rows(lambda ref, g: ref[0:8, 640 * g : 640 * g + 640], shift_ref, 16)
    even_down = jnp.concatenate(tiles[0::2], axis=0).astype(BF16)
    odd_down = jnp.concatenate(tiles[1::2], axis=0).astype(BF16)
    odd_down_before = jnp.concatenate([zeros, odd_down[0:248]], axis=0)
    roll_ref[0:256] = dot(even, tap(2, 1)) + dot(odd, tap(2, 2)) + dot(odd_before, tap(2, 0))
    roll_ref[256:264] = jnp.zeros((8, C), F32)
    total = dot(even_down, tap(0, 1)) + dot(odd_down, tap(0, 2)) + dot(odd_down_before, tap(0, 0))
    total = total + dot(even, tap(1, 1)) + dot(odd, tap(1, 2)) + dot(odd_before, tap(1, 0))
    total = total + roll_ref[1:257]
    for g in range(8):
        wide = jnp.concatenate(
            [total[32 * g + 8 * k : 32 * g + 8 * k + 8] for k in range(4)], axis=1
        )
        rows = jnp.concatenate([wide[2 * i : 2 * i + 1] for i in range(4)], axis=0)
        out_ref[:, 640 * g : 640 * g + 640] = rows.astype(BF16)
    taps = [taps_ref[r] for r in range(3)]
    after = [jnp.concatenate([t[8:256], zeros], axis=0) for t in taps]
    grad_even = dot_t(taps[0], tap(0, 1)) + dot_t(taps[1], tap(1, 1)) + dot_t(taps[2], tap(2, 1))
    grad_odd = dot_t(taps[0], tap(0, 2)) + dot_t(taps[1], tap(1, 2)) + dot_t(taps[2], tap(2, 2))
    for r in range(3):
        grad_odd = grad_odd + dot_t(after[r], tap(r, 0))
    for g in range(16):
        parts = []
        for k in range(2):
            row = 16 * g + 8 * k
            parts += [grad_even[row : row + 8], grad_odd[row : row + 8]]
        grad_ref[:, 640 * g : 640 * g + 640] = jnp.concatenate(parts, axis=1).astype(BF16)


def adam_kernel(got_ref, weight_ref, one_ref, two_ref, new_weight_ref, new_one_ref, new_two_ref, sums_ref):
    for core in range(2):
        total = got_ref[core].astype(F32)
        for y in range(1, 8):
            total = total + got_ref[2 * y + core].astype(F32)
        sums_ref[30 * core : 30 * core + 32] = unpack(total)
    gradient = sums_ref[0:60] / float(COUNT)
    weight = weight_ref[...]
    new_one = beta_one * one_ref[...] + (1.0 - beta_one) * gradient
    new_two = beta_two * two_ref[...] + (1.0 - beta_two) * gradient * gradient
    first_hat = new_one / (1.0 - beta_one**adam_step)
    second_hat = new_two / (1.0 - beta_two**adam_step)
    new_weight_ref[...] = weight - learn_rate * (
        first_hat / (jnp.sqrt(second_hat) + epsilon) + decay_rate * weight
    )
    new_one_ref[...] = new_one
    new_two_ref[...] = new_two


def from_behind(block, distance):
    axes = ("zhi", "y", "core")
    route = [(i - distance, i) for i in range(32) if 0 <= i - distance < 32]
    return lax.ppermute(block, axes, route)


def body(image, cotangent, weight, moment_one, moment_two):
    shape = jax.ShapeDtypeStruct
    image = image.reshape(8, 64 * C)
    cotangent = cotangent.reshape(4, 32 * C)
    below = from_behind(cotangent[0:1], -1)
    above = from_behind(image[7:8], 1)
    core = lax.axis_index("core")
    place = jnp.stack([2 * core + lax.axis_index("zhi"), lax.axis_index("x"), core]).astype(jnp.int32)
    send_one, even, odd, taps = pl.pallas_call(
        grad_kernel,
        in_specs=[SM, VM, VM, VM, VM],
        out_specs=[VM] * 4,
        out_shape=[
            shape((8, SEND_ONE, 128), BF16),
            shape((256, C), BF16),
            shape((256, C), BF16),
            shape((3, 256, C), BF16),
        ],
        scratch_shapes=[
            pltpu.VMEM((8, 32 * C), F32),
            pltpu.VMEM((24, 32 * C), F32),
            pltpu.VMEM((1448, C), F32),
            pltpu.VMEM((64, C), F32),
        ],
        name="kernel_grad",
    )(place, image, cotangent, below, weight)
    got_one = lax.all_to_all(send_one, ("x", "core"), 0, 0, tiled=True)
    send_two = pl.pallas_call(
        first_sum_kernel,
        in_specs=[SM, VM],
        out_specs=VM,
        out_shape=shape((12, SEND_TWO, 128), BF16),
        name="first_sum",
    )(place, got_one)
    got_two = lax.all_to_all(send_two, ("zlo", "zhi"), 0, 0, tiled=True)
    other = lax.ppermute(got_two, "core", [(0, 1), (1, 0)])
    send_three = pl.pallas_call(
        second_sum_kernel,
        in_specs=[VM],
        out_specs=VM,
        out_shape=shape((16, PIECE, 128), BF16),
        name="second_sum",
    )(got_two)
    got_three = lax.all_to_all(send_three, ("y", "core"), 0, 0, tiled=True)
    output, grad_image = pl.pallas_call(
        conv_kernel,
        in_specs=[SM] + [VM] * 7,
        out_specs=[VM] * 2,
        out_shape=[shape((4, 32 * C), BF16), shape((8, 64 * C), BF16)],
        scratch_shapes=[
            pltpu.VMEM((1448, C), F32),
            pltpu.VMEM((16, 64 * C), F32),
            pltpu.VMEM((264, C), F32),
        ],
        name="conv_both",
    )(place, image, above, even, odd, taps, got_two, other)
    new_weight, new_one, new_two = pl.pallas_call(
        adam_kernel,
        in_specs=[VM] * 4,
        out_specs=[VM] * 3,
        out_shape=[shape((60, C), F32)] * 3,
        scratch_shapes=[pltpu.VMEM((64, C), F32)],
        name="adam",
    )(got_three, weight, moment_one, moment_two)
    return (output[None], grad_image[None], new_weight, new_one, new_two)


def solution(mesh):
    fine = Mesh(mesh.devices.reshape(4, 6, 2, 8, 2), ("x", "zlo", "zhi", "y", "core"))
    dp, space = ("x", "zlo"), ("zhi", "y", "core")
    specs = (P(dp, space, None), P(dp, space, None), P(dp, None), P(dp, None), P(dp, None))
    return jax.shard_map(body, mesh=fine, in_specs=specs, out_specs=specs, check_vma=False)
```

time: 427 us -> 87.5 us (0.20)
  blocking collectives: 367 us -> 38.8 us
  Pallas kernels: 0 us -> 11.1 us
  local copies, waits for them, and re-layouts: 12.4 us -> 3.76 us
  waiting for transfers between devices: 20.1 us -> 12.9 us
    psum x1 -> x0, blocking collectives: 215 us -> none  [body(): lax.psum(grad_shard.astype(jnp.bfloat16), 'space').astype(jnp.float32)]
    unnamed x1 -> x0, blocking collectives: 80.2 us -> none
    all_gather x1 -> x0, blocking collectives: 71.4 us -> none  [body(): lax.all_gather(kernel_half, 'dp', axis=0, tiled=True)]
    all_to_all x0 -> x2, blocking collectives: none -> 38.8 us  [the longest x1 24.2 us: body(): got_two = lax.all_to_all(send_two, ('zlo', 'zhi'), 0, 0, tiled=True)]
    pallas_call x0 -> x5, Pallas kernels: none -> 11.1 us  [the longest x1 3.06 us: body(): pl.pallas_call(conv_kernel, in_specs=[SM] + [VM] * 7, out_specs=[VM] * 2,...]
    ppermute x2 -> x3, starting transfers between devices: 19.7 us -> 11.9 us  [the longest x2 9.58 us: from_behind(): return lax.ppermute(block, axes, route)]
    ppermute x2 -> x3, waiting for transfers between devices: 20.1 us -> 12.9 us  [the longest x2 12.9 us: from_behind(): return lax.ppermute(block, axes, route)]
    all_to_all x0 -> x1, starting transfers between devices: none -> 6.41 us  [body(): got_three = lax.all_to_all(send_three, ('y', 'core'), 0, 0, tiled=True)]
  transfers between devices with their start and end apart: 4 -> 4, of which waited for: 1 -> 1; matrix products, arithmetic and copies ran while one was open for 1% -> 2% of each run, Pallas kernels for 0% -> 2%
where the time goes in v1:
time: 87.5 us; the launch traced here: 86.2 us
  blocking collectives  38.8 us (44%)
  starting transfers between devices  18.3 us (21%)
  waiting for transfers between devices  12.9 us (15%)
  Pallas kernels  11.1 us (13%)
  local copies, waits for them, and re-layouts  3.76 us (4%)
    all_to_all x1, blocking collectives, body(): got_two = lax.all_to_all(send_two, ('zlo', 'zhi'), 0, 0, tiled=True)  24.2 us
    all_to_all x1, blocking collectives, body(): got_one = lax.all_to_all(send_one, ('x', 'core'), 0, 0, tiled=True)  14.7 us
    ppermute x2, waiting for transfers between devices, from_behind(): return lax.ppermute(block, axes, route)  12.9 us
    ppermute x2, starting transfers between devices, from_behind(): return lax.ppermute(block, axes, route)  9.58 us
    all_to_all x1, starting transfers between devices, body(): got_three = lax.all_to_all(send_three, ('y', 'core'), 0, 0, tiled=True)  6.41 us
    pallas_call x1, Pallas kernels, body(): pl.pallas_call(conv_kernel, in_specs=[SM] + [VM] * 7, out_specs=[VM] * 2,...  3.06 us
    pallas_call x1, Pallas kernels, body(): pl.pallas_call(grad_kernel, in_specs=[SM, VM, VM, VM, VM], out_specs=[VM]...  2.67 us
    ppermute x1, starting transfers between devices, body(): other = lax.ppermute(got_two, 'core', [(0, 1), (1, 0)])  2.3 us
  transfers between devices with their start and end apart: 4, of which 1 were waited for; matrix products, arithmetic and copies ran while one was open for 2% of the time, Pallas kernels for 2%

profile of v1, /device:TPU:57, one launch (start us, length us, event | category | flops | bytes accessed | tf_op | source)
XLA Modules:
  0.0 86.2 jit_solution(3750391975181828569)
XLA Ops:
  0.6 0.8 slice_bitcast_fusion.1
  1.4 2.6 %collective-permute-start.1 = (bf16[1,5120]{1,0:T(2,128)(2,1)S(1)}, bf16[1,5120]{1,0:T(2,128)(2,1)S(1)}, u32[]{:S(2)}, u32[]{:S(2)}) collective-permute-start(bf16[1,5120]{1,0:T(2,128)(2,1)S(1)} %slice_bitcast_fusion.1), channel_id=1, source_target_pairs={{1,0},{2,1},{3,2},{4,3},{5,4},{6,5},{7,6},{8,7},{9,8},{10,9},{11,1... | collective-permute-start | bytes 30728 | tf_op jit(solution)/shard_map/ppermute | solution.py:233
  4.0 0.6 pad_add_fusion.where_ref
  4.6 12.9 %collective-permute-done.1.below_ref = bf16[1,5120]{1,0:T(2,128)(2,1)S(1)} collective-permute-done((bf16[1,5120]{1,0:T(2,128)(2,1)S(1)}, bf16[1,5120]{1,0:T(2,128)(2,1)S(1)}, u32[]{:S(2)}, u32[]{:S(2)}) %collective-permute-start.1) | collective-permute-done | bytes 10272 | tf_op jit(solution)/shard_map/ppermute | solution.py:233
  17.5 0.0 copy-start.4
  17.5 0.6 copy-done.4
  18.1 2.7 %kernel_grad.1 = (bf16[8,272,128]{2,1,0:T(8,128)(2,1)}, bf16[256,160]{1,0:T(8,128)(2,1)}, bf16[256,160]{1,0:T(8,128)(2,1)}, bf16[3,256,160]{2,1,0:T(8,128)(2,1)}) custom-call(s32[3]{0:T(128)} %pad_add_fusion.where_ref, bf16[8,10240]{1,0:T(8,128)(2,1)} %bitcast.11, bf16[4,5120]{1,0:T(4,128)(2,1)} %bitcast.13, bf16[1,5120]{1,0:T(2,128)(2,1)} %copy-done.4, ...), custom_call_target="tpu_custom_call" | custom-call | tf_op jit(solution)/shard_map/kernel_grad/pallas_call | solution.py:244
  20.8 14.7 %all_to_all.15.got_ref = bf16[8,272,128]{2,1,0:T(8,128)(2,1)} all-to-all(bf16[8,272,128]{2,1,0:T(8,128)(2,1)} %get-tuple-element.17), channel_id=1, replica_groups=mesh['x'=4,'zlo'=6,'zhi'=2,'y'=8,'core'=2] {'x','core'}, dimensions={0} | all-to-all | bytes 1114112 | tf_op jit(solution)/shard_map/all_to_all | solution.py:262
  35.5 1.9 %first_sum.1 = bf16[12,120,128]{2,1,0:T(8,128)(2,1)} custom-call(s32[3]{0:T(128)} %pad_add_fusion.where_ref, bf16[8,272,128]{2,1,0:T(8,128)(2,1)} %all_to_all.15.got_ref), custom_call_target="tpu_custom_call" | custom-call | tf_op jit(solution)/shard_map/first_sum/pallas_call | solution.py:263
  37.3 24.2 %all_to_all.16.own_ref.got_ref = bf16[12,120,128]{2,1,0:T(8,128)(2,1)} all-to-all(bf16[12,120,128]{2,1,0:T(8,128)(2,1)} %first_sum.1), channel_id=1, replica_groups=mesh['x'=4,'zlo'=6,'zhi'=2,'y'=8,'core'=2] {'zlo','zhi'}, dimensions={0} | all-to-all | bytes 737280 | tf_op jit(solution)/shard_map/all_to_all | solution.py:270
  61.5 0.0 copy-start
  61.5 1.8 %second_sum.1 = bf16[16,40,128]{2,1,0:T(8,128)(2,1)} custom-call(bf16[12,120,128]{2,1,0:T(8,128)(2,1)} %all_to_all.16.own_ref.got_ref), custom_call_target="tpu_custom_call" | custom-call | tf_op jit(solution)/shard_map/second_sum/pallas_call | solution.py:272
  63.3 6.4 %all-to-all-start.2 = ((bf16[16,40,128]{2,1,0:T(8,128)(2,1)}), bf16[16,40,128]{2,1,0:T(8,128)(2,1)S(1)}, u32[]{:S(2)}, u32[]{:S(2)}) async-start(bf16[16,40,128]{2,1,0:T(8,128)(2,1)} %second_sum.1), calls=%async_computation.2 | async-start | bytes 327680 | tf_op jit(solution)/shard_map/all_to_all | solution.py:279
  69.7 0.0 copy-done
  69.7 2.3 %collective-permute-start.2 = (bf16[12,120,128]{2,1,0:T(8,128)(2,1)S(1)}, bf16[12,120,128]{2,1,0:T(8,128)(2,1)S(1)}, u32[]{:S(2)}, u32[]{:S(2)}) collective-permute-start(bf16[12,120,128]{2,1,0:T(8,128)(2,1)S(1)} %copy-done), channel_id=1, source_target_pairs={{0,1},{1,0},{2,3},{3,2},{4,5},{5,4},{6,7},{7,6},{8,9},{9,8},{10,11... | collective-permute-start | bytes 1105928 | tf_op jit(solution)/shard_map/ppermute | solution.py:271
  72.0 1.0 %slice_bitcast_fusion = bf16[1,10240]{1,0:T(2,128)(2,1)S(1)} fusion(bf16[1,8,10240]{2,1,0:T(8,128)(2,1)} %param.5), kind=kLoop, calls=%fused_computation | loop fusion | bytes 40960 | tf_op jit(solution)/shard_map/slice | solution.py:241
  73.0 7.0 %collective-permute-start = (bf16[1,10240]{1,0:T(2,128)(2,1)S(1)}, bf16[1,10240]{1,0:T(2,128)(2,1)S(1)}, u32[]{:S(2)}, u32[]{:S(2)}) collective-permute-start(bf16[1,10240]{1,0:T(2,128)(2,1)S(1)} %slice_bitcast_fusion), channel_id=1, source_target_pairs={{0,1},{1,2},{2,3},{3,4},{4,5},{5,6},{6,7},{7,8},{8,9},{9,10},{10,1... | collective-permute-start | bytes 61448 | tf_op jit(solution)/shard_map/ppermute | solution.py:233
  80.0 0.0 all-to-all-done.2.got_ref
  80.0 0.0 copy-start.1
  80.0 0.7 copy-done.1
  80.7 1.7 %adam.1 = (f32[60,160]{1,0:T(8,128)}, f32[60,160]{1,0:T(8,128)}, f32[60,160]{1,0:T(8,128)}) custom-call(bf16[16,40,128]{2,1,0:T(8,128)(2,1)} %copy-done.1, f32[60,160]{1,0:T(8,128)} %weight_ref.3, f32[60,160]{1,0:T(8,128)} %one_ref.1, f32[60,160]{1,0:T(8,128)} %two_ref.1), custom_call_target="tpu_custom_call" | custom-call | tf_op jit(solution)/shard_map/adam/pallas_call | solution.py:292
  82.4 0.0 collective-permute-done.above_ref
  82.4 0.0 copy-start.3
  82.4 0.0 collective-permute-done.2.other_ref
  82.4 0.0 copy-start.2
  82.4 0.6 copy-done.3
  83.0 0.1 copy-done.2
  83.2 3.1 %conv_both.1 = (bf16[4,5120]{1,0:T(4,128)(2,1)}, bf16[8,10240]{1,0:T(8,128)(2,1)}) custom-call(s32[3]{0:T(128)} %pad_add_fusion.where_ref, bf16[8,10240]{1,0:T(8,128)(2,1)} %bitcast.12, bf16[1,10240]{1,0:T(2,128)(2,1)} %copy-done.3, bf16[256,160]{1,0:T(8,128)(2,1)} %get-tuple-element.14.even_ref, bf16[256,160]{1,0:T(8,128)(2,1)} %get-tuple-element.15.odd_ref, ...), custom_call_target="tpu_custom_call" | custom-call | tf_op jit(solution)/shard_map/conv_both/pallas_call | solution.py:280
Async XLA Ops:
  1.4 16.1 %collective-permute-start.1 = (bf16[1,5120]{1,0:T(2,128)(2,1)S(1)}, bf16[1,5120]{1,0:T(2,128)(2,1)S(1)}, u32[]{:S(2)}, u32[]{:S(2)}) collective-permute-start(bf16[1,5120]{1,0:T(2,128)(2,1)S(1)} %slice_bitcast_fusion.1), channel_id=1, source_target_pairs={{1,0},{2,1},{3,2},{4,3},{5,4},{6,5},{7,6},{8,7},{9,8},{10,9},{11,1... | collective-permute-start | bytes 30728 | tf_op jit(solution)/shard_map/ppermute | solution.py:233
  17.5 0.6 copy-start.4
  61.5 8.2 %copy-start = (bf16[12,120,128]{2,1,0:T(8,128)(2,1)S(1)}, bf16[12,120,128]{2,1,0:T(8,128)(2,1)}, u32[]{:S(2)}) copy-start(bf16[12,120,128]{2,1,0:T(8,128)(2,1)} %all_to_all.16.own_ref.got_ref) | copy-start | bytes 1105924
  63.3 16.7 %all-to-all-start.2 = ((bf16[16,40,128]{2,1,0:T(8,128)(2,1)}), bf16[16,40,128]{2,1,0:T(8,128)(2,1)S(1)}, u32[]{:S(2)}, u32[]{:S(2)}) async-start(bf16[16,40,128]{2,1,0:T(8,128)(2,1)} %second_sum.1), calls=%async_computation.2 | async-start | bytes 327680 | tf_op jit(solution)/shard_map/all_to_all | solution.py:279
  69.7 12.7 %collective-permute-start.2 = (bf16[12,120,128]{2,1,0:T(8,128)(2,1)S(1)}, bf16[12,120,128]{2,1,0:T(8,128)(2,1)S(1)}, u32[]{:S(2)}, u32[]{:S(2)}) collective-permute-start(bf16[12,120,128]{2,1,0:T(8,128)(2,1)S(1)} %copy-done), channel_id=1, source_target_pairs={{0,1},{1,0},{2,3},{3,2},{4,5},{5,4},{6,7},{7,6},{8,9},{9,8},{10,11... | collective-permute-start | bytes 1105928 | tf_op jit(solution)/shard_map/ppermute | solution.py:271
  73.0 9.4 %collective-permute-start = (bf16[1,10240]{1,0:T(2,128)(2,1)S(1)}, bf16[1,10240]{1,0:T(2,128)(2,1)S(1)}, u32[]{:S(2)}, u32[]{:S(2)}) collective-permute-start(bf16[1,10240]{1,0:T(2,128)(2,1)S(1)} %slice_bitcast_fusion), channel_id=1, source_target_pairs={{0,1},{1,2},{2,3},{3,4},{4,5},{5,6},{6,7},{7,8},{8,9},{9,10},{10,1... | collective-permute-start | bytes 61448 | tf_op jit(solution)/shard_map/ppermute | solution.py:233
  80.0 0.7 copy-start.1
  82.4 0.6 copy-start.3
  82.4 0.7 copy-start.2

commit v2 on v1

--- a/solution.py
+++ b/solution.py
@@ -6,6 +6,7 @@
 from jax.sharding import Mesh
 from jax.sharding import PartitionSpec as P
 
+
 beta_one = 0.9
 beta_two = 0.999
 learn_rate = 0.01
@@ -18,7 +19,6 @@
 F32 = jnp.float32
 BF16 = jnp.bfloat16
 VM = pl.BlockSpec(memory_space=pltpu.VMEM)
-SM = pl.BlockSpec(memory_space=pltpu.SMEM)
 
 PIECE = 40
 GRAD_ROWS = 6 * PIECE
@@ -26,12 +26,14 @@
 SEND_TWO = PIECE + 80
 
 
-def call(kernel, outs, scratch=(), flops=0, moved=0):
+def call(kernel, outs, scratch=(), limit=16):
+    one = not isinstance(outs, list)
     return pl.pallas_call(
         kernel,
         out_shape=outs,
+        out_specs=VM if one else [VM] * len(outs),
         scratch_shapes=list(scratch),
-        cost_estimate=pl.CostEstimate(flops=flops, bytes_accessed=moved, transcendentals=0),
+        compiler_params=pltpu.CompilerParams(vmem_limit_bytes=limit << 20),
     )
 
 
@@ -60,7 +62,7 @@
 
 
 def grad_kernel(
-    where_ref, image_ref, cotan_ref, below_ref, weight_ref,
+    image_ref, cotan_ref, below_ref, weight_ref,
     send_ref, even_ref, odd_ref, taps_ref,
     five_ref, spread_ref, sums_ref, rows_ref,
 ):
@@ -103,24 +105,24 @@
                 send_ref[2 * x + core, PIECE * low : PIECE * low + PIECE] = piece.astype(BF16)
     rows_ref[0:60] = weight_ref[...]
     rows_ref[60:64] = jnp.zeros((4, C), F32)
-    quarter = where_ref[0]
+    quarter = 2 * lax.axis_index("core") + lax.axis_index("zhi")
     mine = rows_ref[0:16]
     for q in range(1, 4):
         mine = jnp.where(quarter == q, rows_ref[15 * q : 15 * q + 16], mine)
     tail = mine[:, 128:160]
     lane = lax.broadcasted_iota(jnp.int32, (16, 128), 1) // 32
-    tail = jnp.where(lane == where_ref[1], jnp.concatenate([tail] * 4, axis=1), 0.0)
+    tail = jnp.where(lane == lax.axis_index("x"), jnp.concatenate([tail] * 4, axis=1), 0.0)
     both = jnp.concatenate([mine[:, 0:128], tail], axis=0).astype(BF16)
     for n in range(8):
         send_ref[n, GRAD_ROWS:SEND_ONE] = both
 
 
-def first_sum_kernel(where_ref, got_ref, send_ref):
+def first_sum_kernel(got_ref, send_ref):
     total = got_ref[0, 0:GRAD_ROWS].astype(F32)
     for n in range(1, 8):
         total = total + got_ref[n, 0:GRAD_ROWS].astype(F32)
     total = total.astype(BF16)
-    core = where_ref[2]
+    core = lax.axis_index("core")
     heads = [got_ref[2 * x + core, GRAD_ROWS : GRAD_ROWS + 16] for x in range(4)]
     tail = got_ref[core, GRAD_ROWS + 16 : SEND_ONE].astype(F32)
     for x in range(1, 4):
@@ -145,11 +147,11 @@
 
 
 def conv_kernel(
-    where_ref, image_ref, above_ref, even_ref, odd_ref, taps_ref, own_ref, other_ref,
+    image_ref, above_ref, even_ref, odd_ref, taps_ref, own_ref, other_ref,
     out_ref, grad_ref,
     kernel_ref, shift_ref, roll_ref,
 ):
-    core = where_ref[2]
+    core = lax.axis_index("core")
     for x in range(4):
         for low in range(6):
             for c in range(2):
@@ -239,63 +241,38 @@
     cotangent = cotangent.reshape(4, 32 * C)
     below = from_behind(cotangent[0:1], -1)
     above = from_behind(image[7:8], 1)
-    core = lax.axis_index("core")
-    place = jnp.stack([2 * core + lax.axis_index("zhi"), lax.axis_index("x"), core]).astype(jnp.int32)
-    send_one, even, odd, taps = pl.pallas_call(
+    send_one, even, odd, taps = call(
         grad_kernel,
-        in_specs=[SM, VM, VM, VM, VM],
-        out_specs=[VM] * 4,
-        out_shape=[
+        [
             shape((8, SEND_ONE, 128), BF16),
             shape((256, C), BF16),
             shape((256, C), BF16),
             shape((3, 256, C), BF16),
         ],
-        scratch_shapes=[
+        [
             pltpu.VMEM((8, 32 * C), F32),
             pltpu.VMEM((24, 32 * C), F32),
             pltpu.VMEM((1448, C), F32),
             pltpu.VMEM((64, C), F32),
         ],
-        name="kernel_grad",
-    )(place, image, cotangent, below, weight)
+    )(image, cotangent, below, weight)
     got_one = lax.all_to_all(send_one, ("x", "core"), 0, 0, tiled=True)
-    send_two = pl.pallas_call(
-        first_sum_kernel,
-        in_specs=[SM, VM],
-        out_specs=VM,
-        out_shape=shape((12, SEND_TWO, 128), BF16),
-        name="first_sum",
-    )(place, got_one)
+    send_two = call(first_sum_kernel, shape((12, SEND_TWO, 128), BF16))(got_one)
     got_two = lax.all_to_all(send_two, ("zlo", "zhi"), 0, 0, tiled=True)
     other = lax.ppermute(got_two, "core", [(0, 1), (1, 0)])
-    send_three = pl.pallas_call(
-        second_sum_kernel,
-        in_specs=[VM],
-        out_specs=VM,
-        out_shape=shape((16, PIECE, 128), BF16),
-        name="second_sum",
-    )(got_two)
+    send_three = call(second_sum_kernel, shape((16, PIECE, 128), BF16))(got_two)
     got_three = lax.all_to_all(send_three, ("y", "core"), 0, 0, tiled=True)
-    output, grad_image = pl.pallas_call(
+    output, grad_image = call(
         conv_kernel,
-        in_specs=[SM] + [VM] * 7,
-        out_specs=[VM] * 2,
-        out_shape=[shape((4, 32 * C), BF16), shape((8, 64 * C), BF16)],
-        scratch_shapes=[
+        [shape((4, 32 * C), BF16), shape((8, 64 * C), BF16)],
+        [
             pltpu.VMEM((1448, C), F32),
             pltpu.VMEM((16, 64 * C), F32),
             pltpu.VMEM((264, C), F32),
         ],
-        name="conv_both",
-    )(place, image, above, even, odd, taps, got_two, other)
-    new_weight, new_one, new_two = pl.pallas_call(
-        adam_kernel,
-        in_specs=[VM] * 4,
-        out_specs=[VM] * 3,
-        out_shape=[shape((60, C), F32)] * 3,
-        scratch_shapes=[pltpu.VMEM((64, C), F32)],
-        name="adam",
+    )(image, above, even, odd, taps, got_two, other)
+    new_weight, new_one, new_two = call(
+        adam_kernel, [shape((60, C), F32)] * 3, [pltpu.VMEM((64, C), F32)]
     )(got_three, weight, moment_one, moment_two)
     return (output[None], grad_image[None], new_weight, new_one, new_two)
 
@@ -304,4 +281,5 @@
     fine = Mesh(mesh.devices.reshape(4, 6, 2, 8, 2), ("x", "zlo", "zhi", "y", "core"))
     dp, space = ("x", "zlo"), ("zhi", "y", "core")
     specs = (P(dp, space, None), P(dp, space, None), P(dp, None), P(dp, None), P(dp, None))
+
     return jax.shard_map(body, mesh=fine, in_specs=specs, out_specs=specs, check_vma=False)

time: 87.5 us -> 79.8 us (0.912)
  the two profiles are of different devices: /device:TPU:57 before, /device:TPU:1 now
where the time goes in v2:
time: 79.8 us; the launch traced here: 79.3 us
  blocking collectives  37.3 us (47%)
  starting transfers between devices  29.8 us (37%)
  waiting for transfers between devices  4.57 us (6%)
  Pallas kernels  4.16 us (5%)
  local copies, waits for them, and re-layouts  2.68 us (3%)
    all_to_all x1, blocking collectives, body(): got_two = lax.all_to_all(send_two, ('zlo', 'zhi'), 0, 0, tiled=True)  24.5 us
    ppermute x2, starting transfers between devices, from_behind(): return lax.ppermute(block, axes, route)  15.9 us
    all_to_all x1, blocking collectives, body(): got_one = lax.all_to_all(send_one, ('x', 'core'), 0, 0, tiled=True)  12.9 us
    all_to_all x1, starting transfers between devices, body(): got_three = lax.all_to_all(send_three, ('y', 'core'), 0, 0, tiled=True)  11.7 us
    all_to_all x1, waiting for transfers between devices, body(): got_three = lax.all_to_all(send_three, ('y', 'core'), 0, 0, tiled=True)  3.75 us
    ppermute x1, starting transfers between devices, body(): other = lax.ppermute(got_two, 'core', [(0, 1), (1, 0)])  2.14 us
    unnamed x14, local copies, waits for them, and re-layouts  1.77 us
    pallas_call x1, Pallas kernels, body(): call(conv_kernel, [shape((4, 32 * C), BF16), shape((8, 64 * C), BF16)], [...  1.71 us
  transfers between devices with their start and end apart: 4, of which 2 were waited for; matrix products, arithmetic and copies ran while one was open for 0% of the time, Pallas kernels for 1%

profile of v2, /device:TPU:1, one launch (start us, length us, event | category | flops | bytes accessed | tf_op | source)
XLA Modules:
  0.0 79.3 jit_solution(4745352221793446958)
XLA Ops:
  0.6 0.0 copy-start.4
  0.6 0.9 %slice_bitcast_fusion.1 = bf16[1,5120]{1,0:T(2,128)(2,1)S(1)} fusion(bf16[1,4,5120]{2,1,0:T(4,128)(2,1)} %param.6), kind=kLoop, calls=%fused_computation.1 | loop fusion | bytes 20480 | tf_op jit(solution)/shard_map/slice | solution.py:242
  1.5 12.4 %collective-permute-start.1 = (bf16[1,5120]{1,0:T(2,128)(2,1)S(1)}, bf16[1,5120]{1,0:T(2,128)(2,1)S(1)}, u32[]{:S(2)}, u32[]{:S(2)}) collective-permute-start(bf16[1,5120]{1,0:T(2,128)(2,1)S(1)} %slice_bitcast_fusion.1), channel_id=1, source_target_pairs={{1,0},{2,1},{3,2},{4,3},{5,4},{6,5},{7,6},{8,7},{9,8},{10,9},{11,1... | collective-permute-start | bytes 30728 | tf_op jit(solution)/shard_map/ppermute | solution.py:235
  13.9 0.8 %collective-permute-done.1.below_ref = bf16[1,5120]{1,0:T(2,128)(2,1)S(1)} collective-permute-done((bf16[1,5120]{1,0:T(2,128)(2,1)S(1)}, bf16[1,5120]{1,0:T(2,128)(2,1)S(1)}, u32[]{:S(2)}, u32[]{:S(2)}) %collective-permute-start.1) | collective-permute-done | bytes 10272 | tf_op jit(solution)/shard_map/ppermute | solution.py:235
  14.7 0.0 copy-done.4
  14.7 0.0 copy-start
  14.7 0.9 %copy-done = bf16[1,8,10240]{2,1,0:T(8,128)(2,1)S(1)} copy-done((bf16[1,8,10240]{2,1,0:T(8,128)(2,1)S(1)}, bf16[1,8,10240]{2,1,0:T(8,128)(2,1)}, u32[]{:S(2)}) %copy-start) | copy-done | bytes 163864
  15.6 0.0 copy-start.2
  15.6 0.8 %copy-done.2 = f32[60,160]{1,0:T(8,128)S(1)} copy-done((f32[60,160]{1,0:T(8,128)S(1)}, f32[60,160]{1,0:T(8,128)}, u32[]{:S(2)}) %copy-start.2) | copy-done | bytes 38424
  16.5 0.9 %shard_map.92 = (bf16[8,272,128]{2,1,0:T(8,128)(2,1)S(1)}, bf16[256,160]{1,0:T(8,128)(2,1)S(1)}, bf16[256,160]{1,0:T(8,128)(2,1)S(1)}, bf16[3,256,160]{2,1,0:T(8,128)(2,1)S(1)}) custom-call(bf16[8,10240]{1,0:T(8,128)(2,1)S(1)} %bitcast.8, bf16[4,5120]{1,0:T(4,128)(2,1)S(1)} %bitcast.10, bf16[1,5120]{1,0:T(2,128)(2,1)S(1)} %collective-permute-done.1.below_ref, ...), custom_call_target="tpu_custom_call" | custom-call | tf_op jit(solution)/shard_map/pallas_call | solution.py:244
  17.4 12.9 %all_to_all.15.got_ref = bf16[8,272,128]{2,1,0:T(8,128)(2,1)S(1)} all-to-all(bf16[8,272,128]{2,1,0:T(8,128)(2,1)S(1)} %get-tuple-element.17), channel_id=1, replica_groups=mesh['x'=4,'zlo'=6,'zhi'=2,'y'=8,'core'=2] {'x','core'}, dimensions={0} | all-to-all | bytes 1114112 | tf_op jit(solution)/shard_map/all_to_all | solution.py:259
  30.2 0.1 shard_map.93
  30.3 24.5 %all_to_all.16.own_ref.got_ref = bf16[12,120,128]{2,1,0:T(8,128)(2,1)S(1)} all-to-all(bf16[12,120,128]{2,1,0:T(8,128)(2,1)S(1)} %shard_map.93), channel_id=1, replica_groups=mesh['x'=4,'zlo'=6,'zhi'=2,'y'=8,'core'=2] {'zlo','zhi'}, dimensions={0} | all-to-all | bytes 737280 | tf_op jit(solution)/shard_map/all_to_all | solution.py:261
  54.8 0.7 shard_map.95
  55.5 0.0 copy-start.1
  55.5 0.0 copy-start.5
  55.5 0.0 copy-start.6
  55.5 11.7 %all-to-all-start.2 = ((bf16[16,40,128]{2,1,0:T(8,128)(2,1)}), bf16[16,40,128]{2,1,0:T(8,128)(2,1)S(1)}, u32[]{:S(2)}, u32[]{:S(2)}) async-start(bf16[16,40,128]{2,1,0:T(8,128)(2,1)} %shard_map.95), calls=%async_computation.2 | async-start | bytes 327680 | tf_op jit(solution)/shard_map/all_to_all | solution.py:264
  67.2 0.0 copy-start.3
  67.3 2.1 %collective-permute-start.2 = (bf16[12,120,128]{2,1,0:T(8,128)(2,1)S(1)}, bf16[12,120,128]{2,1,0:T(8,128)(2,1)S(1)}, u32[]{:S(2)}, u32[]{:S(2)}) collective-permute-start(bf16[12,120,128]{2,1,0:T(8,128)(2,1)S(1)} %all_to_all.16.own_ref.got_ref), channel_id=1, source_target_pairs={{0,1},{1,0},{2,3},{3,2},{4,5},{5,4},{6,7},{7,6},{8,9},{9,8},{10,11... | collective-permute-start | bytes 1105928 | tf_op jit(solution)/shard_map/ppermute | solution.py:262
  69.4 0.0 copy-done.1
  69.5 3.6 %collective-permute-start = (bf16[1,10240]{1,0:T(2,128)(2,1)S(1)}, bf16[1,10240]{1,0:T(2,128)(2,1)S(1)}, u32[]{:S(2)}, u32[]{:S(2)}) collective-permute-start(bf16[1,10240]{1,0:T(2,128)(2,1)S(1)} %slice_bitcast_fusion), channel_id=1, source_target_pairs={{0,1},{1,2},{2,3},{3,4},{4,5},{5,6},{6,7},{7,8},{8,9},{9,10},{10,1... | collective-permute-start | bytes 61448 | tf_op jit(solution)/shard_map/ppermute | solution.py:235
  73.0 3.7 %all-to-all-done.2.got_ref = bf16[16,40,128]{2,1,0:T(8,128)(2,1)S(1)} async-done(((bf16[16,40,128]{2,1,0:T(8,128)(2,1)}), bf16[16,40,128]{2,1,0:T(8,128)(2,1)S(1)}, u32[]{:S(2)}, u32[]{:S(2)}) %all-to-all-start.2) | async-done | bytes 163872 | tf_op jit(solution)/shard_map/all_to_all | solution.py:264
  76.8 0.0 copy-done.5
  76.8 0.0 copy-done.6
  76.8 0.0 copy-done.3
  76.8 0.8 shard_map.96
  77.6 0.0 collective-permute-done.above_ref
  77.6 0.0 collective-permute-done.2.other_ref
  77.6 1.7 %shard_map.94 = (bf16[4,5120]{1,0:T(4,128)(2,1)}, bf16[8,10240]{1,0:T(8,128)(2,1)}) custom-call(bf16[8,10240]{1,0:T(8,128)(2,1)S(1)} %bitcast.9, bf16[1,10240]{1,0:T(2,128)(2,1)S(1)} %collective-permute-done.above_ref, bf16[256,160]{1,0:T(8,128)(2,1)S(1)} %get-tuple-element.14.even_ref, bf16[256,160]{1,0:T(8,128)(2,1)S(1)} %get-tuple-element.15.odd_ref, ...), custom_call_target="tpu_custom_call" | custom-call | tf_op jit(solution)/shard_map/pallas_call | solution.py:265
  (1 shorter events, 0.0 us)
Async XLA Ops:
  0.6 14.1 %copy-start.4 = (bf16[1,4,5120]{2,1,0:T(4,128)(2,1)S(1)}, bf16[1,4,5120]{2,1,0:T(4,128)(2,1)}, u32[]{:S(2)}) copy-start(bf16[1,4,5120]{2,1,0:T(4,128)(2,1)} %param.6) | copy-start | bytes 122884
  1.5 13.2 %collective-permute-start.1 = (bf16[1,5120]{1,0:T(2,128)(2,1)S(1)}, bf16[1,5120]{1,0:T(2,128)(2,1)S(1)}, u32[]{:S(2)}, u32[]{:S(2)}) collective-permute-start(bf16[1,5120]{1,0:T(2,128)(2,1)S(1)} %slice_bitcast_fusion.1), channel_id=1, source_target_pairs={{1,0},{2,1},{3,2},{4,3},{5,4},{6,5},{7,6},{8,7},{9,8},{10,9},{11,1... | collective-permute-start | bytes 30728 | tf_op jit(solution)/shard_map/ppermute | solution.py:235
  14.7 0.9 %copy-start = (bf16[1,8,10240]{2,1,0:T(8,128)(2,1)S(1)}, bf16[1,8,10240]{2,1,0:T(8,128)(2,1)}, u32[]{:S(2)}) copy-start(bf16[1,8,10240]{2,1,0:T(8,128)(2,1)} %param.5) | copy-start | bytes 491524
  15.6 0.8 %copy-start.2 = (f32[60,160]{1,0:T(8,128)S(1)}, f32[60,160]{1,0:T(8,128)}, u32[]{:S(2)}) copy-start(f32[60,160]{1,0:T(8,128)} %weight_ref.3) | copy-start | bytes 115204
  55.5 13.9 %copy-start.1 = (bf16[1,8,10240]{2,1,0:T(8,128)(2,1)S(1)}, bf16[1,8,10240]{2,1,0:T(8,128)(2,1)}, u32[]{:S(2)}) copy-start(bf16[1,8,10240]{2,1,0:T(8,128)(2,1)} %param.5) | copy-start | bytes 491524
  55.5 21.3 %copy-start.5 = (f32[60,160]{1,0:T(8,128)S(1)}, f32[60,160]{1,0:T(8,128)}, u32[]{:S(2)}) copy-start(f32[60,160]{1,0:T(8,128)} %one_ref.1) | copy-start | bytes 115204
  55.5 21.3 %copy-start.6 = (f32[60,160]{1,0:T(8,128)S(1)}, f32[60,160]{1,0:T(8,128)}, u32[]{:S(2)}) copy-start(f32[60,160]{1,0:T(8,128)} %two_ref.1) | copy-start | bytes 115204
  55.5 21.3 %all-to-all-start.2 = ((bf16[16,40,128]{2,1,0:T(8,128)(2,1)}), bf16[16,40,128]{2,1,0:T(8,128)(2,1)S(1)}, u32[]{:S(2)}, u32[]{:S(2)}) async-start(bf16[16,40,128]{2,1,0:T(8,128)(2,1)} %shard_map.95), calls=%async_computation.2 | async-start | bytes 327680 | tf_op jit(solution)/shard_map/all_to_all | solution.py:264
  67.2 9.5 %copy-start.3 = (f32[60,160]{1,0:T(8,128)S(1)}, f32[60,160]{1,0:T(8,128)}, u32[]{:S(2)}) copy-start(f32[60,160]{1,0:T(8,128)} %weight_ref.3) | copy-start | bytes 115204
  67.3 10.3 %collective-permute-start.2 = (bf16[12,120,128]{2,1,0:T(8,128)(2,1)S(1)}, bf16[12,120,128]{2,1,0:T(8,128)(2,1)S(1)}, u32[]{:S(2)}, u32[]{:S(2)}) collective-permute-start(bf16[12,120,128]{2,1,0:T(8,128)(2,1)S(1)} %all_to_all.16.own_ref.got_ref), channel_id=1, source_target_pairs={{0,1},{1,0},{2,3},{3,2},{4,5},{5,4},{6,7},{7,6},{8,9},{9,8},{10,11... | collective-permute-start | bytes 1105928 | tf_op jit(solution)/shard_map/ppermute | solution.py:262
  69.5 8.1 %collective-permute-start = (bf16[1,10240]{1,0:T(2,128)(2,1)S(1)}, bf16[1,10240]{1,0:T(2,128)(2,1)S(1)}, u32[]{:S(2)}, u32[]{:S(2)}) collective-permute-start(bf16[1,10240]{1,0:T(2,128)(2,1)S(1)} %slice_bitcast_fusion), channel_id=1, source_target_pairs={{0,1},{1,2},{2,3},{3,4},{4,5},{5,6},{6,7},{7,8},{8,9},{9,10},{10,1... | collective-permute-start | bytes 61448 | tf_op jit(solution)/shard_map/ppermute | solution.py:235

commit v3 on v2

v3 whole, which is shorter than its diff:
```python
import jax
import jax.numpy as jnp
from jax import lax
from jax.experimental import pallas as pl
from jax.experimental.pallas import tpu as pltpu
from jax.sharding import Mesh
from jax.sharding import PartitionSpec as P


beta_one = 0.9
beta_two = 0.999
learn_rate = 0.01
decay_rate = 0.01
epsilon = 1e-08
adam_step = 10

C = 160
COUNT = 98304
F32 = jnp.float32
BF16 = jnp.bfloat16
VM = pl.BlockSpec(memory_space=pltpu.VMEM)

PIECE = 40
GRAD_ROWS = 6 * PIECE


def call(kernel, outs, scratch=(), limit=16):
    one = not isinstance(outs, list)
    return pl.pallas_call(
        kernel,
        out_shape=outs,
        out_specs=VM if one else [VM] * len(outs),
        scratch_shapes=list(scratch),
        compiler_params=pltpu.CompilerParams(vmem_limit_bytes=limit << 20),
    )


def tile_rows(piece, wide, groups):
    tiles = []
    for g in range(groups):
        block = piece(wide, g)
        tiles += [block[:, 160 * k : 160 * k + 160] for k in range(4)]
    return tiles


def read_block(ref, g):
    return ref[:, 640 * g : 640 * g + 640].astype(F32)


def pack(rows):
    tail = rows[:, 128:160]
    side = jnp.concatenate([tail[8 * b : 8 * b + 8] for b in range(4)], axis=1)
    return jnp.concatenate([rows[:, 0:128], side], axis=0)


def unpack(piece):
    side = piece[32:40]
    tail = jnp.concatenate([side[:, 32 * b : 32 * b + 32] for b in range(4)], axis=0)
    return jnp.concatenate([piece[0:32], tail], axis=1)


def prepare_kernel(image_ref, weight_ref, even_ref, odd_ref, half_ref, rows_ref):
    tiles = tile_rows(read_block, image_ref, 16)
    even_ref[...] = jnp.concatenate(tiles[0::2], axis=0).astype(BF16)
    odd_ref[...] = jnp.concatenate(tiles[1::2], axis=0).astype(BF16)
    rows_ref[0:60] = weight_ref[...]
    rows_ref[60:64] = jnp.zeros((4, C), F32)
    mine = jnp.where(lax.axis_index("core") == 0, rows_ref[0:32], rows_ref[30:62])
    half_ref[0] = pack(mine).astype(BF16)


def grad_kernel(
    even_ref, odd_ref, cotan_ref, below_ref,
    send_ref, taps_ref,
    five_ref, spread_ref, sums_ref,
):
    even = even_ref[...]
    odd = odd_ref[...]
    five_ref[...] = jnp.zeros_like(five_ref)
    five_ref[0:4] = cotan_ref[...].astype(F32)
    five_ref[4:5] = below_ref[0:1].astype(F32)
    out_row = lax.broadcasted_iota(jnp.int32, (24, 8), 0)
    in_row = lax.broadcasted_iota(jnp.int32, (24, 8), 1)
    pick = (2 * in_row + out_row // 8 - 1 == out_row % 8).astype(F32).astype(BF16)
    spread_ref[...] = jnp.dot(pick, five_ref[...].astype(BF16), preferred_element_type=F32)
    taps = []
    for r in range(3):
        cols = tile_rows(lambda ref, g: ref[8 * r : 8 * r + 8, 640 * g : 640 * g + 640], spread_ref, 8)
        block = jnp.concatenate(cols, axis=0).astype(BF16)
        taps_ref[r] = block
        taps.append(block)
    zeros = jnp.zeros((8, C), BF16)

    def put(r, s, left, right):
        row = (3 * r + s) * C
        sums_ref[row : row + C] = lax.dot_general(
            left, right, (((0,), (0,)), ((), ())), preferred_element_type=F32
        )

    for r in range(3):
        put(r, 1, even, taps[r])
        put(r, 2, odd, taps[r])
        put(r, 0, odd[0:248], taps[r][8:256])
    sums_ref[1440:1448] = zeros.astype(F32)
    for x in range(4):
        for core in range(2):
            for low in range(6):
                start = 30 * (2 * (6 * x + low) + core)
                piece = pack(sums_ref[start : start + 32])
                send_ref[2 * x + core, PIECE * low : PIECE * low + PIECE] = piece.astype(BF16)


def first_sum_kernel(got_ref, send_ref):
    total = got_ref[0].astype(F32)
    for n in range(1, 8):
        total = total + got_ref[n].astype(F32)
    total = total.astype(BF16)
    for n in range(12):
        send_ref[n] = total[PIECE * (n // 2) : PIECE * (n // 2) + PIECE]


def join_kernel(*refs):
    at = 0
    for ref in refs[:-1]:
        refs[-1][at : at + ref.shape[0]] = ref[...]
        at += ref.shape[0]


def decay_kernel(weight_ref, one_ref, two_ref, kept_ref, kept_one_ref, kept_two_ref):
    kept_ref[...] = weight_ref[...] - learn_rate * decay_rate * weight_ref[...]
    kept_one_ref[...] = beta_one * one_ref[...]
    kept_two_ref[...] = beta_two * two_ref[...]


def down_kernel(image_ref, above_ref, even_ref, odd_ref, shift_ref):
    shift_ref[0:1] = above_ref[...].astype(F32)
    shift_ref[1:9] = image_ref[...].astype(F32)
    tiles = tile_rows(lambda ref, g: ref[0:8, 640 * g : 640 * g + 640], shift_ref, 16)
    even_ref[...] = jnp.concatenate(tiles[0::2], axis=0).astype(BF16)
    odd_ref[...] = jnp.concatenate(tiles[1::2], axis=0).astype(BF16)


def second_sum_kernel(got_ref, send_ref):
    total = got_ref[0].astype(F32)
    for n in range(1, 12):
        total = total + got_ref[n].astype(F32)
    total = total.astype(BF16)
    for n in range(16):
        send_ref[n] = total


def conv_kernel(
    even_ref, odd_ref, even_down_ref, odd_down_ref, taps_ref, own_ref, other_ref,
    out_ref, grad_ref,
    kernel_ref, roll_ref,
):
    mine, low_mine, core_mine = lax.axis_index("x"), lax.axis_index("zlo"), lax.axis_index("core")
    for x in range(4):
        apart = jnp.where(mine + x == 3, 2, jnp.where(mine // 2 == x // 2, 1, 3))
        apart = jnp.where(mine == x, 0, apart)
        for low in range(6):
            pair = lax.rem(low_mine // 2 + 3 - low // 2, 3)
            place = 6 * apart + 2 * pair + lax.rem(low_mine + low, 2)
            own = own_ref[place].astype(F32)
            other = other_ref[place].astype(F32)
            for core in range(2):
                start = 30 * (2 * (6 * x + low) + core)
                kernel_ref[start : start + 32] = unpack(jnp.where(core_mine == core, own, other))

    def tap(r, s):
        row = (3 * r + s) * C
        return kernel_ref[row : row + C].astype(BF16)

    def dot(left, right):
        return jnp.dot(left, right, preferred_element_type=F32)

    def dot_t(left, right):
        return lax.dot_general(left, right, (((1,), (1,)), ((), ())), preferred_element_type=F32)

    zeros = jnp.zeros((8, C), BF16)
    even = even_ref[...]
    odd = odd_ref[...]
    odd_before = jnp.concatenate([zeros, odd[0:248]], axis=0)
    even_down = even_down_ref[...]
    odd_down = odd_down_ref[...]
    odd_down_before = jnp.concatenate([zeros, odd_down[0:248]], axis=0)
    roll_ref[0:256] = dot(even, tap(2, 1)) + dot(odd, tap(2, 2)) + dot(odd_before, tap(2, 0))
    roll_ref[256:264] = jnp.zeros((8, C), F32)
    total = dot(even_down, tap(0, 1)) + dot(odd_down, tap(0, 2)) + dot(odd_down_before, tap(0, 0))
    total = total + dot(even, tap(1, 1)) + dot(odd, tap(1, 2)) + dot(odd_before, tap(1, 0))
    total = total + roll_ref[1:257]
    for g in range(8):
        wide = jnp.concatenate(
            [total[32 * g + 8 * k : 32 * g + 8 * k + 8] for k in range(4)], axis=1
        )
        rows = jnp.concatenate([wide[2 * i : 2 * i + 1] for i in range(4)], axis=0)
        out_ref[:, 640 * g : 640 * g + 640] = rows.astype(BF16)
    taps = [taps_ref[r] for r in range(3)]
    after = [jnp.concatenate([t[8:256], zeros], axis=0) for t in taps]
    grad_even = dot_t(taps[0], tap(0, 1)) + dot_t(taps[1], tap(1, 1)) + dot_t(taps[2], tap(2, 1))
    grad_odd = dot_t(taps[0], tap(0, 2)) + dot_t(taps[1], tap(1, 2)) + dot_t(taps[2], tap(2, 2))
    for r in range(3):
        grad_odd = grad_odd + dot_t(after[r], tap(r, 0))
    for g in range(16):
        parts = []
        for k in range(2):
            row = 16 * g + 8 * k
            parts += [grad_even[row : row + 8], grad_odd[row : row + 8]]
        grad_ref[:, 640 * g : 640 * g + 640] = jnp.concatenate(parts, axis=1).astype(BF16)


def adam_kernel(got_ref, weight_ref, one_ref, two_ref, new_weight_ref, new_one_ref, new_two_ref, sums_ref):
    for core in range(2):
        total = got_ref[core].astype(F32)
        for y in range(1, 8):
            total = total + got_ref[2 * y + core].astype(F32)
        sums_ref[30 * core : 30 * core + 32] = unpack(total)
    gradient = sums_ref[0:60] / float(COUNT)
    new_one = one_ref[...] + (1.0 - beta_one) * gradient
    new_two = two_ref[...] + (1.0 - beta_two) * gradient * gradient
    first_hat = new_one / (1.0 - beta_one**adam_step)
    second_hat = new_two / (1.0 - beta_two**adam_step)
    new_weight_ref[...] = weight_ref[...] - learn_rate * (
        first_hat / (jnp.sqrt(second_hat) + epsilon)
    )
    new_one_ref[...] = new_one
    new_two_ref[...] = new_two


def from_behind(block, distance):
    axes = ("zhi", "y", "core")
    route = [(i - distance, i) for i in range(32) if 0 <= i - distance < 32]
    return lax.ppermute(block, axes, route)


def body(image, cotangent, weight, moment_one, moment_two):
    shape = jax.ShapeDtypeStruct
    columns = shape((256, C), BF16)
    image = image.reshape(8, 64 * C)
    cotangent = cotangent.reshape(4, 32 * C)

    def join(*blocks):
        rows = sum(block.shape[0] for block in blocks)
        return call(join_kernel, shape((rows, PIECE, 128), BF16))(*blocks)

    def exchange(block, axis, source):
        route = [(source(i), i) for i in range(lax.axis_size(axis))]
        return lax.ppermute(block, axis, route)

    below = from_behind(cotangent, -1)
    even, odd, half = call(
        prepare_kernel, [columns, columns, shape((1, PIECE, 128), BF16)], [pltpu.VMEM((64, C), F32)]
    )(image, weight)
    send_one, taps = call(
        grad_kernel,
        [shape((8, GRAD_ROWS, 128), BF16), shape((3, 256, C), BF16)],
        [
            pltpu.VMEM((8, 32 * C), F32),
            pltpu.VMEM((24, 32 * C), F32),
            pltpu.VMEM((1448, C), F32),
        ],
    )(even, odd, cotangent, below)
    got_one = lax.all_to_all(send_one, ("x", "core"), 0, 0, tiled=True)
    two = join(half, exchange(half, "zlo", lambda i: i ^ 1))
    next_two = exchange(two, "zlo", lambda i: (i - 2) % 6)
    last_two = exchange(two, "zlo", lambda i: (i - 4) % 6)
    kept = call(decay_kernel, [shape((60, C), F32)] * 3)(weight, moment_one, moment_two)
    send_two = call(first_sum_kernel, shape((12, PIECE, 128), BF16))(got_one)
    got_two = lax.all_to_all(send_two, ("zlo", "zhi"), 0, 0, tiled=True)
    above = from_behind(image[7:8], 1)
    six = join(two, next_two, last_two)
    twelve = join(six, exchange(six, "x", lambda i: i ^ 1))
    across = exchange(twelve, "x", lambda i: 3 - i)
    downs = call(down_kernel, [columns] * 2, [pltpu.VMEM((16, 64 * C), F32)])(image, above)
    send_three = call(second_sum_kernel, shape((16, PIECE, 128), BF16))(got_two)
    got_three = lax.all_to_all(send_three, ("y", "core"), 0, 0, tiled=True)
    own = join(twelve, across)
    other = exchange(own, "core", lambda i: 1 - i)
    output, grad_image = call(
        conv_kernel,
        [shape((4, 32 * C), BF16), shape((8, 64 * C), BF16)],
        [pltpu.VMEM((1448, C), F32), pltpu.VMEM((264, C), F32)],
    )(even, odd, *downs, taps, own, other)
    new_weight, new_one, new_two = call(
        adam_kernel, [shape((60, C), F32)] * 3, [pltpu.VMEM((64, C), F32)]
    )(got_three, *kept)
    return (output[None], grad_image[None], new_weight, new_one, new_two)


def solution(mesh):
    fine = Mesh(mesh.devices.reshape(4, 6, 2, 8, 2), ("x", "zlo", "zhi", "y", "core"))
    dp, space = ("x", "zlo"), ("zhi", "y", "core")
    specs = (P(dp, space, None), P(dp, space, None), P(dp, None), P(dp, None), P(dp, None))

    return jax.shard_map(body, mesh=fine, in_specs=specs, out_specs=specs, check_vma=False)
```

time: 79.8 us -> 94.6 us (1.19)
  the two profiles are of different devices: /device:TPU:1 before, /device:TPU:57 now
where the time goes in v3:
time: 94.6 us; the launch traced here: 93.9 us
  starting transfers between devices  50.2 us (53%)
  waiting for transfers between devices  22.8 us (24%)
  blocking collectives  13.2 us (14%)
  Pallas kernels  5.1 us (5%)
  local copies, waits for them, and re-layouts  1.82 us (2%)
    ppermute x6, starting transfers between devices, exchange(): return lax.ppermute(block, axis, route)  25.2 us
    all_to_all x1, blocking collectives, body(): got_one = lax.all_to_all(send_one, ('x', 'core'), 0, 0, tiled=True)  13.2 us
    ppermute x2, waiting for transfers between devices, from_behind(): return lax.ppermute(block, axes, route)  13 us
    ppermute x2, starting transfers between devices, from_behind(): return lax.ppermute(block, axes, route)  11.3 us
    ppermute x6, waiting for transfers between devices, exchange(): return lax.ppermute(block, axis, route)  9.77 us
    all_to_all x1, starting transfers between devices, body(): got_two = lax.all_to_all(send_two, ('zlo', 'zhi'), 0, 0, tiled=True)  9.28 us
    all_to_all x1, starting transfers between devices, body(): got_three = lax.all_to_all(send_three, ('y', 'core'), 0, 0, tiled=True)  4.38 us
  transfers between devices with their start and end apart: 10, of which 6 were waited for; matrix products, arithmetic and copies ran while one was open for 0% of the time, Pallas kernels for 3%

profile of v3, /device:TPU:57, one launch (start us, length us, event | category | flops | bytes accessed | tf_op | source)
XLA Modules:
  0.0 93.9 jit_solution(1030789648318977400)
XLA Ops:
  0.6 2.6 %collective-permute-start.1 = (bf16[4,5120]{1,0:T(4,128)(2,1)}, bf16[4,5120]{1,0:T(4,128)(2,1)S(1)}, u32[]{:S(2)}, u32[]{:S(2)}) collective-permute-start(bf16[4,5120]{1,0:T(4,128)(2,1)} %bitcast.8), channel_id=1, source_target_pairs={{1,0},{2,1},{3,2},{4,3},{5,4},{6,5},{7,6},{8,7},{9,8},{10,9},{11,1... | collective-permute-start | bytes 122888 | tf_op jit(solution)/shard_map/ppermute | solution.py:233
  3.2 0.0 copy-start
  3.2 0.9 copy-done
  4.1 0.8 copy-done.2
  5.0 0.2 shard_map.92
  5.2 12.0 %collective-permute-done.1.below_ref = bf16[4,5120]{1,0:T(4,128)(2,1)S(1)} collective-permute-done((bf16[4,5120]{1,0:T(4,128)(2,1)}, bf16[4,5120]{1,0:T(4,128)(2,1)S(1)}, u32[]{:S(2)}, u32[]{:S(2)}) %collective-permute-start.1) | collective-permute-done | bytes 40992 | tf_op jit(solution)/shard_map/ppermute | solution.py:233
  17.1 0.8 shard_map.94
  18.0 13.2 %all_to_all.15.got_ref = bf16[8,240,128]{2,1,0:T(8,128)(2,1)S(1)} all-to-all(bf16[8,240,128]{2,1,0:T(8,128)(2,1)S(1)} %get-tuple-element.28), channel_id=1, replica_groups=mesh['x'=4,'zlo'=6,'zhi'=2,'y'=8,'core'=2] {'x','core'}, dimensions={0} | all-to-all | bytes 983040 | tf_op jit(solution)/shard_map/all_to_all | solution.py:263
  31.1 0.7 shard_map.100
  31.9 9.3 %all-to-all-start.1 = ((bf16[12,40,128]{2,1,0:T(8,128)(2,1)}), bf16[12,40,128]{2,1,0:T(8,128)(2,1)S(1)}, u32[]{:S(2)}, u32[]{:S(2)}) async-start(bf16[12,40,128]{2,1,0:T(8,128)(2,1)} %shard_map.100), calls=%async_computation.1 | async-start | bytes 245760 | tf_op jit(solution)/shard_map/all_to_all | solution.py:269
  41.1 3.3 %collective-permute-start.2 = (bf16[1,40,128]{2,1,0:T(8,128)(2,1)S(1)}, bf16[1,40,128]{2,1,0:T(8,128)(2,1)S(1)}, u32[]{:S(2)}, u32[]{:S(2)}) collective-permute-start(bf16[1,40,128]{2,1,0:T(8,128)(2,1)S(1)} %get-tuple-element.25.refs_0_), channel_id=1, source_target_pairs={{32,0},{0,32},{96,64},{64,96},{160,128},{128,160},{33,1},{1,33},{9... | collective-permute-start | bytes 30728 | tf_op jit(solution)/shard_map/ppermute | solution.py:248
  44.5 1.2 %collective-permute-done.2.refs_1_ = bf16[1,40,128]{2,1,0:T(8,128)(2,1)S(1)} collective-permute-done((bf16[1,40,128]{2,1,0:T(8,128)(2,1)S(1)}, bf16[1,40,128]{2,1,0:T(8,128)(2,1)S(1)}, u32[]{:S(2)}, u32[]{:S(2)}) %collective-permute-start.2) | collective-permute-done | bytes 10272 | tf_op jit(solution)/shard_map/ppermute | solution.py:248
  45.7 4.5 %collective-permute-start.3 = (bf16[2,40,128]{2,1,0:T(8,128)(2,1)S(1)}, bf16[2,40,128]{2,1,0:T(8,128)(2,1)S(1)}, u32[]{:S(2)}, u32[]{:S(2)}) collective-permute-start(bf16[2,40,128]{2,1,0:T(8,128)(2,1)S(1)} %shard_map.95.refs_0_), channel_id=1, source_target_pairs={{128,0},{160,32},{0,64},{32,96},{64,128},{96,160},{129,1},{161,33}... | collective-permute-start | bytes 61448 | tf_op jit(solution)/shard_map/ppermute | solution.py:248
  50.2 5.3 %collective-permute-start.4 = (bf16[2,40,128]{2,1,0:T(8,128)(2,1)S(1)}, bf16[2,40,128]{2,1,0:T(8,128)(2,1)S(1)}, u32[]{:S(2)}, u32[]{:S(2)}) collective-permute-start(bf16[2,40,128]{2,1,0:T(8,128)(2,1)S(1)} %shard_map.95.refs_0_), channel_id=1, source_target_pairs={{64,0},{96,32},{128,64},{160,96},{0,128},{32,160},{65,1},{97,33},{... | collective-permute-start | bytes 61448 | tf_op jit(solution)/shard_map/ppermute | solution.py:248
  55.5 0.0 collective-permute-done.3.refs_1_
  55.6 1.8 %collective-permute-done.4.refs_2_ = bf16[2,40,128]{2,1,0:T(8,128)(2,1)S(1)} collective-permute-done((bf16[2,40,128]{2,1,0:T(8,128)(2,1)S(1)}, bf16[2,40,128]{2,1,0:T(8,128)(2,1)S(1)}, u32[]{:S(2)}, u32[]{:S(2)}) %collective-permute-start.4) | collective-permute-done | bytes 20512 | tf_op jit(solution)/shard_map/ppermute | solution.py:248
  57.4 2.2 %collective-permute-start.5 = (bf16[6,40,128]{2,1,0:T(8,128)(2,1)S(1)}, bf16[6,40,128]{2,1,0:T(8,128)(2,1)S(1)}, u32[]{:S(2)}, u32[]{:S(2)}) collective-permute-start(bf16[6,40,128]{2,1,0:T(8,128)(2,1)S(1)} %shard_map.96.refs_0_), channel_id=1, source_target_pairs={{192,0},{0,192},{576,384},{384,576},{193,1},{1,193},{577,385},{385... | collective-permute-start | bytes 184328 | tf_op jit(solution)/shard_map/ppermute | solution.py:248
  59.5 2.8 %collective-permute-done.5.refs_1_ = bf16[6,40,128]{2,1,0:T(8,128)(2,1)S(1)} collective-permute-done((bf16[6,40,128]{2,1,0:T(8,128)(2,1)S(1)}, bf16[6,40,128]{2,1,0:T(8,128)(2,1)S(1)}, u32[]{:S(2)}, u32[]{:S(2)}) %collective-permute-start.5) | collective-permute-done | bytes 61472 | tf_op jit(solution)/shard_map/ppermute | solution.py:248
  62.3 2.8 %collective-permute-start.6 = (bf16[12,40,128]{2,1,0:T(8,128)(2,1)S(1)}, bf16[12,40,128]{2,1,0:T(8,128)(2,1)S(1)}, u32[]{:S(2)}, u32[]{:S(2)}) collective-permute-start(bf16[12,40,128]{2,1,0:T(8,128)(2,1)S(1)} %shard_map.97.refs_0_), channel_id=1, source_target_pairs={{576,0},{384,192},{192,384},{0,576},{577,1},{385,193},{193,385},{1... | collective-permute-start | bytes 368648 | tf_op jit(solution)/shard_map/ppermute | solution.py:248
  65.1 4.0 %collective-permute-done.6.refs_1_ = bf16[12,40,128]{2,1,0:T(8,128)(2,1)S(1)} collective-permute-done((bf16[12,40,128]{2,1,0:T(8,128)(2,1)S(1)}, bf16[12,40,128]{2,1,0:T(8,128)(2,1)S(1)}, u32[]{:S(2)}, u32[]{:S(2)}) %collective-permute-start.6) | collective-permute-done | bytes 122912 | tf_op jit(solution)/shard_map/ppermute | solution.py:248
  69.2 7.1 %collective-permute-start.7 = (bf16[24,40,128]{2,1,0:T(8,128)(2,1)S(1)}, bf16[24,40,128]{2,1,0:T(8,128)(2,1)S(1)}, u32[]{:S(2)}, u32[]{:S(2)}) collective-permute-start(bf16[24,40,128]{2,1,0:T(8,128)(2,1)S(1)} %shard_map.98.own_ref), channel_id=1, source_target_pairs={{1,0},{0,1},{3,2},{2,3},{5,4},{4,5},{7,6},{6,7},{9,8},{8,9},{11,10... | collective-permute-start | bytes 737288 | tf_op jit(solution)/shard_map/ppermute | solution.py:248
  76.3 0.0 all-to-all-done.1.got_ref
  76.3 0.7 shard_map.101
  77.0 4.4 %all-to-all-start.2 = ((bf16[16,40,128]{2,1,0:T(8,128)(2,1)}), bf16[16,40,128]{2,1,0:T(8,128)(2,1)S(1)}, u32[]{:S(2)}, u32[]{:S(2)}) async-start(bf16[16,40,128]{2,1,0:T(8,128)(2,1)} %shard_map.101), calls=%async_computation.2 | async-start | bytes 327680 | tf_op jit(solution)/shard_map/all_to_all | solution.py:276
  81.4 0.0 copy-start.3
  81.4 8.7 %collective-permute-start = (bf16[1,10240]{1,0:T(2,128)(2,1)S(1)}, bf16[1,10240]{1,0:T(2,128)(2,1)S(1)}, u32[]{:S(2)}, u32[]{:S(2)}) collective-permute-start(bf16[1,10240]{1,0:T(2,128)(2,1)S(1)} %slice_bitcast_fusion), channel_id=1, source_target_pairs={{0,1},{1,2},{2,3},{3,4},{4,5},{5,6},{6,7},{7,8},{8,9},{9,10},{10,1... | collective-permute-start | bytes 61448 | tf_op jit(solution)/shard_map/ppermute | solution.py:233
  90.2 1.0 %collective-permute-done.above_ref = bf16[1,10240]{1,0:T(2,128)(2,1)S(1)} collective-permute-done((bf16[1,10240]{1,0:T(2,128)(2,1)S(1)}, bf16[1,10240]{1,0:T(2,128)(2,1)S(1)}, u32[]{:S(2)}, u32[]{:S(2)}) %collective-permute-start) | collective-permute-done | bytes 20512 | tf_op jit(solution)/shard_map/ppermute | solution.py:233
  91.2 0.2 shard_map.93
  91.4 0.0 collective-permute-done.7.other_ref
  91.5 1.7 %shard_map.99 = (bf16[4,5120]{1,0:T(4,128)(2,1)}, bf16[8,10240]{1,0:T(8,128)(2,1)}) custom-call(bf16[256,160]{1,0:T(8,128)(2,1)S(1)} %get-tuple-element.20.even_ref, bf16[256,160]{1,0:T(8,128)(2,1)S(1)} %get-tuple-element.21.odd_ref, bf16[256,160]{1,0:T(8,128)(2,1)S(1)} %get-tuple-element.22.even_down_ref, ...), custom_call_target="tpu_custom_call" | custom-call | tf_op jit(solution)/shard_map/pallas_call | solution.py:279
  93.1 0.0 all-to-all-done.2.got_ref
  93.1 0.8 shard_map.103
  (16 shorter events, 0.1 us)
Async XLA Ops:
  0.6 16.5 %collective-permute-start.1 = (bf16[4,5120]{1,0:T(4,128)(2,1)}, bf16[4,5120]{1,0:T(4,128)(2,1)S(1)}, u32[]{:S(2)}, u32[]{:S(2)}) collective-permute-start(bf16[4,5120]{1,0:T(4,128)(2,1)} %bitcast.8), channel_id=1, source_target_pairs={{1,0},{2,1},{3,2},{4,3},{5,4},{6,5},{7,6},{8,7},{9,8},{10,9},{11,1... | collective-permute-start | bytes 122888 | tf_op jit(solution)/shard_map/ppermute | solution.py:233
  3.2 0.9 copy-start
  4.1 0.8 copy-start.2
  5.0 12.2 %copy-start.6 = (bf16[1,4,5120]{2,1,0:T(4,128)(2,1)S(1)}, bf16[1,4,5120]{2,1,0:T(4,128)(2,1)}, u32[]{:S(2)}) copy-start(bf16[1,4,5120]{2,1,0:T(4,128)(2,1)} %param.6) | copy-start | bytes 122884
  31.9 44.4 %all-to-all-start.1 = ((bf16[12,40,128]{2,1,0:T(8,128)(2,1)}), bf16[12,40,128]{2,1,0:T(8,128)(2,1)S(1)}, u32[]{:S(2)}, u32[]{:S(2)}) async-start(bf16[12,40,128]{2,1,0:T(8,128)(2,1)} %shard_map.100), calls=%async_computation.1 | async-start | bytes 245760 | tf_op jit(solution)/shard_map/all_to_all | solution.py:269
  41.1 4.5 %collective-permute-start.2 = (bf16[1,40,128]{2,1,0:T(8,128)(2,1)S(1)}, bf16[1,40,128]{2,1,0:T(8,128)(2,1)S(1)}, u32[]{:S(2)}, u32[]{:S(2)}) collective-permute-start(bf16[1,40,128]{2,1,0:T(8,128)(2,1)S(1)} %get-tuple-element.25.refs_0_), channel_id=1, source_target_pairs={{32,0},{0,32},{96,64},{64,96},{160,128},{128,160},{33,1},{1,33},{9... | collective-permute-start | bytes 30728 | tf_op jit(solution)/shard_map/ppermute | solution.py:248
  45.7 9.9 %collective-permute-start.3 = (bf16[2,40,128]{2,1,0:T(8,128)(2,1)S(1)}, bf16[2,40,128]{2,1,0:T(8,128)(2,1)S(1)}, u32[]{:S(2)}, u32[]{:S(2)}) collective-permute-start(bf16[2,40,128]{2,1,0:T(8,128)(2,1)S(1)} %shard_map.95.refs_0_), channel_id=1, source_target_pairs={{128,0},{160,32},{0,64},{32,96},{64,128},{96,160},{129,1},{161,33}... | collective-permute-start | bytes 61448 | tf_op jit(solution)/shard_map/ppermute | solution.py:248
  50.2 7.1 %collective-permute-start.4 = (bf16[2,40,128]{2,1,0:T(8,128)(2,1)S(1)}, bf16[2,40,128]{2,1,0:T(8,128)(2,1)S(1)}, u32[]{:S(2)}, u32[]{:S(2)}) collective-permute-start(bf16[2,40,128]{2,1,0:T(8,128)(2,1)S(1)} %shard_map.95.refs_0_), channel_id=1, source_target_pairs={{64,0},{96,32},{128,64},{160,96},{0,128},{32,160},{65,1},{97,33},{... | collective-permute-start | bytes 61448 | tf_op jit(solution)/shard_map/ppermute | solution.py:248
  57.4 5.0 %collective-permute-start.5 = (bf16[6,40,128]{2,1,0:T(8,128)(2,1)S(1)}, bf16[6,40,128]{2,1,0:T(8,128)(2,1)S(1)}, u32[]{:S(2)}, u32[]{:S(2)}) collective-permute-start(bf16[6,40,128]{2,1,0:T(8,128)(2,1)S(1)} %shard_map.96.refs_0_), channel_id=1, source_target_pairs={{192,0},{0,192},{576,384},{384,576},{193,1},{1,193},{577,385},{385... | collective-permute-start | bytes 184328 | tf_op jit(solution)/shard_map/ppermute | solution.py:248
  62.3 6.8 %collective-permute-start.6 = (bf16[12,40,128]{2,1,0:T(8,128)(2,1)S(1)}, bf16[12,40,128]{2,1,0:T(8,128)(2,1)S(1)}, u32[]{:S(2)}, u32[]{:S(2)}) collective-permute-start(bf16[12,40,128]{2,1,0:T(8,128)(2,1)S(1)} %shard_map.97.refs_0_), channel_id=1, source_target_pairs={{576,0},{384,192},{192,384},{0,576},{577,1},{385,193},{193,385},{1... | collective-permute-start | bytes 368648 | tf_op jit(solution)/shard_map/ppermute | solution.py:248
  69.2 22.3 %collective-permute-start.7 = (bf16[24,40,128]{2,1,0:T(8,128)(2,1)S(1)}, bf16[24,40,128]{2,1,0:T(8,128)(2,1)S(1)}, u32[]{:S(2)}, u32[]{:S(2)}) collective-permute-start(bf16[24,40,128]{2,1,0:T(8,128)(2,1)S(1)} %shard_map.98.own_ref), channel_id=1, source_target_pairs={{1,0},{0,1},{3,2},{2,3},{5,4},{4,5},{7,6},{6,7},{9,8},{8,9},{11,10... | collective-permute-start | bytes 737288 | tf_op jit(solution)/shard_map/ppermute | solution.py:248
  77.0 4.4 %copy-start.1 = (bf16[1,8,10240]{2,1,0:T(8,128)(2,1)S(1)}, bf16[1,8,10240]{2,1,0:T(8,128)(2,1)}, u32[]{:S(2)}) copy-start(bf16[1,8,10240]{2,1,0:T(8,128)(2,1)} %param.5) | copy-start | bytes 491524
  77.0 13.2 %copy-start.4 = (f32[60,160]{1,0:T(8,128)S(1)}, f32[60,160]{1,0:T(8,128)}, u32[]{:S(2)}) copy-start(f32[60,160]{1,0:T(8,128)} %one_ref.1) | copy-start | bytes 115204
  77.0 13.2 %copy-start.5 = (f32[60,160]{1,0:T(8,128)S(1)}, f32[60,160]{1,0:T(8,128)}, u32[]{:S(2)}) copy-start(f32[60,160]{1,0:T(8,128)} %two_ref.1) | copy-start | bytes 115204
  77.0 16.2 %all-to-all-start.2 = ((bf16[16,40,128]{2,1,0:T(8,128)(2,1)}), bf16[16,40,128]{2,1,0:T(8,128)(2,1)S(1)}, u32[]{:S(2)}, u32[]{:S(2)}) async-start(bf16[16,40,128]{2,1,0:T(8,128)(2,1)} %shard_map.101), calls=%async_computation.2 | async-start | bytes 327680 | tf_op jit(solution)/shard_map/all_to_all | solution.py:276
  81.4 8.8 %copy-start.3 = (f32[60,160]{1,0:T(8,128)S(1)}, f32[60,160]{1,0:T(8,128)}, u32[]{:S(2)}) copy-start(f32[60,160]{1,0:T(8,128)} %weight_ref.3) | copy-start | bytes 115204
  81.4 9.8 %collective-permute-start = (bf16[1,10240]{1,0:T(2,128)(2,1)S(1)}, bf16[1,10240]{1,0:T(2,128)(2,1)S(1)}, u32[]{:S(2)}, u32[]{:S(2)}) collective-permute-start(bf16[1,10240]{1,0:T(2,128)(2,1)S(1)} %slice_bitcast_fusion), channel_id=1, source_target_pairs={{0,1},{1,2},{2,3},{3,4},{4,5},{5,6},{6,7},{7,8},{8,9},{9,10},{10,1... | collective-permute-start | bytes 61448 | tf_op jit(solution)/shard_map/ppermute | solution.py:233

commit v4 on v2

--- a/solution.py
+++ b/solution.py
@@ -26,10 +26,12 @@
 SEND_TWO = PIECE + 80
 
 
-def call(kernel, outs, scratch=(), limit=16):
+def call(kernel, outs, scratch=(), ins=None, limit=16):
     one = not isinstance(outs, list)
+    more = {} if ins is None else {"in_specs": ins}
     return pl.pallas_call(
         kernel,
+        **more,
         out_shape=outs,
         out_specs=VM if one else [VM] * len(outs),
         scratch_shapes=list(scratch),
@@ -61,19 +63,45 @@
     return jnp.concatenate([piece[0:32], tail], axis=1)
 
 
+def prepare_kernel(
+    image_hbm, cotan_hbm, weight_hbm,
+    even_ref, odd_ref, cotan_ref, rows_ref,
+    image_ref, own_ref, weight_ref, done,
+):
+    reads = [
+        pltpu.make_async_copy(image_hbm, image_ref, done.at[0]),
+        pltpu.make_async_copy(cotan_hbm, cotan_ref, done.at[1]),
+        pltpu.make_async_copy(weight_hbm, own_ref, done.at[2]),
+    ]
+    for read in reads:
+        read.start()
+    for read in reads:
+        read.wait()
+    tiles = tile_rows(read_block, image_ref, 16)
+    even_ref[...] = jnp.concatenate(tiles[0::2], axis=0).astype(BF16)
+    odd_ref[...] = jnp.concatenate(tiles[1::2], axis=0).astype(BF16)
+    weight_ref[0:60] = own_ref[...]
+    weight_ref[60:64] = jnp.zeros((4, C), F32)
+    quarter = 2 * lax.axis_index("core") + lax.axis_index("zhi")
+    mine = weight_ref[0:16]
+    for q in range(1, 4):
+        mine = jnp.where(quarter == q, weight_ref[15 * q : 15 * q + 16], mine)
+    tail = mine[:, 128:160]
+    lane = lax.broadcasted_iota(jnp.int32, (16, 128), 1) // 32
+    tail = jnp.where(lane == lax.axis_index("x"), jnp.concatenate([tail] * 4, axis=1), 0.0)
+    rows_ref[...] = jnp.concatenate([mine[:, 0:128], tail], axis=0).astype(BF16)
+
+
 def grad_kernel(
-    image_ref, cotan_ref, below_ref, weight_ref,
-    send_ref, even_ref, odd_ref, taps_ref,
-    five_ref, spread_ref, sums_ref, rows_ref,
+    even_ref, odd_ref, cotan_ref, rows_ref, below_ref,
+    send_ref, taps_ref,
+    five_ref, spread_ref, sums_ref,
 ):
-    tiles = tile_rows(read_block, image_ref, 16)
-    even = jnp.concatenate(tiles[0::2], axis=0).astype(BF16)
-    odd = jnp.concatenate(tiles[1::2], axis=0).astype(BF16)
-    even_ref[...] = even
-    odd_ref[...] = odd
+    even = even_ref[...]
+    odd = odd_ref[...]
     five_ref[...] = jnp.zeros_like(five_ref)
     five_ref[0:4] = cotan_ref[...].astype(F32)
-    five_ref[4:5] = below_ref[...].astype(F32)
+    five_ref[4:5] = below_ref[0:1].astype(F32)
     out_row = lax.broadcasted_iota(jnp.int32, (24, 8), 0)
     in_row = lax.broadcasted_iota(jnp.int32, (24, 8), 1)
     pick = (2 * in_row + out_row // 8 - 1 == out_row % 8).astype(F32).astype(BF16)
@@ -103,18 +131,14 @@
                 start = 30 * (2 * (6 * x + low) + core)
                 piece = pack(sums_ref[start : start + 32])
                 send_ref[2 * x + core, PIECE * low : PIECE * low + PIECE] = piece.astype(BF16)
-    rows_ref[0:60] = weight_ref[...]
-    rows_ref[60:64] = jnp.zeros((4, C), F32)
-    quarter = 2 * lax.axis_index("core") + lax.axis_index("zhi")
-    mine = rows_ref[0:16]
-    for q in range(1, 4):
-        mine = jnp.where(quarter == q, rows_ref[15 * q : 15 * q + 16], mine)
-    tail = mine[:, 128:160]
-    lane = lax.broadcasted_iota(jnp.int32, (16, 128), 1) // 32
-    tail = jnp.where(lane == lax.axis_index("x"), jnp.concatenate([tail] * 4, axis=1), 0.0)
-    both = jnp.concatenate([mine[:, 0:128], tail], axis=0).astype(BF16)
     for n in range(8):
-        send_ref[n, GRAD_ROWS:SEND_ONE] = both
+        send_ref[n, GRAD_ROWS:SEND_ONE] = rows_ref[...]
+
+
+def decay_kernel(weight_ref, one_ref, two_ref, kept_ref, kept_one_ref, kept_two_ref):
+    kept_ref[...] = weight_ref[...] - learn_rate * decay_rate * weight_ref[...]
+    kept_one_ref[...] = beta_one * one_ref[...]
+    kept_two_ref[...] = beta_two * two_ref[...]
 
 
 def first_sum_kernel(got_ref, send_ref):
@@ -217,13 +241,12 @@
             total = total + got_ref[2 * y + core].astype(F32)
         sums_ref[30 * core : 30 * core + 32] = unpack(total)
     gradient = sums_ref[0:60] / float(COUNT)
-    weight = weight_ref[...]
-    new_one = beta_one * one_ref[...] + (1.0 - beta_one) * gradient
-    new_two = beta_two * two_ref[...] + (1.0 - beta_two) * gradient * gradient
+    new_one = one_ref[...] + (1.0 - beta_one) * gradient
+    new_two = two_ref[...] + (1.0 - beta_two) * gradient * gradient
     first_hat = new_one / (1.0 - beta_one**adam_step)
     second_hat = new_two / (1.0 - beta_two**adam_step)
-    new_weight_ref[...] = weight - learn_rate * (
-        first_hat / (jnp.sqrt(second_hat) + epsilon) + decay_rate * weight
+    new_weight_ref[...] = weight_ref[...] - learn_rate * (
+        first_hat / (jnp.sqrt(second_hat) + epsilon)
     )
     new_one_ref[...] = new_one
     new_two_ref[...] = new_two
@@ -239,24 +262,35 @@
     shape = jax.ShapeDtypeStruct
     image = image.reshape(8, 64 * C)
     cotangent = cotangent.reshape(4, 32 * C)
-    below = from_behind(cotangent[0:1], -1)
-    above = from_behind(image[7:8], 1)
-    send_one, even, odd, taps = call(
-        grad_kernel,
+    below = from_behind(cotangent, -1)
+    even, odd, strip, rows = call(
+        prepare_kernel,
         [
-            shape((8, SEND_ONE, 128), BF16),
             shape((256, C), BF16),
             shape((256, C), BF16),
-            shape((3, 256, C), BF16),
+            shape((4, 32 * C), BF16),
+            shape((32, 128), BF16),
         ],
+        [
+            pltpu.VMEM((8, 64 * C), BF16),
+            pltpu.VMEM((60, C), F32),
+            pltpu.VMEM((64, C), F32),
+            pltpu.SemaphoreType.DMA((3,)),
+        ],
+        [pl.BlockSpec(memory_space=pltpu.HBM)] * 3,
+    )(*[pltpu.with_memory_space_constraint(a, pltpu.HBM) for a in (image, cotangent, weight)])
+    send_one, taps = call(
+        grad_kernel,
+        [shape((8, SEND_ONE, 128), BF16), shape((3, 256, C), BF16)],
         [
             pltpu.VMEM((8, 32 * C), F32),
             pltpu.VMEM((24, 32 * C), F32),
             pltpu.VMEM((1448, C), F32),
-            pltpu.VMEM((64, C), F32),
         ],
-    )(image, cotangent, below, weight)
+    )(even, odd, strip, rows, below)
     got_one = lax.all_to_all(send_one, ("x", "core"), 0, 0, tiled=True)
+    above = from_behind(image[7:8], 1)
+    kept = call(decay_kernel, [shape((60, C), F32)] * 3)(weight, moment_one, moment_two)
     send_two = call(first_sum_kernel, shape((12, SEND_TWO, 128), BF16))(got_one)
     got_two = lax.all_to_all(send_two, ("zlo", "zhi"), 0, 0, tiled=True)
     other = lax.ppermute(got_two, "core", [(0, 1), (1, 0)])
@@ -273,7 +307,7 @@
     )(image, above, even, odd, taps, got_two, other)
     new_weight, new_one, new_two = call(
         adam_kernel, [shape((60, C), F32)] * 3, [pltpu.VMEM((64, C), F32)]
-    )(got_three, weight, moment_one, moment_two)
+    )(got_three, *kept)
     return (output[None], grad_image[None], new_weight, new_one, new_two)
 
 

time: 79.8 us -> 77.4 us (0.970)
  the two profiles are of different devices: /device:TPU:1 before, /device:TPU:57 now
where the time goes in v4:
time: 77.4 us; the launch traced here: 75.8 us
  blocking collectives  38.2 us (49%)
  starting transfers between devices  18.6 us (24%)
  waiting for transfers between devices  13 us (17%)
  Pallas kernels  5.25 us (7%)
    all_to_all x1, blocking collectives, body(): got_two = lax.all_to_all(send_two, ('zlo', 'zhi'), 0, 0, tiled=True)  23.9 us
    all_to_all x1, blocking collectives, body(): got_one = lax.all_to_all(send_one, ('x', 'core'), 0, 0, tiled=True)  14.3 us
    ppermute x2, waiting for transfers between devices, from_behind(): return lax.ppermute(block, axes, route)  13 us
    ppermute x2, starting transfers between devices, from_behind(): return lax.ppermute(block, axes, route)  9.58 us
    all_to_all x1, starting transfers between devices, body(): got_three = lax.all_to_all(send_three, ('y', 'core'), 0, 0, tiled=True)  6.54 us
    ppermute x1, starting transfers between devices, body(): other = lax.ppermute(got_two, 'core', [(0, 1), (1, 0)])  2.43 us
    pallas_call x1, Pallas kernels, body(): call(conv_kernel, [shape((4, 32 * C), BF16), shape((8, 64 * C), BF16)], [...  1.72 us
  transfers between devices with their start and end apart: 4, of which 2 were waited for; matrix products, arithmetic and copies ran while one was open for 0% of the time, Pallas kernels for 3%

profile of v4, /device:TPU:57, one launch (start us, length us, event | category | flops | bytes accessed | tf_op | source)
XLA Modules:
  0.0 75.8 jit_solution(444892965989384075)
XLA Ops:
  0.6 2.6 %collective-permute-start.1 = (bf16[4,5120]{1,0:T(4,128)(2,1)}, bf16[4,5120]{1,0:T(4,128)(2,1)S(1)}, u32[]{:S(2)}, u32[]{:S(2)}) collective-permute-start(bf16[4,5120]{1,0:T(4,128)(2,1)} %bitcast.8), channel_id=1, source_target_pairs={{1,0},{2,1},{3,2},{4,3},{5,4},{6,5},{7,6},{8,7},{9,8},{10,9},{11,1... | collective-permute-start | bytes 122888 | tf_op jit(solution)/shard_map/ppermute | solution.py:258
  3.2 1.2 %shard_map.92 = (bf16[256,160]{1,0:T(8,128)(2,1)S(1)}, bf16[256,160]{1,0:T(8,128)(2,1)S(1)}, bf16[4,5120]{1,0:T(4,128)(2,1)S(1)}, bf16[32,128]{1,0:T(8,128)(2,1)S(1)}) custom-call(bf16[8,10240]{1,0:T(8,128)(2,1)} %bitcast.6, bf16[4,5120]{1,0:T(4,128)(2,1)} %bitcast.9, f32[60,160]{1,0:T(8,128)} %weight_ref.1), custom_call_target="tpu_custom_call" | custom-call | tf_op jit(solution)/shard_map/pallas_call | solution.py:266
  4.4 12.8 %collective-permute-done.1.below_ref = bf16[4,5120]{1,0:T(4,128)(2,1)S(1)} collective-permute-done((bf16[4,5120]{1,0:T(4,128)(2,1)}, bf16[4,5120]{1,0:T(4,128)(2,1)S(1)}, u32[]{:S(2)}, u32[]{:S(2)}) %collective-permute-start.1) | collective-permute-done | bytes 40992 | tf_op jit(solution)/shard_map/ppermute | solution.py:258
  17.1 0.8 %shard_map.93 = (bf16[8,272,128]{2,1,0:T(8,128)(2,1)S(1)}, bf16[3,256,160]{2,1,0:T(8,128)(2,1)S(1)}) custom-call(bf16[256,160]{1,0:T(8,128)(2,1)S(1)} %get-tuple-element.19.even_ref, bf16[256,160]{1,0:T(8,128)(2,1)S(1)} %get-tuple-element.20.odd_ref, bf16[4,5120]{1,0:T(4,128)(2,1)S(1)} %get-tuple-element.21.cotan_ref, ...), custom_call_target="tpu_custom_call" | custom-call | tf_op jit(solution)/shard_map/pallas_call | solution.py:282
  18.0 14.3 %all_to_all.15.got_ref = bf16[8,272,128]{2,1,0:T(8,128)(2,1)S(1)} all-to-all(bf16[8,272,128]{2,1,0:T(8,128)(2,1)S(1)} %get-tuple-element.24), channel_id=1, replica_groups=mesh['x'=4,'zlo'=6,'zhi'=2,'y'=8,'core'=2] {'x','core'}, dimensions={0} | all-to-all | bytes 1114112 | tf_op jit(solution)/shard_map/all_to_all | solution.py:291
  32.3 0.1 shard_map.94
  32.4 23.9 %all_to_all.16.own_ref.got_ref = bf16[12,120,128]{2,1,0:T(8,128)(2,1)S(1)} all-to-all(bf16[12,120,128]{2,1,0:T(8,128)(2,1)S(1)} %shard_map.94), channel_id=1, replica_groups=mesh['x'=4,'zlo'=6,'zhi'=2,'y'=8,'core'=2] {'zlo','zhi'}, dimensions={0} | all-to-all | bytes 737280 | tf_op jit(solution)/shard_map/all_to_all | solution.py:295
  56.3 0.7 shard_map.96
  57.0 0.0 copy-start
  57.0 0.0 copy-start.2
  57.0 0.0 copy-start.3
  57.0 6.5 %all-to-all-start.2 = ((bf16[16,40,128]{2,1,0:T(8,128)(2,1)}), bf16[16,40,128]{2,1,0:T(8,128)(2,1)S(1)}, u32[]{:S(2)}, u32[]{:S(2)}) async-start(bf16[16,40,128]{2,1,0:T(8,128)(2,1)} %shard_map.96), calls=%async_computation.2 | async-start | bytes 327680 | tf_op jit(solution)/shard_map/all_to_all | solution.py:298
  63.5 0.0 copy-start.1
  63.5 2.4 %collective-permute-start.2 = (bf16[12,120,128]{2,1,0:T(8,128)(2,1)S(1)}, bf16[12,120,128]{2,1,0:T(8,128)(2,1)S(1)}, u32[]{:S(2)}, u32[]{:S(2)}) collective-permute-start(bf16[12,120,128]{2,1,0:T(8,128)(2,1)S(1)} %all_to_all.16.own_ref.got_ref), channel_id=1, source_target_pairs={{0,1},{1,0},{2,3},{3,2},{4,5},{5,4},{6,7},{7,6},{8,9},{9,8},{10,11... | collective-permute-start | bytes 1105928 | tf_op jit(solution)/shard_map/ppermute | solution.py:296
  66.0 0.0 copy-done
  66.0 7.0 %collective-permute-start = (bf16[1,10240]{1,0:T(2,128)(2,1)S(1)}, bf16[1,10240]{1,0:T(2,128)(2,1)S(1)}, u32[]{:S(2)}, u32[]{:S(2)}) collective-permute-start(bf16[1,10240]{1,0:T(2,128)(2,1)S(1)} %slice_bitcast_fusion), channel_id=1, source_target_pairs={{0,1},{1,2},{2,3},{3,4},{4,5},{5,6},{6,7},{7,8},{8,9},{9,10},{10,1... | collective-permute-start | bytes 61448 | tf_op jit(solution)/shard_map/ppermute | solution.py:258
  73.0 0.0 copy-done.2
  73.0 0.0 copy-done.3
  73.0 0.0 copy-done.1
  73.1 0.0 all-to-all-done.2.got_ref
  73.1 0.8 %shard_map.98 = (f32[60,160]{1,0:T(8,128)}, f32[60,160]{1,0:T(8,128)}, f32[60,160]{1,0:T(8,128)}) custom-call(bf16[16,40,128]{2,1,0:T(8,128)(2,1)S(1)} %all-to-all-done.2.got_ref, f32[60,160]{1,0:T(8,128)S(1)} %get-tuple-element.27.weight_ref, f32[60,160]{1,0:T(8,128)S(1)} %get-tuple-element.28.one_ref, f32[60,160]{1,0:T(8,128)S(1)} %get-tuple-element.29.two_ref), custom_call_target="tpu_custom_call" | custom-call | tf_op jit(solution)/shard_map/pallas_call | solution.py:308
  73.9 0.2 collective-permute-done.above_ref
  74.1 0.0 collective-permute-done.2.other_ref
  74.1 1.7 %shard_map.95 = (bf16[4,5120]{1,0:T(4,128)(2,1)}, bf16[8,10240]{1,0:T(8,128)(2,1)}) custom-call(bf16[8,10240]{1,0:T(8,128)(2,1)S(1)} %bitcast.7, bf16[1,10240]{1,0:T(2,128)(2,1)S(1)} %collective-permute-done.above_ref, bf16[256,160]{1,0:T(8,128)(2,1)S(1)} %get-tuple-element.19.even_ref, bf16[256,160]{1,0:T(8,128)(2,1)S(1)} %get-tuple-element.20.odd_ref, ...), custom_call_target="tpu_custom_call" | custom-call | tf_op jit(solution)/shard_map/pallas_call | solution.py:299
  (2 shorter events, 0.1 us)
Async XLA Ops:
  0.6 16.5 %collective-permute-start.1 = (bf16[4,5120]{1,0:T(4,128)(2,1)}, bf16[4,5120]{1,0:T(4,128)(2,1)S(1)}, u32[]{:S(2)}, u32[]{:S(2)}) collective-permute-start(bf16[4,5120]{1,0:T(4,128)(2,1)} %bitcast.8), channel_id=1, source_target_pairs={{1,0},{2,1},{3,2},{4,3},{5,4},{6,5},{7,6},{8,7},{9,8},{10,9},{11,1... | collective-permute-start | bytes 122888 | tf_op jit(solution)/shard_map/ppermute | solution.py:258
  57.0 9.0 %copy-start = (bf16[1,8,10240]{2,1,0:T(8,128)(2,1)S(1)}, bf16[1,8,10240]{2,1,0:T(8,128)(2,1)}, u32[]{:S(2)}) copy-start(bf16[1,8,10240]{2,1,0:T(8,128)(2,1)} %param.5) | copy-start | bytes 491524
  57.0 16.1 %copy-start.2 = (f32[60,160]{1,0:T(8,128)S(1)}, f32[60,160]{1,0:T(8,128)}, u32[]{:S(2)}) copy-start(f32[60,160]{1,0:T(8,128)} %one_ref.1) | copy-start | bytes 115204
  57.0 16.1 %copy-start.3 = (f32[60,160]{1,0:T(8,128)S(1)}, f32[60,160]{1,0:T(8,128)}, u32[]{:S(2)}) copy-start(f32[60,160]{1,0:T(8,128)} %two_ref.1) | copy-start | bytes 115204
  57.0 16.1 %all-to-all-start.2 = ((bf16[16,40,128]{2,1,0:T(8,128)(2,1)}), bf16[16,40,128]{2,1,0:T(8,128)(2,1)S(1)}, u32[]{:S(2)}, u32[]{:S(2)}) async-start(bf16[16,40,128]{2,1,0:T(8,128)(2,1)} %shard_map.96), calls=%async_computation.2 | async-start | bytes 327680 | tf_op jit(solution)/shard_map/all_to_all | solution.py:298
  63.5 9.5 %copy-start.1 = (f32[60,160]{1,0:T(8,128)S(1)}, f32[60,160]{1,0:T(8,128)}, u32[]{:S(2)}) copy-start(f32[60,160]{1,0:T(8,128)} %weight_ref.1) | copy-start | bytes 115204
  63.5 10.6 %collective-permute-start.2 = (bf16[12,120,128]{2,1,0:T(8,128)(2,1)S(1)}, bf16[12,120,128]{2,1,0:T(8,128)(2,1)S(1)}, u32[]{:S(2)}, u32[]{:S(2)}) collective-permute-start(bf16[12,120,128]{2,1,0:T(8,128)(2,1)S(1)} %all_to_all.16.own_ref.got_ref), channel_id=1, source_target_pairs={{0,1},{1,0},{2,3},{3,2},{4,5},{5,4},{6,7},{7,6},{8,9},{9,8},{10,11... | collective-permute-start | bytes 1105928 | tf_op jit(solution)/shard_map/ppermute | solution.py:296
  66.0 8.1 %collective-permute-start = (bf16[1,10240]{1,0:T(2,128)(2,1)S(1)}, bf16[1,10240]{1,0:T(2,128)(2,1)S(1)}, u32[]{:S(2)}, u32[]{:S(2)}) collective-permute-start(bf16[1,10240]{1,0:T(2,128)(2,1)S(1)} %slice_bitcast_fusion), channel_id=1, source_target_pairs={{0,1},{1,2},{2,3},{3,4},{4,5},{5,6},{6,7},{7,8},{8,9},{9,10},{10,1... | collective-permute-start | bytes 61448 | tf_op jit(solution)/shard_map/ppermute | solution.py:258

commit v5 on v4

--- a/solution.py
+++ b/solution.py
@@ -93,8 +93,8 @@
 
 
 def grad_kernel(
-    even_ref, odd_ref, cotan_ref, rows_ref, below_ref,
-    send_ref, taps_ref,
+    even_ref, odd_ref, cotan_ref, below_ref,
+    keep_ref, give_ref, taps_ref,
     five_ref, spread_ref, sums_ref,
 ):
     even = even_ref[...]
@@ -125,14 +125,21 @@
         put(r, 2, odd, taps[r])
         put(r, 0, odd[0:248], taps[r][8:256])
     sums_ref[1440:1448] = zeros.astype(F32)
+    first = lax.axis_index("core") == 0
     for x in range(4):
-        for core in range(2):
-            for low in range(6):
-                start = 30 * (2 * (6 * x + low) + core)
-                piece = pack(sums_ref[start : start + 32])
-                send_ref[2 * x + core, PIECE * low : PIECE * low + PIECE] = piece.astype(BF16)
-    for n in range(8):
-        send_ref[n, GRAD_ROWS:SEND_ONE] = rows_ref[...]
+        for low in range(6):
+            start = 60 * (6 * x + low)
+            halves = [pack(sums_ref[start + 30 * c : start + 30 * c + 32]) for c in range(2)]
+            at = slice(PIECE * low, PIECE * low + PIECE)
+            keep_ref[x, at] = jnp.where(first, halves[0], halves[1]).astype(BF16)
+            give_ref[x, at] = jnp.where(first, halves[1], halves[0]).astype(BF16)
+
+
+def core_sum_kernel(keep_ref, got_ref, rows_ref, send_ref):
+    for x in range(4):
+        total = keep_ref[x].astype(F32) + got_ref[x].astype(F32)
+        send_ref[x, 0:GRAD_ROWS] = total.astype(BF16)
+        send_ref[x, GRAD_ROWS:SEND_ONE] = rows_ref[...]
 
 
 def decay_kernel(weight_ref, one_ref, two_ref, kept_ref, kept_one_ref, kept_two_ref):
@@ -143,15 +150,13 @@
 
 def first_sum_kernel(got_ref, send_ref):
     total = got_ref[0, 0:GRAD_ROWS].astype(F32)
-    for n in range(1, 8):
-        total = total + got_ref[n, 0:GRAD_ROWS].astype(F32)
+    tail = got_ref[0, GRAD_ROWS + 16 : SEND_ONE].astype(F32)
+    for x in range(1, 4):
+        total = total + got_ref[x, 0:GRAD_ROWS].astype(F32)
+        tail = tail + got_ref[x, GRAD_ROWS + 16 : SEND_ONE].astype(F32)
     total = total.astype(BF16)
-    core = lax.axis_index("core")
-    heads = [got_ref[2 * x + core, GRAD_ROWS : GRAD_ROWS + 16] for x in range(4)]
-    tail = got_ref[core, GRAD_ROWS + 16 : SEND_ONE].astype(F32)
-    for x in range(1, 4):
-        tail = tail + got_ref[2 * x + core, GRAD_ROWS + 16 : SEND_ONE].astype(F32)
     tail = tail.astype(BF16)
+    heads = [got_ref[x, GRAD_ROWS : GRAD_ROWS + 16] for x in range(4)]
     for low in range(6):
         for high in range(2):
             n = 2 * low + high
@@ -279,16 +284,18 @@
         ],
         [pl.BlockSpec(memory_space=pltpu.HBM)] * 3,
     )(*[pltpu.with_memory_space_constraint(a, pltpu.HBM) for a in (image, cotangent, weight)])
-    send_one, taps = call(
+    keep, give, taps = call(
         grad_kernel,
-        [shape((8, SEND_ONE, 128), BF16), shape((3, 256, C), BF16)],
+        [shape((4, GRAD_ROWS, 128), BF16)] * 2 + [shape((3, 256, C), BF16)],
         [
             pltpu.VMEM((8, 32 * C), F32),
             pltpu.VMEM((24, 32 * C), F32),
             pltpu.VMEM((1448, C), F32),
         ],
-    )(even, odd, strip, rows, below)
-    got_one = lax.all_to_all(send_one, ("x", "core"), 0, 0, tiled=True)
+    )(even, odd, strip, below)
+    given = lax.ppermute(give, "core", [(0, 1), (1, 0)])
+    send_one = call(core_sum_kernel, shape((4, SEND_ONE, 128), BF16))(keep, given, rows)
+    got_one = lax.all_to_all(send_one, "x", 0, 0, tiled=True)
     above = from_behind(image[7:8], 1)
     kept = call(decay_kernel, [shape((60, C), F32)] * 3)(weight, moment_one, moment_two)
     send_two = call(first_sum_kernel, shape((12, SEND_TWO, 128), BF16))(got_one)

time: 77.4 us -> 79.1 us (1.022)
  the two profiles are of different devices: /device:TPU:57 before, /device:TPU:1 now
where the time goes in v5:
time: 79.1 us; the launch traced here: 78.7 us
  starting transfers between devices  36.2 us (46%)
  blocking collectives  31.4 us (40%)
  Pallas kernels  5.3 us (7%)
  waiting for transfers between devices  4.96 us (6%)
    all_to_all x1, blocking collectives, body(): got_two = lax.all_to_all(send_two, ('zlo', 'zhi'), 0, 0, tiled=True)  22.6 us
    all_to_all x1, starting transfers between devices, body(): got_three = lax.all_to_all(send_three, ('y', 'core'), 0, 0, tiled=True)  16 us
    ppermute x2, starting transfers between devices, from_behind(): return lax.ppermute(block, axes, route)  15.9 us
    all_to_all x1, blocking collectives, body(): got_one = lax.all_to_all(send_one, 'x', 0, 0, tiled=True)  8.87 us
    all_to_all x1, waiting for transfers between devices, body(): got_three = lax.all_to_all(send_three, ('y', 'core'), 0, 0, tiled=True)  3.69 us
    ppermute x1, starting transfers between devices, body(): other = lax.ppermute(got_two, 'core', [(0, 1), (1, 0)])  2.14 us
    ppermute x1, starting transfers between devices, body(): given = lax.ppermute(give, 'core', [(0, 1), (1, 0)])  2.14 us
    pallas_call x1, Pallas kernels, body(): call(conv_kernel, [shape((4, 32 * C), BF16), shape((8, 64 * C), BF16)], [...  1.72 us
  transfers between devices with their start and end apart: 5, of which 2 were waited for; matrix products, arithmetic and copies ran while one was open for 0% of the time, Pallas kernels for 2%

profile of v5, /device:TPU:1, one launch (start us, length us, event | category | flops | bytes accessed | tf_op | source)
XLA Modules:
  0.0 78.7 jit_solution(10843691256877083443)
XLA Ops:
  0.6 12.4 %collective-permute-start.1 = (bf16[4,5120]{1,0:T(4,128)(2,1)}, bf16[4,5120]{1,0:T(4,128)(2,1)S(1)}, u32[]{:S(2)}, u32[]{:S(2)}) collective-permute-start(bf16[4,5120]{1,0:T(4,128)(2,1)} %bitcast.8), channel_id=1, source_target_pairs={{1,0},{2,1},{3,2},{4,3},{5,4},{6,5},{7,6},{8,7},{9,8},{10,9},{11,1... | collective-permute-start | bytes 122888 | tf_op jit(solution)/shard_map/ppermute | solution.py:263
  13.0 1.2 %shard_map.92 = (bf16[256,160]{1,0:T(8,128)(2,1)S(1)}, bf16[256,160]{1,0:T(8,128)(2,1)S(1)}, bf16[4,5120]{1,0:T(4,128)(2,1)S(1)}, bf16[32,128]{1,0:T(8,128)(2,1)S(1)}) custom-call(bf16[8,10240]{1,0:T(8,128)(2,1)} %bitcast.6, bf16[4,5120]{1,0:T(4,128)(2,1)} %bitcast.9, f32[60,160]{1,0:T(8,128)} %weight_ref.1), custom_call_target="tpu_custom_call" | custom-call | tf_op jit(solution)/shard_map/pallas_call | solution.py:271
  14.2 0.0 collective-permute-done.1.below_ref
  14.2 0.8 %shard_map.93 = (bf16[4,240,128]{2,1,0:T(8,128)(2,1)S(1)}, bf16[4,240,128]{2,1,0:T(8,128)(2,1)S(1)}, bf16[3,256,160]{2,1,0:T(8,128)(2,1)S(1)}) custom-call(bf16[256,160]{1,0:T(8,128)(2,1)S(1)} %get-tuple-element.20.even_ref, bf16[256,160]{1,0:T(8,128)(2,1)S(1)} %get-tuple-element.21.odd_ref, bf16[4,5120]{1,0:T(4,128)(2,1)S(1)} %get-tuple-element.22.cotan_ref, ...), custom_call_target="tpu_custom_call" | custom-call | tf_op jit(solution)/shard_map/pallas_call | solution.py:287
  15.0 2.1 %collective-permute-start.2 = (bf16[4,240,128]{2,1,0:T(8,128)(2,1)S(1)}, bf16[4,240,128]{2,1,0:T(8,128)(2,1)S(1)}, u32[]{:S(2)}, u32[]{:S(2)}) collective-permute-start(bf16[4,240,128]{2,1,0:T(8,128)(2,1)S(1)} %get-tuple-element.25), channel_id=1, source_target_pairs={{0,1},{1,0},{2,3},{3,2},{4,5},{5,4},{6,7},{7,6},{8,9},{9,8},{10,11... | collective-permute-start | bytes 737288 | tf_op jit(solution)/shard_map/ppermute | solution.py:296
  17.2 1.3 %collective-permute-done.2.got_ref = bf16[4,240,128]{2,1,0:T(8,128)(2,1)S(1)} collective-permute-done((bf16[4,240,128]{2,1,0:T(8,128)(2,1)S(1)}, bf16[4,240,128]{2,1,0:T(8,128)(2,1)S(1)}, u32[]{:S(2)}, u32[]{:S(2)}) %collective-permute-start.2) | collective-permute-done | bytes 245792 | tf_op jit(solution)/shard_map/ppermute | solution.py:296
  18.4 0.1 shard_map.94
  18.5 8.9 %all_to_all.15.got_ref = bf16[4,272,128]{2,1,0:T(8,128)(2,1)S(1)} all-to-all(bf16[4,272,128]{2,1,0:T(8,128)(2,1)S(1)} %shard_map.94), channel_id=1, replica_groups=mesh['x'=4,'zlo'=6,'zhi'=2,'y'=8,'core'=2] {'x'}, dimensions={0} | all-to-all | bytes 557056 | tf_op jit(solution)/shard_map/all_to_all | solution.py:298
  27.4 0.1 shard_map.95
  27.4 22.6 %all_to_all.16.own_ref.got_ref = bf16[12,120,128]{2,1,0:T(8,128)(2,1)S(1)} all-to-all(bf16[12,120,128]{2,1,0:T(8,128)(2,1)S(1)} %shard_map.95), channel_id=1, replica_groups=mesh['x'=4,'zlo'=6,'zhi'=2,'y'=8,'core'=2] {'zlo','zhi'}, dimensions={0} | all-to-all | bytes 737280 | tf_op jit(solution)/shard_map/all_to_all | solution.py:302
  50.0 0.7 shard_map.97
  50.7 0.0 copy-start
  50.7 0.0 copy-start.2
  50.7 0.0 copy-start.3
  50.7 16.0 %all-to-all-start.2 = ((bf16[16,40,128]{2,1,0:T(8,128)(2,1)}), bf16[16,40,128]{2,1,0:T(8,128)(2,1)S(1)}, u32[]{:S(2)}, u32[]{:S(2)}) async-start(bf16[16,40,128]{2,1,0:T(8,128)(2,1)} %shard_map.97), calls=%async_computation.2 | async-start | bytes 327680 | tf_op jit(solution)/shard_map/all_to_all | solution.py:305
  66.7 0.0 copy-start.1
  66.7 2.1 %collective-permute-start.3 = (bf16[12,120,128]{2,1,0:T(8,128)(2,1)S(1)}, bf16[12,120,128]{2,1,0:T(8,128)(2,1)S(1)}, u32[]{:S(2)}, u32[]{:S(2)}) collective-permute-start(bf16[12,120,128]{2,1,0:T(8,128)(2,1)S(1)} %all_to_all.16.own_ref.got_ref), channel_id=1, source_target_pairs={{0,1},{1,0},{2,3},{3,2},{4,5},{5,4},{6,7},{7,6},{8,9},{9,8},{10,11... | collective-permute-start | bytes 1105928 | tf_op jit(solution)/shard_map/ppermute | solution.py:303
  68.8 0.0 copy-done
  68.9 3.6 %collective-permute-start = (bf16[1,10240]{1,0:T(2,128)(2,1)S(1)}, bf16[1,10240]{1,0:T(2,128)(2,1)S(1)}, u32[]{:S(2)}, u32[]{:S(2)}) collective-permute-start(bf16[1,10240]{1,0:T(2,128)(2,1)S(1)} %slice_bitcast_fusion), channel_id=1, source_target_pairs={{0,1},{1,2},{2,3},{3,4},{4,5},{5,6},{6,7},{7,8},{8,9},{9,10},{10,1... | collective-permute-start | bytes 61448 | tf_op jit(solution)/shard_map/ppermute | solution.py:263
  72.4 0.0 copy-done.2
  72.4 0.0 copy-done.3
  72.5 0.0 copy-done.1
  72.5 3.7 %all-to-all-done.2.got_ref = bf16[16,40,128]{2,1,0:T(8,128)(2,1)S(1)} async-done(((bf16[16,40,128]{2,1,0:T(8,128)(2,1)}), bf16[16,40,128]{2,1,0:T(8,128)(2,1)S(1)}, u32[]{:S(2)}, u32[]{:S(2)}) %all-to-all-start.2) | async-done | bytes 163872 | tf_op jit(solution)/shard_map/all_to_all | solution.py:305
  76.2 0.8 shard_map.99
  77.0 0.0 collective-permute-done.above_ref
  77.0 0.0 collective-permute-done.3.other_ref
  77.0 1.7 %shard_map.96 = (bf16[4,5120]{1,0:T(4,128)(2,1)}, bf16[8,10240]{1,0:T(8,128)(2,1)}) custom-call(bf16[8,10240]{1,0:T(8,128)(2,1)S(1)} %bitcast.7, bf16[1,10240]{1,0:T(2,128)(2,1)S(1)} %collective-permute-done.above_ref, bf16[256,160]{1,0:T(8,128)(2,1)S(1)} %get-tuple-element.20.even_ref, bf16[256,160]{1,0:T(8,128)(2,1)S(1)} %get-tuple-element.21.odd_ref, ...), custom_call_target="tpu_custom_call" | custom-call | tf_op jit(solution)/shard_map/pallas_call | solution.py:306
  (2 shorter events, 0.1 us)
Async XLA Ops:
  0.6 13.6 %collective-permute-start.1 = (bf16[4,5120]{1,0:T(4,128)(2,1)}, bf16[4,5120]{1,0:T(4,128)(2,1)S(1)}, u32[]{:S(2)}, u32[]{:S(2)}) collective-permute-start(bf16[4,5120]{1,0:T(4,128)(2,1)} %bitcast.8), channel_id=1, source_target_pairs={{1,0},{2,1},{3,2},{4,3},{5,4},{6,5},{7,6},{8,7},{9,8},{10,9},{11,1... | collective-permute-start | bytes 122888 | tf_op jit(solution)/shard_map/ppermute | solution.py:263
  15.0 3.4 %collective-permute-start.2 = (bf16[4,240,128]{2,1,0:T(8,128)(2,1)S(1)}, bf16[4,240,128]{2,1,0:T(8,128)(2,1)S(1)}, u32[]{:S(2)}, u32[]{:S(2)}) collective-permute-start(bf16[4,240,128]{2,1,0:T(8,128)(2,1)S(1)} %get-tuple-element.25), channel_id=1, source_target_pairs={{0,1},{1,0},{2,3},{3,2},{4,5},{5,4},{6,7},{7,6},{8,9},{9,8},{10,11... | collective-permute-start | bytes 737288 | tf_op jit(solution)/shard_map/ppermute | solution.py:296
  50.7 18.1 %copy-start = (bf16[1,8,10240]{2,1,0:T(8,128)(2,1)S(1)}, bf16[1,8,10240]{2,1,0:T(8,128)(2,1)}, u32[]{:S(2)}) copy-start(bf16[1,8,10240]{2,1,0:T(8,128)(2,1)} %param.5) | copy-start | bytes 491524
  50.7 21.7 %copy-start.2 = (f32[60,160]{1,0:T(8,128)S(1)}, f32[60,160]{1,0:T(8,128)}, u32[]{:S(2)}) copy-start(f32[60,160]{1,0:T(8,128)} %one_ref.1) | copy-start | bytes 115204
  50.7 21.7 %copy-start.3 = (f32[60,160]{1,0:T(8,128)S(1)}, f32[60,160]{1,0:T(8,128)}, u32[]{:S(2)}) copy-start(f32[60,160]{1,0:T(8,128)} %two_ref.1) | copy-start | bytes 115204
  50.7 25.5 %all-to-all-start.2 = ((bf16[16,40,128]{2,1,0:T(8,128)(2,1)}), bf16[16,40,128]{2,1,0:T(8,128)(2,1)S(1)}, u32[]{:S(2)}, u32[]{:S(2)}) async-start(bf16[16,40,128]{2,1,0:T(8,128)(2,1)} %shard_map.97), calls=%async_computation.2 | async-start | bytes 327680 | tf_op jit(solution)/shard_map/all_to_all | solution.py:305
  66.7 5.8 %copy-start.1 = (f32[60,160]{1,0:T(8,128)S(1)}, f32[60,160]{1,0:T(8,128)}, u32[]{:S(2)}) copy-start(f32[60,160]{1,0:T(8,128)} %weight_ref.1) | copy-start | bytes 115204
  66.7 10.3 %collective-permute-start.3 = (bf16[12,120,128]{2,1,0:T(8,128)(2,1)S(1)}, bf16[12,120,128]{2,1,0:T(8,128)(2,1)S(1)}, u32[]{:S(2)}, u32[]{:S(2)}) collective-permute-start(bf16[12,120,128]{2,1,0:T(8,128)(2,1)S(1)} %all_to_all.16.own_ref.got_ref), channel_id=1, source_target_pairs={{0,1},{1,0},{2,3},{3,2},{4,5},{5,4},{6,7},{7,6},{8,9},{9,8},{10,11... | collective-permute-start | bytes 1105928 | tf_op jit(solution)/shard_map/ppermute | solution.py:303
  68.9 8.1 %collective-permute-start = (bf16[1,10240]{1,0:T(2,128)(2,1)S(1)}, bf16[1,10240]{1,0:T(2,128)(2,1)S(1)}, u32[]{:S(2)}, u32[]{:S(2)}) collective-permute-start(bf16[1,10240]{1,0:T(2,128)(2,1)S(1)} %slice_bitcast_fusion), channel_id=1, source_target_pairs={{0,1},{1,2},{2,3},{3,4},{4,5},{5,6},{6,7},{7,8},{8,9},{9,10},{10,1... | collective-permute-start | bytes 61448 | tf_op jit(solution)/shard_map/ppermute | solution.py:263

commit v6 on v5

--- a/solution.py
+++ b/solution.py
@@ -24,6 +24,7 @@
 GRAD_ROWS = 6 * PIECE
 SEND_ONE = GRAD_ROWS + 32
 SEND_TWO = PIECE + 80
+SWAP_ROWS = GRAD_ROWS + PIECE
 
 
 def call(kernel, outs, scratch=(), ins=None, limit=16):
@@ -51,6 +52,14 @@
     return ref[:, 640 * g : 640 * g + 640].astype(F32)
 
 
+def every(offset, across=False):
+    shape, short, long = ((256, 32), 1, 0) if across else ((32, 256), 0, 1)
+    hit = lax.broadcasted_iota(jnp.int32, shape, long) == 8 * lax.broadcasted_iota(
+        jnp.int32, shape, short
+    ) + offset
+    return hit.astype(F32).astype(BF16)
+
+
 def pack(rows):
     tail = rows[:, 128:160]
     side = jnp.concatenate([tail[8 * b : 8 * b + 8] for b in range(4)], axis=1)
@@ -65,7 +74,7 @@
 
 def prepare_kernel(
     image_hbm, cotan_hbm, weight_hbm,
-    even_ref, odd_ref, cotan_ref, rows_ref,
+    even_ref, odd_ref, cotan_ref, rows_ref, edge_ref,
     image_ref, own_ref, weight_ref, done,
 ):
     reads = [
@@ -78,8 +87,12 @@
     for read in reads:
         read.wait()
     tiles = tile_rows(read_block, image_ref, 16)
-    even_ref[...] = jnp.concatenate(tiles[0::2], axis=0).astype(BF16)
-    odd_ref[...] = jnp.concatenate(tiles[1::2], axis=0).astype(BF16)
+    even = jnp.concatenate(tiles[0::2], axis=0).astype(BF16)
+    odd = jnp.concatenate(tiles[1::2], axis=0).astype(BF16)
+    even_ref[...] = even
+    odd_ref[...] = odd
+    edge_ref[0] = jnp.dot(every(7), even, preferred_element_type=F32).astype(BF16)
+    edge_ref[1] = jnp.dot(every(7), odd, preferred_element_type=F32).astype(BF16)
     weight_ref[0:60] = own_ref[...]
     weight_ref[60:64] = jnp.zeros((4, C), F32)
     quarter = 2 * lax.axis_index("core") + lax.axis_index("zhi")
@@ -93,15 +106,14 @@
 
 
 def grad_kernel(
-    even_ref, odd_ref, cotan_ref, below_ref,
-    keep_ref, give_ref, taps_ref,
+    even_ref, odd_ref, cotan_ref, edge_ref,
+    keep_ref, give_ref, taps_ref, first_ref,
     five_ref, spread_ref, sums_ref,
 ):
     even = even_ref[...]
     odd = odd_ref[...]
     five_ref[...] = jnp.zeros_like(five_ref)
     five_ref[0:4] = cotan_ref[...].astype(F32)
-    five_ref[4:5] = below_ref[0:1].astype(F32)
     out_row = lax.broadcasted_iota(jnp.int32, (24, 8), 0)
     in_row = lax.broadcasted_iota(jnp.int32, (24, 8), 1)
     pick = (2 * in_row + out_row // 8 - 1 == out_row % 8).astype(F32).astype(BF16)
@@ -133,12 +145,54 @@
             at = slice(PIECE * low, PIECE * low + PIECE)
             keep_ref[x, at] = jnp.where(first, halves[0], halves[1]).astype(BF16)
             give_ref[x, at] = jnp.where(first, halves[1], halves[0]).astype(BF16)
-
-
-def core_sum_kernel(keep_ref, got_ref, rows_ref, send_ref):
+    top = jnp.dot(every(0), taps[1], preferred_element_type=F32)
+    first_ref[...] = top.astype(BF16)
+    edges = [edge_ref[0].astype(F32), edge_ref[1].astype(F32), top, jnp.zeros_like(top)]
+    for k in range(4):
+        give_ref[k, GRAD_ROWS:SWAP_ROWS] = pack(edges[k]).astype(BF16)
+
+
+def core_sum_kernel(
+    keep_ref, got_ref, rows_ref, edge_ref, first_ref, next_zero_ref, next_one_ref,
+    send_ref, below_ref,
+    edge_sum_ref,
+):
+    first = lax.axis_index("core") == 0
+
+    def other(k):
+        return unpack(got_ref[k, GRAD_ROWS:SWAP_ROWS].astype(F32))
+
+    def both(k):
+        mine, yours = edge_ref[k].astype(F32), other(k)
+        pair = [jnp.where(first, mine, yours), jnp.where(first, yours, mine)]
+        return jnp.concatenate(pair, axis=0).astype(BF16)
+
+    inner = jnp.where(first, other(2), first_ref[...].astype(F32))
+    flat = next_zero_ref[...].astype(F32) + next_one_ref[...].astype(F32)
+    outer = jnp.concatenate([flat[0:1, C * j : C * j + C] for j in range(32)], axis=0)
+    below_ref[...] = jnp.where(first, inner, outer).astype(BF16)
+    zero = jnp.zeros((1, C), F32)
+    rights = [
+        jnp.concatenate([inner[1:32], zero, outer[1:32], zero], axis=0).astype(BF16),
+        jnp.concatenate([inner, outer], axis=0).astype(BF16),
+    ]
+    even, odd = both(0), both(1)
+    edge_sum_ref[480:512] = jnp.zeros((32, C), F32)
+    for s, left in ((0, odd), (1, even), (2, odd)):
+        edge_sum_ref[C * s : C * s + C] = lax.dot_general(
+            left, rights[min(s, 1)], (((0,), (0,)), ((), ())), preferred_element_type=F32
+        )
     for x in range(4):
-        total = keep_ref[x].astype(F32) + got_ref[x].astype(F32)
-        send_ref[x, 0:GRAD_ROWS] = total.astype(BF16)
+        total = keep_ref[x].astype(F32) + got_ref[x, 0:GRAD_ROWS].astype(F32)
+        parts = []
+        for low in range(6):
+            part = total[PIECE * low : PIECE * low + PIECE]
+            start = 60 * (6 * x + low)
+            if start < 480:
+                halves = [edge_sum_ref[start + 30 * c : start + 30 * c + 32] for c in range(2)]
+                part = part + pack(jnp.where(first, halves[0], halves[1]))
+            parts.append(part)
+        send_ref[x, 0:GRAD_ROWS] = jnp.concatenate(parts, axis=0).astype(BF16)
         send_ref[x, GRAD_ROWS:SEND_ONE] = rows_ref[...]
 
 
@@ -176,7 +230,7 @@
 
 
 def conv_kernel(
-    image_ref, above_ref, even_ref, odd_ref, taps_ref, own_ref, other_ref,
+    image_ref, above_ref, even_ref, odd_ref, taps_ref, below_ref, own_ref, other_ref,
     out_ref, grad_ref,
     kernel_ref, shift_ref, roll_ref,
 ):
@@ -226,6 +280,8 @@
         rows = jnp.concatenate([wide[2 * i : 2 * i + 1] for i in range(4)], axis=0)
         out_ref[:, 640 * g : 640 * g + 640] = rows.astype(BF16)
     taps = [taps_ref[r] for r in range(3)]
+    last = jnp.dot(every(7, True), below_ref[...], preferred_element_type=F32)
+    taps[0] = (taps[0].astype(F32) + last).astype(BF16)
     after = [jnp.concatenate([t[8:256], zeros], axis=0) for t in taps]
     grad_even = dot_t(taps[0], tap(0, 1)) + dot_t(taps[1], tap(1, 1)) + dot_t(taps[2], tap(2, 1))
     grad_odd = dot_t(taps[0], tap(0, 2)) + dot_t(taps[1], tap(1, 2)) + dot_t(taps[2], tap(2, 2))
@@ -267,14 +323,19 @@
     shape = jax.ShapeDtypeStruct
     image = image.reshape(8, 64 * C)
     cotangent = cotangent.reshape(4, 32 * C)
-    below = from_behind(cotangent, -1)
-    even, odd, strip, rows = call(
+    axes = ("zhi", "y", "core")
+    next_chip = []
+    for core in range(2):
+        route = [(i, i - 2 + core) for i in range(2, 32, 2)]
+        next_chip.append(lax.ppermute(cotangent, axes, route))
+    even, odd, strip, rows, edge = call(
         prepare_kernel,
         [
             shape((256, C), BF16),
             shape((256, C), BF16),
             shape((4, 32 * C), BF16),
             shape((32, 128), BF16),
+            shape((2, 32, C), BF16),
         ],
         [
             pltpu.VMEM((8, 64 * C), BF16),
@@ -284,17 +345,26 @@
         ],
         [pl.BlockSpec(memory_space=pltpu.HBM)] * 3,
     )(*[pltpu.with_memory_space_constraint(a, pltpu.HBM) for a in (image, cotangent, weight)])
-    keep, give, taps = call(
+    keep, give, taps, first = call(
         grad_kernel,
-        [shape((4, GRAD_ROWS, 128), BF16)] * 2 + [shape((3, 256, C), BF16)],
+        [
+            shape((4, GRAD_ROWS, 128), BF16),
+            shape((4, SWAP_ROWS, 128), BF16),
+            shape((3, 256, C), BF16),
+            shape((32, C), BF16),
+        ],
         [
             pltpu.VMEM((8, 32 * C), F32),
             pltpu.VMEM((24, 32 * C), F32),
             pltpu.VMEM((1448, C), F32),
         ],
-    )(even, odd, strip, below)
+    )(even, odd, strip, edge)
     given = lax.ppermute(give, "core", [(0, 1), (1, 0)])
-    send_one = call(core_sum_kernel, shape((4, SEND_ONE, 128), BF16))(keep, given, rows)
+    send_one, under = call(
+        core_sum_kernel,
+        [shape((4, SEND_ONE, 128), BF16), shape((32, C), BF16)],
+        [pltpu.VMEM((512, C), F32)],
+    )(keep, given, rows, edge, first, *next_chip)
     got_one = lax.all_to_all(send_one, "x", 0, 0, tiled=True)
     above = from_behind(image[7:8], 1)
     kept = call(decay_kernel, [shape((60, C), F32)] * 3)(weight, moment_one, moment_two)
@@ -311,7 +381,7 @@
             pltpu.VMEM((16, 64 * C), F32),
             pltpu.VMEM((264, C), F32),
         ],
-    )(image, above, even, odd, taps, got_two, other)
+    )(image, above, even, odd, taps, under, got_two, other)
     new_weight, new_one, new_two = call(
         adam_kernel, [shape((60, C), F32)] * 3, [pltpu.VMEM((64, C), F32)]
     )(got_three, *kept)

time: 79.1 us -> 79.7 us (level)
  starting transfers between devices: 36.2 us -> 32.3 us
  waiting for transfers between devices: 4.96 us -> 8.24 us
    ppermute x2 -> x1, starting transfers between devices: 15.9 us -> 3.55 us  [from_behind(): return lax.ppermute(block, axes, route)]
    ppermute x1, starting transfers between devices: 2.14 us -> 12.4 us  [body(): given = lax.ppermute(give, 'core', [(0, 1), (1, 0)])]
    ppermute x0 -> x2, waiting for transfers between devices: none -> 4.54 us  [body(): next_chip.append(lax.ppermute(cotangent, axes, route))]
    all_to_all x1, starting transfers between devices: 16 us -> 12.3 us  [body(): got_three = lax.all_to_all(send_three, ('y', 'core'), 0, 0, tiled=True)]
    ppermute x0 -> x2, starting transfers between devices: none -> 1.96 us  [body(): next_chip.append(lax.ppermute(cotangent, axes, route))]
    ppermute x1, waiting for transfers between devices: 1.26 us -> 0.01 us  [body(): given = lax.ppermute(give, 'core', [(0, 1), (1, 0)])]
  transfers between devices with their start and end apart: 5 -> 6, of which waited for: 2 -> 2; matrix products, arithmetic and copies ran while one was open for 0% -> 0% of each run, Pallas kernels for 2% -> 1%
where the time goes in v6:
time: 79.7 us; the launch traced here: 79.3 us
  starting transfers between devices  32.3 us (41%)
  blocking collectives  31.9 us (40%)
  waiting for transfers between devices  8.24 us (10%)
  Pallas kernels  6.01 us (8%)
    all_to_all x1, blocking collectives, body(): got_two = lax.all_to_all(send_two, ('zlo', 'zhi'), 0, 0, tiled=True)  22.4 us
    ppermute x1, starting transfers between devices, body(): given = lax.ppermute(give, 'core', [(0, 1), (1, 0)])  12.4 us
    all_to_all x1, starting transfers between devices, body(): got_three = lax.all_to_all(send_three, ('y', 'core'), 0, 0, tiled=True)  12.3 us
    all_to_all x1, blocking collectives, body(): got_one = lax.all_to_all(send_one, 'x', 0, 0, tiled=True)  9.46 us
    ppermute x2, waiting for transfers between devices, body(): next_chip.append(lax.ppermute(cotangent, axes, route))  4.54 us
    all_to_all x1, waiting for transfers between devices, body(): got_three = lax.all_to_all(send_three, ('y', 'core'), 0, 0, tiled=True)  3.69 us
    ppermute x1, starting transfers between devices, from_behind(): return lax.ppermute(block, axes, route)  3.55 us
    ppermute x1, starting transfers between devices, body(): other = lax.ppermute(got_two, 'core', [(0, 1), (1, 0)])  2.14 us
  transfers between devices with their start and end apart: 6, of which 2 were waited for; matrix products, arithmetic and copies ran while one was open for 0% of the time, Pallas kernels for 1%

profile of v6, /device:TPU:1, one launch (start us, length us, event | category | flops | bytes accessed | tf_op | source)
XLA Modules:
  0.0 79.3 jit_solution(18293252416456747033)
XLA Ops:
  0.6 1.3 %shard_map.92 = (bf16[256,160]{1,0:T(8,128)(2,1)S(1)}, bf16[256,160]{1,0:T(8,128)(2,1)S(1)}, bf16[4,5120]{1,0:T(4,128)(2,1)S(1)}, bf16[32,128]{1,0:T(8,128)(2,1)S(1)}, bf16[2,32,160]{2,1,0:T(8,128)(2,1)S(1)}) custom-call(bf16[8,10240]{1,0:T(8,128)(2,1)} %bitcast.6, bf16[4,5120]{1,0:T(4,128)(2,1)} %bitcast.8, f32[60,160]{1,0:T(8,128)} %weight_ref.1), custom_call_target="tpu_custom_call" | custom-call | tf_op jit(solution)/shard_map/pallas_call | solution.py:331
  1.9 0.0 copy-start.4
  1.9 0.9 %shard_map.93 = (bf16[4,240,128]{2,1,0:T(8,128)(2,1)S(1)}, bf16[4,280,128]{2,1,0:T(8,128)(2,1)S(1)}, bf16[3,256,160]{2,1,0:T(8,128)(2,1)S(1)}, bf16[32,160]{1,0:T(8,128)(2,1)S(1)}) custom-call(bf16[256,160]{1,0:T(8,128)(2,1)S(1)} %get-tuple-element.24.even_ref, bf16[256,160]{1,0:T(8,128)(2,1)S(1)} %get-tuple-element.25.odd_ref, ...), custom_call_target="tpu_custom_call" | custom-call | tf_op jit(solution)/shard_map/pallas_call | solution.py:348
  2.8 12.4 %collective-permute-start.1 = (bf16[4,280,128]{2,1,0:T(8,128)(2,1)S(1)}, bf16[4,280,128]{2,1,0:T(8,128)(2,1)S(1)}, u32[]{:S(2)}, u32[]{:S(2)}) collective-permute-start(bf16[4,280,128]{2,1,0:T(8,128)(2,1)S(1)} %get-tuple-element.30), channel_id=1, source_target_pairs={{0,1},{1,0},{2,3},{3,2},{4,5},{5,4},{6,7},{7,6},{8,9},{9,8},{10,11... | collective-permute-start | bytes 860168 | tf_op jit(solution)/shard_map/ppermute | solution.py:362
  15.2 0.0 copy-done.4
  15.2 0.7 collective-permute-start.2
  15.9 1.3 %collective-permute-start.3 = (bf16[4,5120]{1,0:T(4,128)(2,1)S(1)}, bf16[4,5120]{1,0:T(4,128)(2,1)S(1)}, u32[]{:S(2)}, u32[]{:S(2)}) collective-permute-start(bf16[4,5120]{1,0:T(4,128)(2,1)S(1)} %bitcast.10), channel_id=1, source_target_pairs={{2,1},{4,3},{6,5},{8,7},{10,9},{12,11},{14,13},{16,15},{18,17},{20... | collective-permute-start | bytes 122888 | tf_op jit(solution)/shard_map/ppermute | solution.py:330
  17.2 0.0 collective-permute-done.2.next_zero_ref
  17.2 4.5 %collective-permute-done.3.next_one_ref = bf16[4,5120]{1,0:T(4,128)(2,1)S(1)} collective-permute-done((bf16[4,5120]{1,0:T(4,128)(2,1)S(1)}, bf16[4,5120]{1,0:T(4,128)(2,1)S(1)}, u32[]{:S(2)}, u32[]{:S(2)}) %collective-permute-start.3) | collective-permute-done | bytes 40992 | tf_op jit(solution)/shard_map/ppermute | solution.py:330
  21.7 0.0 collective-permute-done.1.got_ref
  21.7 0.4 shard_map.94
  22.1 9.5 %all_to_all.15.got_ref = bf16[4,272,128]{2,1,0:T(8,128)(2,1)S(1)} all-to-all(bf16[4,272,128]{2,1,0:T(8,128)(2,1)S(1)} %get-tuple-element.34), channel_id=1, replica_groups=mesh['x'=4,'zlo'=6,'zhi'=2,'y'=8,'core'=2] {'x'}, dimensions={0} | all-to-all | bytes 557056 | tf_op jit(solution)/shard_map/all_to_all | solution.py:368
  31.6 0.1 shard_map.95
  31.6 22.4 %all_to_all.16.own_ref.got_ref = bf16[12,120,128]{2,1,0:T(8,128)(2,1)S(1)} all-to-all(bf16[12,120,128]{2,1,0:T(8,128)(2,1)S(1)} %shard_map.95), channel_id=1, replica_groups=mesh['x'=4,'zlo'=6,'zhi'=2,'y'=8,'core'=2] {'zlo','zhi'}, dimensions={0} | all-to-all | bytes 737280 | tf_op jit(solution)/shard_map/all_to_all | solution.py:372
  54.1 0.7 shard_map.97
  54.8 0.0 copy-start
  54.8 0.0 copy-start.2
  54.8 0.0 copy-start.3
  54.8 12.3 %all-to-all-start.2 = ((bf16[16,40,128]{2,1,0:T(8,128)(2,1)}), bf16[16,40,128]{2,1,0:T(8,128)(2,1)S(1)}, u32[]{:S(2)}, u32[]{:S(2)}) async-start(bf16[16,40,128]{2,1,0:T(8,128)(2,1)} %shard_map.97), calls=%async_computation.2 | async-start | bytes 327680 | tf_op jit(solution)/shard_map/all_to_all | solution.py:375
  67.1 0.0 copy-start.1
  67.1 2.1 %collective-permute-start.4 = (bf16[12,120,128]{2,1,0:T(8,128)(2,1)S(1)}, bf16[12,120,128]{2,1,0:T(8,128)(2,1)S(1)}, u32[]{:S(2)}, u32[]{:S(2)}) collective-permute-start(bf16[12,120,128]{2,1,0:T(8,128)(2,1)S(1)} %all_to_all.16.own_ref.got_ref), channel_id=1, source_target_pairs={{0,1},{1,0},{2,3},{3,2},{4,5},{5,4},{6,7},{7,6},{8,9},{9,8},{10,11... | collective-permute-start | bytes 1105928 | tf_op jit(solution)/shard_map/ppermute | solution.py:373
  69.2 0.0 copy-done
  69.3 3.6 %collective-permute-start = (bf16[1,10240]{1,0:T(2,128)(2,1)S(1)}, bf16[1,10240]{1,0:T(2,128)(2,1)S(1)}, u32[]{:S(2)}, u32[]{:S(2)}) collective-permute-start(bf16[1,10240]{1,0:T(2,128)(2,1)S(1)} %slice_bitcast_fusion), channel_id=1, source_target_pairs={{0,1},{1,2},{2,3},{3,4},{4,5},{5,6},{6,7},{7,8},{8,9},{9,10},{10,1... | collective-permute-start | bytes 61448 | tf_op jit(solution)/shard_map/ppermute | solution.py:319
  72.9 0.0 copy-done.2
  72.9 0.0 copy-done.3
  72.9 0.0 copy-done.1
  72.9 3.7 %all-to-all-done.2.got_ref = bf16[16,40,128]{2,1,0:T(8,128)(2,1)S(1)} async-done(((bf16[16,40,128]{2,1,0:T(8,128)(2,1)}), bf16[16,40,128]{2,1,0:T(8,128)(2,1)S(1)}, u32[]{:S(2)}, u32[]{:S(2)}) %all-to-all-start.2) | async-done | bytes 163872 | tf_op jit(solution)/shard_map/all_to_all | solution.py:375
  76.6 0.8 shard_map.99
  77.4 0.0 collective-permute-done.above_ref
  77.4 0.0 collective-permute-done.4.other_ref
  77.4 1.9 %shard_map.96 = (bf16[4,5120]{1,0:T(4,128)(2,1)}, bf16[8,10240]{1,0:T(8,128)(2,1)}) custom-call(bf16[8,10240]{1,0:T(8,128)(2,1)S(1)} %bitcast.7, bf16[1,10240]{1,0:T(2,128)(2,1)S(1)} %collective-permute-done.above_ref, bf16[256,160]{1,0:T(8,128)(2,1)S(1)} %get-tuple-element.24.even_ref, bf16[256,160]{1,0:T(8,128)(2,1)S(1)} %get-tuple-element.25.odd_ref, ...), custom_call_target="tpu_custom_call" | custom-call | tf_op jit(solution)/shard_map/pallas_call | solution.py:376
  (2 shorter events, 0.1 us)
Async XLA Ops:
  1.9 13.3 %copy-start.4 = (bf16[1,4,5120]{2,1,0:T(4,128)(2,1)S(1)}, bf16[1,4,5120]{2,1,0:T(4,128)(2,1)}, u32[]{:S(2)}) copy-start(bf16[1,4,5120]{2,1,0:T(4,128)(2,1)} %param.6) | copy-start | bytes 122884
  2.8 18.9 %collective-permute-start.1 = (bf16[4,280,128]{2,1,0:T(8,128)(2,1)S(1)}, bf16[4,280,128]{2,1,0:T(8,128)(2,1)S(1)}, u32[]{:S(2)}, u32[]{:S(2)}) collective-permute-start(bf16[4,280,128]{2,1,0:T(8,128)(2,1)S(1)} %get-tuple-element.30), channel_id=1, source_target_pairs={{0,1},{1,0},{2,3},{3,2},{4,5},{5,4},{6,7},{7,6},{8,9},{9,8},{10,11... | collective-permute-start | bytes 860168 | tf_op jit(solution)/shard_map/ppermute | solution.py:362
  15.2 2.0 %collective-permute-start.2 = (bf16[4,5120]{1,0:T(4,128)(2,1)S(1)}, bf16[4,5120]{1,0:T(4,128)(2,1)S(1)}, u32[]{:S(2)}, u32[]{:S(2)}) collective-permute-start(bf16[4,5120]{1,0:T(4,128)(2,1)S(1)} %bitcast.9), channel_id=1, source_target_pairs={{2,0},{4,2},{6,4},{8,6},{10,8},{12,10},{14,12},{16,14},{18,16},{20... | collective-permute-start | bytes 122888 | tf_op jit(solution)/shard_map/ppermute | solution.py:330
  15.9 5.8 %collective-permute-start.3 = (bf16[4,5120]{1,0:T(4,128)(2,1)S(1)}, bf16[4,5120]{1,0:T(4,128)(2,1)S(1)}, u32[]{:S(2)}, u32[]{:S(2)}) collective-permute-start(bf16[4,5120]{1,0:T(4,128)(2,1)S(1)} %bitcast.10), channel_id=1, source_target_pairs={{2,1},{4,3},{6,5},{8,7},{10,9},{12,11},{14,13},{16,15},{18,17},{20... | collective-permute-start | bytes 122888 | tf_op jit(solution)/shard_map/ppermute | solution.py:330
  54.8 14.5 %copy-start = (bf16[1,8,10240]{2,1,0:T(8,128)(2,1)S(1)}, bf16[1,8,10240]{2,1,0:T(8,128)(2,1)}, u32[]{:S(2)}) copy-start(bf16[1,8,10240]{2,1,0:T(8,128)(2,1)} %param.5) | copy-start | bytes 491524
  54.8 18.1 %copy-start.2 = (f32[60,160]{1,0:T(8,128)S(1)}, f32[60,160]{1,0:T(8,128)}, u32[]{:S(2)}) copy-start(f32[60,160]{1,0:T(8,128)} %one_ref.1) | copy-start | bytes 115204
  54.8 18.1 %copy-start.3 = (f32[60,160]{1,0:T(8,128)S(1)}, f32[60,160]{1,0:T(8,128)}, u32[]{:S(2)}) copy-start(f32[60,160]{1,0:T(8,128)} %two_ref.1) | copy-start | bytes 115204
  54.8 21.8 %all-to-all-start.2 = ((bf16[16,40,128]{2,1,0:T(8,128)(2,1)}), bf16[16,40,128]{2,1,0:T(8,128)(2,1)S(1)}, u32[]{:S(2)}, u32[]{:S(2)}) async-start(bf16[16,40,128]{2,1,0:T(8,128)(2,1)} %shard_map.97), calls=%async_computation.2 | async-start | bytes 327680 | tf_op jit(solution)/shard_map/all_to_all | solution.py:375
  67.1 5.8 %copy-start.1 = (f32[60,160]{1,0:T(8,128)S(1)}, f32[60,160]{1,0:T(8,128)}, u32[]{:S(2)}) copy-start(f32[60,160]{1,0:T(8,128)} %weight_ref.1) | copy-start | bytes 115204
  67.1 10.3 %collective-permute-start.4 = (bf16[12,120,128]{2,1,0:T(8,128)(2,1)S(1)}, bf16[12,120,128]{2,1,0:T(8,128)(2,1)S(1)}, u32[]{:S(2)}, u32[]{:S(2)}) collective-permute-start(bf16[12,120,128]{2,1,0:T(8,128)(2,1)S(1)} %all_to_all.16.own_ref.got_ref), channel_id=1, source_target_pairs={{0,1},{1,0},{2,3},{3,2},{4,5},{5,4},{6,7},{7,6},{8,9},{9,8},{10,11... | collective-permute-start | bytes 1105928 | tf_op jit(solution)/shard_map/ppermute | solution.py:373
  69.3 8.1 %collective-permute-start = (bf16[1,10240]{1,0:T(2,128)(2,1)S(1)}, bf16[1,10240]{1,0:T(2,128)(2,1)S(1)}, u32[]{:S(2)}, u32[]{:S(2)}) collective-permute-start(bf16[1,10240]{1,0:T(2,128)(2,1)S(1)} %slice_bitcast_fusion), channel_id=1, source_target_pairs={{0,1},{1,2},{2,3},{3,4},{4,5},{5,6},{6,7},{7,8},{8,9},{9,10},{10,1... | collective-permute-start | bytes 61448 | tf_op jit(solution)/shard_map/ppermute | solution.py:319

commit v7 on v6

--- a/solution.py
+++ b/solution.py
@@ -74,7 +74,7 @@
 
 def prepare_kernel(
     image_hbm, cotan_hbm, weight_hbm,
-    even_ref, odd_ref, cotan_ref, rows_ref, edge_ref,
+    even_ref, odd_ref, cotan_ref, rows_ref, edge_ref, trade_ref,
     image_ref, own_ref, weight_ref, done,
 ):
     reads = [
@@ -91,8 +91,17 @@
     odd = jnp.concatenate(tiles[1::2], axis=0).astype(BF16)
     even_ref[...] = even
     odd_ref[...] = odd
-    edge_ref[0] = jnp.dot(every(7), even, preferred_element_type=F32).astype(BF16)
-    edge_ref[1] = jnp.dot(every(7), odd, preferred_element_type=F32).astype(BF16)
+    flat = cotan_ref[...].astype(F32)
+    edges = [
+        jnp.dot(every(7), even, preferred_element_type=F32),
+        jnp.dot(every(7), odd, preferred_element_type=F32),
+        jnp.concatenate([flat[0:1, C * j : C * j + C] for j in range(32)], axis=0),
+    ]
+    for k in range(3):
+        edge_ref[k] = pack(edges[k]).astype(BF16)
+    first = lax.axis_index("core") == 0
+    trade_ref[0] = jnp.where(first, edge_ref[2].astype(F32), edge_ref[0].astype(F32)).astype(BF16)
+    trade_ref[1] = edge_ref[1]
     weight_ref[0:60] = own_ref[...]
     weight_ref[60:64] = jnp.zeros((4, C), F32)
     quarter = 2 * lax.axis_index("core") + lax.axis_index("zhi")
@@ -107,7 +116,7 @@
 
 def grad_kernel(
     even_ref, odd_ref, cotan_ref, edge_ref,
-    keep_ref, give_ref, taps_ref, first_ref,
+    keep_ref, give_ref, taps_ref,
     five_ref, spread_ref, sums_ref,
 ):
     even = even_ref[...]
@@ -145,38 +154,39 @@
             at = slice(PIECE * low, PIECE * low + PIECE)
             keep_ref[x, at] = jnp.where(first, halves[0], halves[1]).astype(BF16)
             give_ref[x, at] = jnp.where(first, halves[1], halves[0]).astype(BF16)
-    top = jnp.dot(every(0), taps[1], preferred_element_type=F32)
-    first_ref[...] = top.astype(BF16)
-    edges = [edge_ref[0].astype(F32), edge_ref[1].astype(F32), top, jnp.zeros_like(top)]
-    for k in range(4):
-        give_ref[k, GRAD_ROWS:SWAP_ROWS] = pack(edges[k]).astype(BF16)
+    for k in range(3):
+        give_ref[k, GRAD_ROWS:SWAP_ROWS] = edge_ref[k]
+    give_ref[3, GRAD_ROWS:SWAP_ROWS] = edge_ref[2]
 
 
 def core_sum_kernel(
-    keep_ref, got_ref, rows_ref, edge_ref, first_ref, next_zero_ref, next_one_ref,
-    send_ref, below_ref,
+    keep_ref, got_ref, rows_ref, edge_ref, trade_ref,
+    send_ref, below_ref, above_ref,
     edge_sum_ref,
 ):
     first = lax.axis_index("core") == 0
-
-    def other(k):
-        return unpack(got_ref[k, GRAD_ROWS:SWAP_ROWS].astype(F32))
-
-    def both(k):
-        mine, yours = edge_ref[k].astype(F32), other(k)
-        pair = [jnp.where(first, mine, yours), jnp.where(first, yours, mine)]
-        return jnp.concatenate(pair, axis=0).astype(BF16)
-
-    inner = jnp.where(first, other(2), first_ref[...].astype(F32))
-    flat = next_zero_ref[...].astype(F32) + next_one_ref[...].astype(F32)
-    outer = jnp.concatenate([flat[0:1, C * j : C * j + C] for j in range(32)], axis=0)
-    below_ref[...] = jnp.where(first, inner, outer).astype(BF16)
+    mine = [unpack(edge_ref[k].astype(F32)) for k in range(3)]
+    partner = [unpack(got_ref[k, GRAD_ROWS:SWAP_ROWS].astype(F32)) for k in range(3)]
+    far = [unpack(trade_ref[k].astype(F32)) for k in range(2)]
+
+    def choose(zero, one):
+        return jnp.where(first, zero, one)
+
+    inner_cotan, outer_cotan = choose(partner[2], mine[2]), choose(mine[2], far[0])
     zero = jnp.zeros((1, C), F32)
     rights = [
-        jnp.concatenate([inner[1:32], zero, outer[1:32], zero], axis=0).astype(BF16),
-        jnp.concatenate([inner, outer], axis=0).astype(BF16),
+        jnp.concatenate([inner_cotan[1:32], zero, outer_cotan[1:32], zero], axis=0).astype(BF16),
+        jnp.concatenate([inner_cotan, outer_cotan], axis=0).astype(BF16),
     ]
-    even, odd = both(0), both(1)
+    even, odd = [
+        jnp.concatenate(
+            [choose(mine[k], partner[k]), choose(far[k], mine[k])], axis=0
+        ).astype(BF16)
+        for k in range(2)
+    ]
+    below_ref[...] = choose(partner[2], far[0]).astype(BF16)
+    for k in range(2):
+        above_ref[k] = choose(far[k], partner[k]).astype(BF16)
     edge_sum_ref[480:512] = jnp.zeros((32, C), F32)
     for s, left in ((0, odd), (1, even), (2, odd)):
         edge_sum_ref[C * s : C * s + C] = lax.dot_general(
@@ -190,16 +200,10 @@
             start = 60 * (6 * x + low)
             if start < 480:
                 halves = [edge_sum_ref[start + 30 * c : start + 30 * c + 32] for c in range(2)]
-                part = part + pack(jnp.where(first, halves[0], halves[1]))
+                part = part + pack(choose(*halves))
             parts.append(part)
         send_ref[x, 0:GRAD_ROWS] = jnp.concatenate(parts, axis=0).astype(BF16)
         send_ref[x, GRAD_ROWS:SEND_ONE] = rows_ref[...]
-
-
-def decay_kernel(weight_ref, one_ref, two_ref, kept_ref, kept_one_ref, kept_two_ref):
-    kept_ref[...] = weight_ref[...] - learn_rate * decay_rate * weight_ref[...]
-    kept_one_ref[...] = beta_one * one_ref[...]
-    kept_two_ref[...] = beta_two * two_ref[...]
 
 
 def first_sum_kernel(got_ref, send_ref):
@@ -230,7 +234,7 @@
 
 
 def conv_kernel(
-    image_ref, above_ref, even_ref, odd_ref, taps_ref, below_ref, own_ref, other_ref,
+    even_ref, odd_ref, taps_ref, below_ref, above_ref, own_ref, other_ref,
     out_ref, grad_ref,
     kernel_ref, shift_ref, roll_ref,
 ):
@@ -262,11 +266,16 @@
     even = even_ref[...]
     odd = odd_ref[...]
     odd_before = jnp.concatenate([zeros, odd[0:248]], axis=0)
-    shift_ref[0:1] = above_ref[...].astype(F32)
-    shift_ref[1:9] = image_ref[...].astype(F32)
-    tiles = tile_rows(lambda ref, g: ref[0:8, 640 * g : 640 * g + 640], shift_ref, 16)
-    even_down = jnp.concatenate(tiles[0::2], axis=0).astype(BF16)
-    odd_down = jnp.concatenate(tiles[1::2], axis=0).astype(BF16)
+    start_row = lax.broadcasted_iota(jnp.int32, (256, C), 0) % 8 == 0
+
+    def down(columns, above):
+        shift_ref[8:264] = columns.astype(F32)
+        top = jnp.dot(every(0, True), above, preferred_element_type=F32)
+        return jnp.where(start_row, top, shift_ref[7:263]).astype(BF16)
+
+    shift_ref[0:8] = jnp.zeros((8, C), F32)
+    even_down = down(even, above_ref[0])
+    odd_down = down(odd, above_ref[1])
     odd_down_before = jnp.concatenate([zeros, odd_down[0:248]], axis=0)
     roll_ref[0:256] = dot(even, tap(2, 1)) + dot(odd, tap(2, 2)) + dot(odd_before, tap(2, 0))
     roll_ref[256:264] = jnp.zeros((8, C), F32)
@@ -302,40 +311,31 @@
             total = total + got_ref[2 * y + core].astype(F32)
         sums_ref[30 * core : 30 * core + 32] = unpack(total)
     gradient = sums_ref[0:60] / float(COUNT)
-    new_one = one_ref[...] + (1.0 - beta_one) * gradient
-    new_two = two_ref[...] + (1.0 - beta_two) * gradient * gradient
+    weight = weight_ref[...]
+    new_one = beta_one * one_ref[...] + (1.0 - beta_one) * gradient
+    new_two = beta_two * two_ref[...] + (1.0 - beta_two) * gradient * gradient
     first_hat = new_one / (1.0 - beta_one**adam_step)
     second_hat = new_two / (1.0 - beta_two**adam_step)
-    new_weight_ref[...] = weight_ref[...] - learn_rate * (
-        first_hat / (jnp.sqrt(second_hat) + epsilon)
+    new_weight_ref[...] = weight - learn_rate * (
+        first_hat / (jnp.sqrt(second_hat) + epsilon) + decay_rate * weight
     )
     new_one_ref[...] = new_one
     new_two_ref[...] = new_two
-
-
-def from_behind(block, distance):
-    axes = ("zhi", "y", "core")
-    route = [(i - distance, i) for i in range(32) if 0 <= i - distance < 32]
-    return lax.ppermute(block, axes, route)
 
 
 def body(image, cotangent, weight, moment_one, moment_two):
     shape = jax.ShapeDtypeStruct
     image = image.reshape(8, 64 * C)
     cotangent = cotangent.reshape(4, 32 * C)
-    axes = ("zhi", "y", "core")
-    next_chip = []
-    for core in range(2):
-        route = [(i, i - 2 + core) for i in range(2, 32, 2)]
-        next_chip.append(lax.ppermute(cotangent, axes, route))
-    even, odd, strip, rows, edge = call(
+    even, odd, strip, rows, edge, trade = call(
         prepare_kernel,
         [
             shape((256, C), BF16),
             shape((256, C), BF16),
             shape((4, 32 * C), BF16),
             shape((32, 128), BF16),
-            shape((2, 32, C), BF16),
+            shape((3, PIECE, 128), BF16),
+            shape((2, PIECE, 128), BF16),
         ],
         [
             pltpu.VMEM((8, 64 * C), BF16),
@@ -345,13 +345,14 @@
         ],
         [pl.BlockSpec(memory_space=pltpu.HBM)] * 3,
     )(*[pltpu.with_memory_space_constraint(a, pltpu.HBM) for a in (image, cotangent, weight)])
-    keep, give, taps, first = call(
+    route = [(i, i - 1 if i % 2 == 0 else i + 1) for i in range(1, 31)]
+    traded = lax.ppermute(trade, ("zhi", "y", "core"), route)
+    keep, give, taps = call(
         grad_kernel,
         [
             shape((4, GRAD_ROWS, 128), BF16),
             shape((4, SWAP_ROWS, 128), BF16),
             shape((3, 256, C), BF16),
-            shape((32, C), BF16),
         ],
         [
             pltpu.VMEM((8, 32 * C), F32),
@@ -360,14 +361,12 @@
         ],
     )(even, odd, strip, edge)
     given = lax.ppermute(give, "core", [(0, 1), (1, 0)])
-    send_one, under = call(
+    send_one, below, above = call(
         core_sum_kernel,
-        [shape((4, SEND_ONE, 128), BF16), shape((32, C), BF16)],
+        [shape((4, SEND_ONE, 128), BF16), shape((32, C), BF16), shape((2, 32, C), BF16)],
         [pltpu.VMEM((512, C), F32)],
-    )(keep, given, rows, edge, first, *next_chip)
+    )(keep, given, rows, edge, traded)
     got_one = lax.all_to_all(send_one, "x", 0, 0, tiled=True)
-    above = from_behind(image[7:8], 1)
-    kept = call(decay_kernel, [shape((60, C), F32)] * 3)(weight, moment_one, moment_two)
     send_two = call(first_sum_kernel, shape((12, SEND_TWO, 128), BF16))(got_one)
     got_two = lax.all_to_all(send_two, ("zlo", "zhi"), 0, 0, tiled=True)
     other = lax.ppermute(got_two, "core", [(0, 1), (1, 0)])
@@ -378,13 +377,13 @@
         [shape((4, 32 * C), BF16), shape((8, 64 * C), BF16)],
         [
             pltpu.VMEM((1448, C), F32),
-            pltpu.VMEM((16, 64 * C), F32),
             pltpu.VMEM((264, C), F32),
-        ],
-    )(image, above, even, odd, taps, under, got_two, other)
+            pltpu.VMEM((264, C), F32),
+        ],
+    )(even, odd, taps, below, above, got_two, other)
     new_weight, new_one, new_two = call(
         adam_kernel, [shape((60, C), F32)] * 3, [pltpu.VMEM((64, C), F32)]
-    )(got_three, *kept)
+    )(got_three, weight, moment_one, moment_two)
     return (output[None], grad_image[None], new_weight, new_one, new_two)
 
 

time: 79.7 us -> 77.1 us (0.967)
  blocking collectives: 31.9 us -> 40.2 us
  waiting for transfers between devices: 8.24 us -> 3.18 us
  starting transfers between devices: 32.3 us -> 27.3 us
    all_to_all x0 -> x1, blocking collectives: none -> 14.2 us  [body(): got_three = lax.all_to_all(send_three, ('y', 'core'), 0, 0, tiled=True)]
    all_to_all x1 -> x0, starting transfers between devices: 12.3 us -> none  [body(): got_three = lax.all_to_all(send_three, ('y', 'core'), 0, 0, tiled=True)]
    ppermute x1, starting transfers between devices: 2.14 us -> 13 us  [body(): other = lax.ppermute(got_two, 'core', [(0, 1), (1, 0)])]
    all_to_all x1, blocking collectives: 22.4 us -> 18.1 us  [body(): got_two = lax.all_to_all(send_two, ('zlo', 'zhi'), 0, 0, tiled=True)]
    all_to_all x1 -> x0, waiting for transfers between devices: 3.69 us -> none  [body(): got_three = lax.all_to_all(send_three, ('y', 'core'), 0, 0, tiled=True)]
    ppermute x3 -> x1, starting transfers between devices: 5.51 us -> 1.92 us  [body(): traded = lax.ppermute(trade, ('zhi', 'y', 'core'), route)]
    all_to_all x1, blocking collectives: 9.46 us -> 7.97 us  [body(): got_one = lax.all_to_all(send_one, 'x', 0, 0, tiled=True)]
    ppermute x3 -> x1, waiting for transfers between devices: 4.54 us -> 3.17 us  [body(): traded = lax.ppermute(trade, ('zhi', 'y', 'core'), route)]
  transfers between devices with their start and end apart: 6 -> 3, of which waited for: 2 -> 1; matrix products, arithmetic and copies ran while one was open for 0% -> 0% of each run, Pallas kernels for 1% -> 1%
where the time goes in v7:
time: 77.1 us; the launch traced here: 76.8 us
  blocking collectives  40.2 us (52%)
  starting transfers between devices  27.3 us (35%)
  Pallas kernels  5.4 us (7%)
  waiting for transfers between devices  3.18 us (4%)
    all_to_all x1, blocking collectives, body(): got_two = lax.all_to_all(send_two, ('zlo', 'zhi'), 0, 0, tiled=True)  18.1 us
    all_to_all x1, blocking collectives, body(): got_three = lax.all_to_all(send_three, ('y', 'core'), 0, 0, tiled=True)  14.2 us
    ppermute x1, starting transfers between devices, body(): other = lax.ppermute(got_two, 'core', [(0, 1), (1, 0)])  13 us
    ppermute x1, starting transfers between devices, body(): given = lax.ppermute(give, 'core', [(0, 1), (1, 0)])  12.4 us
    all_to_all x1, blocking collectives, body(): got_one = lax.all_to_all(send_one, 'x', 0, 0, tiled=True)  7.97 us
    ppermute x1, waiting for transfers between devices, body(): traded = lax.ppermute(trade, ('zhi', 'y', 'core'), route)  3.17 us
    pallas_call x1, Pallas kernels, body(): call(conv_kernel, [shape((4, 32 * C), BF16), shape((8, 64 * C), BF16)], [...  1.98 us
    ppermute x1, starting transfers between devices, body(): traded = lax.ppermute(trade, ('zhi', 'y', 'core'), route)  1.92 us
  transfers between devices with their start and end apart: 3, of which 1 were waited for; matrix products, arithmetic and copies ran while one was open for 0% of the time, Pallas kernels for 1%

profile of v7, /device:TPU:1, one launch (start us, length us, event | category | flops | bytes accessed | tf_op | source)
XLA Modules:
  0.0 76.8 jit_solution(4719983035439895934)
XLA Ops:
  0.6 1.3 %shard_map.92 = (bf16[256,160]{1,0:T(8,128)(2,1)S(1)}, bf16[256,160]{1,0:T(8,128)(2,1)S(1)}, bf16[4,5120]{1,0:T(4,128)(2,1)S(1)}, bf16[32,128]{1,0:T(8,128)(2,1)...) custom-call(bf16[8,10240]{1,0:T(8,128)(2,1)} %bitcast.4, bf16[4,5120]{1,0:T(4,128)(2,1)} %bitcast.5, ...), custom_call_target="tpu_custom_call" | custom-call | tf_op jit(solution)/shard_map/pallas_call | solution.py:330
  2.0 0.8 %shard_map.93 = (bf16[4,240,128]{2,1,0:T(8,128)(2,1)S(1)}, bf16[4,280,128]{2,1,0:T(8,128)(2,1)S(1)}, bf16[3,256,160]{2,1,0:T(8,128)(2,1)S(1)}) custom-call(bf16[256,160]{1,0:T(8,128)(2,1)S(1)} %get-tuple-element.22.even_ref, bf16[256,160]{1,0:T(8,128)(2,1)S(1)} %get-tuple-element.23.odd_ref, bf16[4,5120]{1,0:T(4,128)(2,1)S(1)} %get-tuple-element.24.cotan_ref, ...), custom_call_target="tpu_custom_call" | custom-call | tf_op jit(solution)/shard_map/pallas_call | solution.py:350
  2.8 12.4 %collective-permute-start = (bf16[4,280,128]{2,1,0:T(8,128)(2,1)S(1)}, bf16[4,280,128]{2,1,0:T(8,128)(2,1)S(1)}, u32[]{:S(2)}, u32[]{:S(2)}) collective-permute-start(bf16[4,280,128]{2,1,0:T(8,128)(2,1)S(1)} %get-tuple-element.28), channel_id=1, source_target_pairs={{0,1},{1,0},{2,3},{3,2},{4,5},{5,4},{6,7},{7,6},{8,9},{9,8},{10,11... | collective-permute-start | bytes 860168 | tf_op jit(solution)/shard_map/ppermute | solution.py:363
  15.2 1.9 %collective-permute-start.1 = (bf16[2,40,128]{2,1,0:T(8,128)(2,1)S(1)}, bf16[2,40,128]{2,1,0:T(8,128)(2,1)S(1)}, u32[]{:S(2)}, u32[]{:S(2)}) collective-permute-start(bf16[2,40,128]{2,1,0:T(8,128)(2,1)S(1)} %get-tuple-element.30), channel_id=1, source_target_pairs={{1,2},{2,1},{3,4},{4,3},{5,6},{6,5},{7,8},{8,7},{9,10},{10,9},{11,... | collective-permute-start | bytes 61448 | tf_op jit(solution)/shard_map/ppermute | solution.py:349
  17.1 3.2 %collective-permute-done.1.trade_ref = bf16[2,40,128]{2,1,0:T(8,128)(2,1)S(1)} collective-permute-done((bf16[2,40,128]{2,1,0:T(8,128)(2,1)S(1)}, bf16[2,40,128]{2,1,0:T(8,128)(2,1)S(1)}, u32[]{:S(2)}, u32[]{:S(2)}) %collective-permute-start.1) | collective-permute-done | bytes 20512 | tf_op jit(solution)/shard_map/ppermute | solution.py:349
  20.3 0.0 collective-permute-done.got_ref
  20.3 0.4 shard_map.94
  20.7 8.0 %all_to_all.15.got_ref = bf16[4,272,128]{2,1,0:T(8,128)(2,1)S(1)} all-to-all(bf16[4,272,128]{2,1,0:T(8,128)(2,1)S(1)} %get-tuple-element.33), channel_id=1, replica_groups=mesh['x'=4,'zlo'=6,'zhi'=2,'y'=8,'core'=2] {'x'}, dimensions={0} | all-to-all | bytes 557056 | tf_op jit(solution)/shard_map/all_to_all | solution.py:369
  28.7 0.1 shard_map.95
  28.7 18.1 %all_to_all.16.own_ref.got_ref = bf16[12,120,128]{2,1,0:T(8,128)(2,1)S(1)} all-to-all(bf16[12,120,128]{2,1,0:T(8,128)(2,1)S(1)} %shard_map.95), channel_id=1, replica_groups=mesh['x'=4,'zlo'=6,'zhi'=2,'y'=8,'core'=2] {'zlo','zhi'}, dimensions={0} | all-to-all | bytes 737280 | tf_op jit(solution)/shard_map/all_to_all | solution.py:371
  46.8 13.0 %collective-permute-start.2 = (bf16[12,120,128]{2,1,0:T(8,128)(2,1)S(1)}, bf16[12,120,128]{2,1,0:T(8,128)(2,1)S(1)}, u32[]{:S(2)}, u32[]{:S(2)}) collective-permute-start(bf16[12,120,128]{2,1,0:T(8,128)(2,1)S(1)} %all_to_all.16.own_ref.got_ref), channel_id=1, source_target_pairs={{0,1},{1,0},{2,3},{3,2},{4,5},{5,4},{6,7},{7,6},{8,9},{9,8},{10,11... | collective-permute-start | bytes 1105928 | tf_op jit(solution)/shard_map/ppermute | solution.py:372
  59.8 0.0 copy-start
  59.8 0.0 copy-start.1
  59.8 0.0 copy-start.2
  59.8 14.2 %all_to_all.17.got_ref = bf16[16,40,128]{2,1,0:T(8,128)(2,1)S(1)} all-to-all(bf16[16,40,128]{2,1,0:T(8,128)(2,1)S(1)} %shard_map.97), channel_id=1, replica_groups=mesh['x'=4,'zlo'=6,'zhi'=2,'y'=8,'core'=2] {'y','core'}, dimensions={0} | all-to-all | bytes 327680 | tf_op jit(solution)/shard_map/all_to_all | solution.py:374
  74.0 0.0 copy-done
  74.0 0.0 copy-done.1
  74.0 0.0 copy-done.2
  74.0 0.8 %shard_map.98 = (f32[60,160]{1,0:T(8,128)}, f32[60,160]{1,0:T(8,128)}, f32[60,160]{1,0:T(8,128)}) custom-call(bf16[16,40,128]{2,1,0:T(8,128)(2,1)S(1)} %all_to_all.17.got_ref, f32[60,160]{1,0:T(8,128)S(1)} %copy-done, f32[60,160]{1,0:T(8,128)S(1)} %copy-done.1, f32[60,160]{1,0:T(8,128)S(1)} %copy-done.2), custom_call_target="tpu_custom_call" | custom-call | tf_op jit(solution)/shard_map/pallas_call | solution.py:384
  74.8 0.0 collective-permute-done.2.other_ref
  74.8 2.0 %shard_map.96 = (bf16[4,5120]{1,0:T(4,128)(2,1)}, bf16[8,10240]{1,0:T(8,128)(2,1)}) custom-call(bf16[256,160]{1,0:T(8,128)(2,1)S(1)} %get-tuple-element.22.even_ref, bf16[256,160]{1,0:T(8,128)(2,1)S(1)} %get-tuple-element.23.odd_ref, bf16[3,256,160]{2,1,0:T(8,128)(2,1)S(1)} %get-tuple-element.26.taps_ref, bf16[32,160]{1,0:T(8,128)(2,1)S(1)} %get-tuple-element.31.below_ref, ...), custom_call_target="tpu_custom_call" | custom-call | tf_op jit(solution)/shard_map/pallas_call | solution.py:375
  (1 shorter events, 0.0 us)
Async XLA Ops:
  2.8 17.5 %collective-permute-start = (bf16[4,280,128]{2,1,0:T(8,128)(2,1)S(1)}, bf16[4,280,128]{2,1,0:T(8,128)(2,1)S(1)}, u32[]{:S(2)}, u32[]{:S(2)}) collective-permute-start(bf16[4,280,128]{2,1,0:T(8,128)(2,1)S(1)} %get-tuple-element.28), channel_id=1, source_target_pairs={{0,1},{1,0},{2,3},{3,2},{4,5},{5,4},{6,7},{7,6},{8,9},{9,8},{10,11... | collective-permute-start | bytes 860168 | tf_op jit(solution)/shard_map/ppermute | solution.py:363
  15.2 5.1 %collective-permute-start.1 = (bf16[2,40,128]{2,1,0:T(8,128)(2,1)S(1)}, bf16[2,40,128]{2,1,0:T(8,128)(2,1)S(1)}, u32[]{:S(2)}, u32[]{:S(2)}) collective-permute-start(bf16[2,40,128]{2,1,0:T(8,128)(2,1)S(1)} %get-tuple-element.30), channel_id=1, source_target_pairs={{1,2},{2,1},{3,4},{4,3},{5,6},{6,5},{7,8},{8,7},{9,10},{10,9},{11,... | collective-permute-start | bytes 61448 | tf_op jit(solution)/shard_map/ppermute | solution.py:349
  46.8 28.0 %collective-permute-start.2 = (bf16[12,120,128]{2,1,0:T(8,128)(2,1)S(1)}, bf16[12,120,128]{2,1,0:T(8,128)(2,1)S(1)}, u32[]{:S(2)}, u32[]{:S(2)}) collective-permute-start(bf16[12,120,128]{2,1,0:T(8,128)(2,1)S(1)} %all_to_all.16.own_ref.got_ref), channel_id=1, source_target_pairs={{0,1},{1,0},{2,3},{3,2},{4,5},{5,4},{6,7},{7,6},{8,9},{9,8},{10,11... | collective-permute-start | bytes 1105928 | tf_op jit(solution)/shard_map/ppermute | solution.py:372
  59.8 14.2 %copy-start = (f32[60,160]{1,0:T(8,128)S(1)}, f32[60,160]{1,0:T(8,128)}, u32[]{:S(2)}) copy-start(f32[60,160]{1,0:T(8,128)} %weight_ref.1) | copy-start | bytes 115204
  59.8 14.2 %copy-start.1 = (f32[60,160]{1,0:T(8,128)S(1)}, f32[60,160]{1,0:T(8,128)}, u32[]{:S(2)}) copy-start(f32[60,160]{1,0:T(8,128)} %one_ref.1) | copy-start | bytes 115204
  59.8 14.2 %copy-start.2 = (f32[60,160]{1,0:T(8,128)S(1)}, f32[60,160]{1,0:T(8,128)}, u32[]{:S(2)}) copy-start(f32[60,160]{1,0:T(8,128)} %two_ref.1) | copy-start | bytes 115204

commit v8 on v7

--- a/solution.py
+++ b/solution.py
@@ -217,7 +217,7 @@
     heads = [got_ref[x, GRAD_ROWS : GRAD_ROWS + 16] for x in range(4)]
     for low in range(6):
         for high in range(2):
-            n = 2 * low + high
+            n = 6 * high + low
             send_ref[n, 0:PIECE] = total[PIECE * low : PIECE * low + PIECE]
             for x in range(4):
                 send_ref[n, PIECE + 16 * x : PIECE + 16 * x + 16] = heads[x]
@@ -243,7 +243,7 @@
         for low in range(6):
             for c in range(2):
                 for high in range(2):
-                    n = 2 * low + high
+                    n = 6 * high + low
                     own = own_ref[n, PIECE:SEND_TWO].astype(F32)
                     other = other_ref[n, PIECE:SEND_TWO].astype(F32)
                     block = jnp.where(core == c, own, other)
@@ -368,7 +368,7 @@
     )(keep, given, rows, edge, traded)
     got_one = lax.all_to_all(send_one, "x", 0, 0, tiled=True)
     send_two = call(first_sum_kernel, shape((12, SEND_TWO, 128), BF16))(got_one)
-    got_two = lax.all_to_all(send_two, ("zlo", "zhi"), 0, 0, tiled=True)
+    got_two = lax.all_to_all(send_two, ("zhi", "zlo"), 0, 0, tiled=True)
     other = lax.ppermute(got_two, "core", [(0, 1), (1, 0)])
     send_three = call(second_sum_kernel, shape((16, PIECE, 128), BF16))(got_two)
     got_three = lax.all_to_all(send_three, ("y", "core"), 0, 0, tiled=True)

time: 77.1 us -> 77.9 us (1.010)
    all_to_all x1, blocking collectives: 18.1 us -> 20.4 us  [body(): got_two = lax.all_to_all(send_two, ('zhi', 'zlo'), 0, 0, tiled=True)]
    all_to_all x1, blocking collectives: 14.2 us -> 12.4 us  [body(): got_three = lax.all_to_all(send_three, ('y', 'core'), 0, 0, tiled=True)]
where the time goes in v8:
time: 77.9 us; the launch traced here: 77.6 us
  blocking collectives  40.8 us (52%)
  starting transfers between devices  27.5 us (35%)
  Pallas kernels  5.38 us (7%)
  waiting for transfers between devices  3.18 us (4%)
    all_to_all x1, blocking collectives, body(): got_two = lax.all_to_all(send_two, ('zhi', 'zlo'), 0, 0, tiled=True)  20.4 us
    ppermute x1, starting transfers between devices, body(): other = lax.ppermute(got_two, 'core', [(0, 1), (1, 0)])  13.2 us
    all_to_all x1, blocking collectives, body(): got_three = lax.all_to_all(send_three, ('y', 'core'), 0, 0, tiled=True)  12.4 us
    ppermute x1, starting transfers between devices, body(): given = lax.ppermute(give, 'core', [(0, 1), (1, 0)])  12.4 us
    all_to_all x1, blocking collectives, body(): got_one = lax.all_to_all(send_one, 'x', 0, 0, tiled=True)  7.97 us
    ppermute x1, waiting for transfers between devices, body(): traded = lax.ppermute(trade, ('zhi', 'y', 'core'), route)  3.17 us
    pallas_call x1, Pallas kernels, body(): call(conv_kernel, [shape((4, 32 * C), BF16), shape((8, 64 * C), BF16)], [...  1.97 us
    ppermute x1, starting transfers between devices, body(): traded = lax.ppermute(trade, ('zhi', 'y', 'core'), route)  1.92 us
  transfers between devices with their start and end apart: 3, of which 1 were waited for; matrix products, arithmetic and copies ran while one was open for 0% of the time, Pallas kernels for 1%

profile of v8, /device:TPU:1, one launch (start us, length us, event | category | flops | bytes accessed | tf_op | source)
XLA Modules:
  0.0 77.6 jit_solution(11853923044890917820)
XLA Ops:
  0.6 1.3 %shard_map.92 = (bf16[256,160]{1,0:T(8,128)(2,1)S(1)}, bf16[256,160]{1,0:T(8,128)(2,1)S(1)}, bf16[4,5120]{1,0:T(4,128)(2,1)S(1)}, bf16[32,128]{1,0:T(8,128)(2,1)...) custom-call(bf16[8,10240]{1,0:T(8,128)(2,1)} %bitcast.4, bf16[4,5120]{1,0:T(4,128)(2,1)} %bitcast.5, ...), custom_call_target="tpu_custom_call" | custom-call | tf_op jit(solution)/shard_map/pallas_call | solution.py:330
  2.0 0.8 %shard_map.93 = (bf16[4,240,128]{2,1,0:T(8,128)(2,1)S(1)}, bf16[4,280,128]{2,1,0:T(8,128)(2,1)S(1)}, bf16[3,256,160]{2,1,0:T(8,128)(2,1)S(1)}) custom-call(bf16[256,160]{1,0:T(8,128)(2,1)S(1)} %get-tuple-element.22.even_ref, bf16[256,160]{1,0:T(8,128)(2,1)S(1)} %get-tuple-element.23.odd_ref, bf16[4,5120]{1,0:T(4,128)(2,1)S(1)} %get-tuple-element.24.cotan_ref, ...), custom_call_target="tpu_custom_call" | custom-call | tf_op jit(solution)/shard_map/pallas_call | solution.py:350
  2.8 12.4 %collective-permute-start = (bf16[4,280,128]{2,1,0:T(8,128)(2,1)S(1)}, bf16[4,280,128]{2,1,0:T(8,128)(2,1)S(1)}, u32[]{:S(2)}, u32[]{:S(2)}) collective-permute-start(bf16[4,280,128]{2,1,0:T(8,128)(2,1)S(1)} %get-tuple-element.28), channel_id=1, source_target_pairs={{0,1},{1,0},{2,3},{3,2},{4,5},{5,4},{6,7},{7,6},{8,9},{9,8},{10,11... | collective-permute-start | bytes 860168 | tf_op jit(solution)/shard_map/ppermute | solution.py:363
  15.2 1.9 %collective-permute-start.1 = (bf16[2,40,128]{2,1,0:T(8,128)(2,1)S(1)}, bf16[2,40,128]{2,1,0:T(8,128)(2,1)S(1)}, u32[]{:S(2)}, u32[]{:S(2)}) collective-permute-start(bf16[2,40,128]{2,1,0:T(8,128)(2,1)S(1)} %get-tuple-element.30), channel_id=1, source_target_pairs={{1,2},{2,1},{3,4},{4,3},{5,6},{6,5},{7,8},{8,7},{9,10},{10,9},{11,... | collective-permute-start | bytes 61448 | tf_op jit(solution)/shard_map/ppermute | solution.py:349
  17.1 3.2 %collective-permute-done.1.trade_ref = bf16[2,40,128]{2,1,0:T(8,128)(2,1)S(1)} collective-permute-done((bf16[2,40,128]{2,1,0:T(8,128)(2,1)S(1)}, bf16[2,40,128]{2,1,0:T(8,128)(2,1)S(1)}, u32[]{:S(2)}, u32[]{:S(2)}) %collective-permute-start.1) | collective-permute-done | bytes 20512 | tf_op jit(solution)/shard_map/ppermute | solution.py:349
  20.3 0.0 collective-permute-done.got_ref
  20.3 0.4 shard_map.94
  20.7 8.0 %all_to_all.15.got_ref = bf16[4,272,128]{2,1,0:T(8,128)(2,1)S(1)} all-to-all(bf16[4,272,128]{2,1,0:T(8,128)(2,1)S(1)} %get-tuple-element.33), channel_id=1, replica_groups=mesh['x'=4,'zlo'=6,'zhi'=2,'y'=8,'core'=2] {'x'}, dimensions={0} | all-to-all | bytes 557056 | tf_op jit(solution)/shard_map/all_to_all | solution.py:369
  28.7 20.4 %all_to_all.16.own_ref.got_ref = bf16[12,120,128]{2,1,0:T(8,128)(2,1)S(1)} all-to-all(bf16[12,120,128]{2,1,0:T(8,128)(2,1)S(1)} %shard_map.95), channel_id=1, replica_groups=mesh['x'=4,'zlo'=6,'zhi'=2,'y'=8,'core'=2] {'zhi','zlo'}, dimensions={0} | all-to-all | bytes 737280 | tf_op jit(solution)/shard_map/all_to_all | solution.py:371
  49.1 13.2 %collective-permute-start.2 = (bf16[12,120,128]{2,1,0:T(8,128)(2,1)S(1)}, bf16[12,120,128]{2,1,0:T(8,128)(2,1)S(1)}, u32[]{:S(2)}, u32[]{:S(2)}) collective-permute-start(bf16[12,120,128]{2,1,0:T(8,128)(2,1)S(1)} %all_to_all.16.own_ref.got_ref), channel_id=1, source_target_pairs={{0,1},{1,0},{2,3},{3,2},{4,5},{5,4},{6,7},{7,6},{8,9},{9,8},{10,11... | collective-permute-start | bytes 1105928 | tf_op jit(solution)/shard_map/ppermute | solution.py:372
  62.3 0.0 copy-start
  62.4 0.0 copy-start.1
  62.4 0.0 copy-start.2
  62.4 12.4 %all_to_all.17.got_ref = bf16[16,40,128]{2,1,0:T(8,128)(2,1)S(1)} all-to-all(bf16[16,40,128]{2,1,0:T(8,128)(2,1)S(1)} %shard_map.97), channel_id=1, replica_groups=mesh['x'=4,'zlo'=6,'zhi'=2,'y'=8,'core'=2] {'y','core'}, dimensions={0} | all-to-all | bytes 327680 | tf_op jit(solution)/shard_map/all_to_all | solution.py:374
  74.8 0.0 copy-done
  74.8 0.0 copy-done.1
  74.8 0.0 copy-done.2
  74.8 0.8 shard_map.98
  75.6 0.0 collective-permute-done.2.other_ref
  75.6 2.0 %shard_map.96 = (bf16[4,5120]{1,0:T(4,128)(2,1)}, bf16[8,10240]{1,0:T(8,128)(2,1)}) custom-call(bf16[256,160]{1,0:T(8,128)(2,1)S(1)} %get-tuple-element.22.even_ref, bf16[256,160]{1,0:T(8,128)(2,1)S(1)} %get-tuple-element.23.odd_ref, bf16[3,256,160]{2,1,0:T(8,128)(2,1)S(1)} %get-tuple-element.26.taps_ref, bf16[32,160]{1,0:T(8,128)(2,1)S(1)} %get-tuple-element.31.below_ref, ...), custom_call_target="tpu_custom_call" | custom-call | tf_op jit(solution)/shard_map/pallas_call | solution.py:375
  (2 shorter events, 0.1 us)
Async XLA Ops:
  2.8 17.5 %collective-permute-start = (bf16[4,280,128]{2,1,0:T(8,128)(2,1)S(1)}, bf16[4,280,128]{2,1,0:T(8,128)(2,1)S(1)}, u32[]{:S(2)}, u32[]{:S(2)}) collective-permute-start(bf16[4,280,128]{2,1,0:T(8,128)(2,1)S(1)} %get-tuple-element.28), channel_id=1, source_target_pairs={{0,1},{1,0},{2,3},{3,2},{4,5},{5,4},{6,7},{7,6},{8,9},{9,8},{10,11... | collective-permute-start | bytes 860168 | tf_op jit(solution)/shard_map/ppermute | solution.py:363
  15.2 5.1 %collective-permute-start.1 = (bf16[2,40,128]{2,1,0:T(8,128)(2,1)S(1)}, bf16[2,40,128]{2,1,0:T(8,128)(2,1)S(1)}, u32[]{:S(2)}, u32[]{:S(2)}) collective-permute-start(bf16[2,40,128]{2,1,0:T(8,128)(2,1)S(1)} %get-tuple-element.30), channel_id=1, source_target_pairs={{1,2},{2,1},{3,4},{4,3},{5,6},{6,5},{7,8},{8,7},{9,10},{10,9},{11,... | collective-permute-start | bytes 61448 | tf_op jit(solution)/shard_map/ppermute | solution.py:349
  49.1 26.5 %collective-permute-start.2 = (bf16[12,120,128]{2,1,0:T(8,128)(2,1)S(1)}, bf16[12,120,128]{2,1,0:T(8,128)(2,1)S(1)}, u32[]{:S(2)}, u32[]{:S(2)}) collective-permute-start(bf16[12,120,128]{2,1,0:T(8,128)(2,1)S(1)} %all_to_all.16.own_ref.got_ref), channel_id=1, source_target_pairs={{0,1},{1,0},{2,3},{3,2},{4,5},{5,4},{6,7},{7,6},{8,9},{9,8},{10,11... | collective-permute-start | bytes 1105928 | tf_op jit(solution)/shard_map/ppermute | solution.py:372
  62.3 12.5 %copy-start = (f32[60,160]{1,0:T(8,128)S(1)}, f32[60,160]{1,0:T(8,128)}, u32[]{:S(2)}) copy-start(f32[60,160]{1,0:T(8,128)} %weight_ref.1) | copy-start | bytes 115204
  62.4 12.5 %copy-start.1 = (f32[60,160]{1,0:T(8,128)S(1)}, f32[60,160]{1,0:T(8,128)}, u32[]{:S(2)}) copy-start(f32[60,160]{1,0:T(8,128)} %one_ref.1) | copy-start | bytes 115204
  62.4 12.5 %copy-start.2 = (f32[60,160]{1,0:T(8,128)S(1)}, f32[60,160]{1,0:T(8,128)}, u32[]{:S(2)}) copy-start(f32[60,160]{1,0:T(8,128)} %two_ref.1) | copy-start | bytes 115204

commit v9 on v7

--- a/solution.py
+++ b/solution.py
@@ -346,7 +346,7 @@
         [pl.BlockSpec(memory_space=pltpu.HBM)] * 3,
     )(*[pltpu.with_memory_space_constraint(a, pltpu.HBM) for a in (image, cotangent, weight)])
     route = [(i, i - 1 if i % 2 == 0 else i + 1) for i in range(1, 31)]
-    traded = lax.ppermute(trade, ("zhi", "y", "core"), route)
+    traded = lax.ppermute(trade, ("zhi", "yhi", "ylo", "core"), route)
     keep, give, taps = call(
         grad_kernel,
         [
@@ -371,7 +371,7 @@
     got_two = lax.all_to_all(send_two, ("zlo", "zhi"), 0, 0, tiled=True)
     other = lax.ppermute(got_two, "core", [(0, 1), (1, 0)])
     send_three = call(second_sum_kernel, shape((16, PIECE, 128), BF16))(got_two)
-    got_three = lax.all_to_all(send_three, ("y", "core"), 0, 0, tiled=True)
+    got_three = lax.all_to_all(send_three, ("ylo", "yhi", "core"), 0, 0, tiled=True)
     output, grad_image = call(
         conv_kernel,
         [shape((4, 32 * C), BF16), shape((8, 64 * C), BF16)],
@@ -388,8 +388,8 @@
 
 
 def solution(mesh):
-    fine = Mesh(mesh.devices.reshape(4, 6, 2, 8, 2), ("x", "zlo", "zhi", "y", "core"))
-    dp, space = ("x", "zlo"), ("zhi", "y", "core")
+    fine = Mesh(mesh.devices.reshape(4, 6, 2, 2, 4, 2), ("x", "zlo", "zhi", "yhi", "ylo", "core"))
+    dp, space = ("x", "zlo"), ("zhi", "yhi", "ylo", "core")
     specs = (P(dp, space, None), P(dp, space, None), P(dp, None), P(dp, None), P(dp, None))
 
     return jax.shard_map(body, mesh=fine, in_specs=specs, out_specs=specs, check_vma=False)

time: 77.1 us -> 77.3 us (level)
  no operation moved by 1% of the time
where the time goes in v9:
time: 77.3 us; the launch traced here: 76.9 us
  blocking collectives  40.4 us (52%)
  starting transfers between devices  27.3 us (35%)
  Pallas kernels  5.4 us (7%)
  waiting for transfers between devices  3.18 us (4%)
    all_to_all x1, blocking collectives, body(): got_two = lax.all_to_all(send_two, ('zlo', 'zhi'), 0, 0, tiled=True)  18.1 us
    all_to_all x1, blocking collectives, body(): lax.all_to_all(send_three, ('ylo', 'yhi', 'core'), 0, 0, tiled=True)  14.4 us
    ppermute x1, starting transfers between devices, body(): other = lax.ppermute(got_two, 'core', [(0, 1), (1, 0)])  13 us
    ppermute x1, starting transfers between devices, body(): given = lax.ppermute(give, 'core', [(0, 1), (1, 0)])  12.4 us
    all_to_all x1, blocking collectives, body(): got_one = lax.all_to_all(send_one, 'x', 0, 0, tiled=True)  7.97 us
    ppermute x1, waiting for transfers between devices, body(): traded = lax.ppermute(trade, ('zhi', 'yhi', 'ylo', 'core'), route)  3.17 us
    pallas_call x1, Pallas kernels, body(): call(conv_kernel, [shape((4, 32 * C), BF16), shape((8, 64 * C), BF16)], [...  1.99 us
    ppermute x1, starting transfers between devices, body(): traded = lax.ppermute(trade, ('zhi', 'yhi', 'ylo', 'core'), route)  1.92 us
  transfers between devices with their start and end apart: 3, of which 1 were waited for; matrix products, arithmetic and copies ran while one was open for 0% of the time, Pallas kernels for 1%

profile of v9, /device:TPU:1, one launch (start us, length us, event | category | flops | bytes accessed | tf_op | source)
XLA Modules:
  0.0 76.9 jit_solution(8089071403984632049)
XLA Ops:
  0.6 1.3 %shard_map.92 = (bf16[256,160]{1,0:T(8,128)(2,1)S(1)}, bf16[256,160]{1,0:T(8,128)(2,1)S(1)}, bf16[4,5120]{1,0:T(4,128)(2,1)S(1)}, bf16[32,128]{1,0:T(8,128)(2,1)...) custom-call(bf16[8,10240]{1,0:T(8,128)(2,1)} %bitcast.4, bf16[4,5120]{1,0:T(4,128)(2,1)} %bitcast.5, ...), custom_call_target="tpu_custom_call" | custom-call | tf_op jit(solution)/shard_map/pallas_call | solution.py:330
  2.0 0.8 %shard_map.93 = (bf16[4,240,128]{2,1,0:T(8,128)(2,1)S(1)}, bf16[4,280,128]{2,1,0:T(8,128)(2,1)S(1)}, bf16[3,256,160]{2,1,0:T(8,128)(2,1)S(1)}) custom-call(bf16[256,160]{1,0:T(8,128)(2,1)S(1)} %get-tuple-element.22.even_ref, bf16[256,160]{1,0:T(8,128)(2,1)S(1)} %get-tuple-element.23.odd_ref, bf16[4,5120]{1,0:T(4,128)(2,1)S(1)} %get-tuple-element.24.cotan_ref, ...), custom_call_target="tpu_custom_call" | custom-call | tf_op jit(solution)/shard_map/pallas_call | solution.py:350
  2.8 12.4 %collective-permute-start = (bf16[4,280,128]{2,1,0:T(8,128)(2,1)S(1)}, bf16[4,280,128]{2,1,0:T(8,128)(2,1)S(1)}, u32[]{:S(2)}, u32[]{:S(2)}) collective-permute-start(bf16[4,280,128]{2,1,0:T(8,128)(2,1)S(1)} %get-tuple-element.28), channel_id=1, source_target_pairs={{0,1},{1,0},{2,3},{3,2},{4,5},{5,4},{6,7},{7,6},{8,9},{9,8},{10,11... | collective-permute-start | bytes 860168 | tf_op jit(solution)/shard_map/ppermute | solution.py:363
  15.2 1.9 %collective-permute-start.1 = (bf16[2,40,128]{2,1,0:T(8,128)(2,1)S(1)}, bf16[2,40,128]{2,1,0:T(8,128)(2,1)S(1)}, u32[]{:S(2)}, u32[]{:S(2)}) collective-permute-start(bf16[2,40,128]{2,1,0:T(8,128)(2,1)S(1)} %get-tuple-element.30), channel_id=1, source_target_pairs={{1,2},{2,1},{3,4},{4,3},{5,6},{6,5},{7,8},{8,7},{9,10},{10,9},{11,... | collective-permute-start | bytes 61448 | tf_op jit(solution)/shard_map/ppermute | solution.py:349
  17.1 3.2 %collective-permute-done.1.trade_ref = bf16[2,40,128]{2,1,0:T(8,128)(2,1)S(1)} collective-permute-done((bf16[2,40,128]{2,1,0:T(8,128)(2,1)S(1)}, bf16[2,40,128]{2,1,0:T(8,128)(2,1)S(1)}, u32[]{:S(2)}, u32[]{:S(2)}) %collective-permute-start.1) | collective-permute-done | bytes 20512 | tf_op jit(solution)/shard_map/ppermute | solution.py:349
  20.3 0.0 collective-permute-done.got_ref
  20.3 0.4 shard_map.94
  20.7 8.0 %all_to_all.15.got_ref = bf16[4,272,128]{2,1,0:T(8,128)(2,1)S(1)} all-to-all(bf16[4,272,128]{2,1,0:T(8,128)(2,1)S(1)} %get-tuple-element.33), channel_id=1, replica_groups=mesh['x'=4,'zlo'=6,'zhi'=2,'yhi'=2,'ylo'=4,'core'=2] {'x'}, dimensions={0} | all-to-all | bytes 557056 | tf_op jit(solution)/shard_map/all_to_all | solution.py:369
  28.7 0.1 shard_map.95
  28.7 18.1 %all_to_all.16.own_ref.got_ref = bf16[12,120,128]{2,1,0:T(8,128)(2,1)S(1)} all-to-all(bf16[12,120,128]{2,1,0:T(8,128)(2,1)S(1)} %shard_map.95), channel_id=1, replica_groups=mesh['x'=4,'zlo'=6,'zhi'=2,'yhi'=2,'ylo'=4,'core'=2] {'zlo','zhi'}, dimensions={0} | all-to-all | bytes 737280 | tf_op jit(solution)/shard_map/all_to_all | solution.py:371
  46.8 13.0 %collective-permute-start.2 = (bf16[12,120,128]{2,1,0:T(8,128)(2,1)S(1)}, bf16[12,120,128]{2,1,0:T(8,128)(2,1)S(1)}, u32[]{:S(2)}, u32[]{:S(2)}) collective-permute-start(bf16[12,120,128]{2,1,0:T(8,128)(2,1)S(1)} %all_to_all.16.own_ref.got_ref), channel_id=1, source_target_pairs={{0,1},{1,0},{2,3},{3,2},{4,5},{5,4},{6,7},{7,6},{8,9},{9,8},{10,11... | collective-permute-start | bytes 1105928 | tf_op jit(solution)/shard_map/ppermute | solution.py:372
  59.8 0.0 copy-start
  59.8 0.0 copy-start.1
  59.8 0.0 copy-start.2
  59.8 14.4 %all_to_all.17.got_ref = bf16[16,40,128]{2,1,0:T(8,128)(2,1)S(1)} all-to-all(bf16[16,40,128]{2,1,0:T(8,128)(2,1)S(1)} %shard_map.97), channel_id=1, replica_groups=mesh['x'=4,'zlo'=6,'zhi'=2,'yhi'=2,'ylo'=4,'core'=2] {'ylo','yhi','core'}, dimensions={0} | all-to-all | bytes 327680 | tf_op jit(solution)/shard_map/all_to_all | solution.py:374
  74.2 0.0 copy-done
  74.2 0.0 copy-done.1
  74.2 0.0 copy-done.2
  74.2 0.8 %shard_map.98 = (f32[60,160]{1,0:T(8,128)}, f32[60,160]{1,0:T(8,128)}, f32[60,160]{1,0:T(8,128)}) custom-call(bf16[16,40,128]{2,1,0:T(8,128)(2,1)S(1)} %all_to_all.17.got_ref, f32[60,160]{1,0:T(8,128)S(1)} %copy-done, f32[60,160]{1,0:T(8,128)S(1)} %copy-done.1, f32[60,160]{1,0:T(8,128)S(1)} %copy-done.2), custom_call_target="tpu_custom_call" | custom-call | tf_op jit(solution)/shard_map/pallas_call | solution.py:384
  75.0 0.0 collective-permute-done.2.other_ref
  75.0 2.0 %shard_map.96 = (bf16[4,5120]{1,0:T(4,128)(2,1)}, bf16[8,10240]{1,0:T(8,128)(2,1)}) custom-call(bf16[256,160]{1,0:T(8,128)(2,1)S(1)} %get-tuple-element.22.even_ref, bf16[256,160]{1,0:T(8,128)(2,1)S(1)} %get-tuple-element.23.odd_ref, bf16[3,256,160]{2,1,0:T(8,128)(2,1)S(1)} %get-tuple-element.26.taps_ref, bf16[32,160]{1,0:T(8,128)(2,1)S(1)} %get-tuple-element.31.below_ref, ...), custom_call_target="tpu_custom_call" | custom-call | tf_op jit(solution)/shard_map/pallas_call | solution.py:375
  (1 shorter events, 0.0 us)
Async XLA Ops:
  2.8 17.5 %collective-permute-start = (bf16[4,280,128]{2,1,0:T(8,128)(2,1)S(1)}, bf16[4,280,128]{2,1,0:T(8,128)(2,1)S(1)}, u32[]{:S(2)}, u32[]{:S(2)}) collective-permute-start(bf16[4,280,128]{2,1,0:T(8,128)(2,1)S(1)} %get-tuple-element.28), channel_id=1, source_target_pairs={{0,1},{1,0},{2,3},{3,2},{4,5},{5,4},{6,7},{7,6},{8,9},{9,8},{10,11... | collective-permute-start | bytes 860168 | tf_op jit(solution)/shard_map/ppermute | solution.py:363
  15.2 5.1 %collective-permute-start.1 = (bf16[2,40,128]{2,1,0:T(8,128)(2,1)S(1)}, bf16[2,40,128]{2,1,0:T(8,128)(2,1)S(1)}, u32[]{:S(2)}, u32[]{:S(2)}) collective-permute-start(bf16[2,40,128]{2,1,0:T(8,128)(2,1)S(1)} %get-tuple-element.30), channel_id=1, source_target_pairs={{1,2},{2,1},{3,4},{4,3},{5,6},{6,5},{7,8},{8,7},{9,10},{10,9},{11,... | collective-permute-start | bytes 61448 | tf_op jit(solution)/shard_map/ppermute | solution.py:349
  46.8 28.2 %collective-permute-start.2 = (bf16[12,120,128]{2,1,0:T(8,128)(2,1)S(1)}, bf16[12,120,128]{2,1,0:T(8,128)(2,1)S(1)}, u32[]{:S(2)}, u32[]{:S(2)}) collective-permute-start(bf16[12,120,128]{2,1,0:T(8,128)(2,1)S(1)} %all_to_all.16.own_ref.got_ref), channel_id=1, source_target_pairs={{0,1},{1,0},{2,3},{3,2},{4,5},{5,4},{6,7},{7,6},{8,9},{9,8},{10,11... | collective-permute-start | bytes 1105928 | tf_op jit(solution)/shard_map/ppermute | solution.py:372
  59.8 14.4 %copy-start = (f32[60,160]{1,0:T(8,128)S(1)}, f32[60,160]{1,0:T(8,128)}, u32[]{:S(2)}) copy-start(f32[60,160]{1,0:T(8,128)} %weight_ref.1) | copy-start | bytes 115204
  59.8 14.4 %copy-start.1 = (f32[60,160]{1,0:T(8,128)S(1)}, f32[60,160]{1,0:T(8,128)}, u32[]{:S(2)}) copy-start(f32[60,160]{1,0:T(8,128)} %one_ref.1) | copy-start | bytes 115204
  59.8 14.4 %copy-start.2 = (f32[60,160]{1,0:T(8,128)S(1)}, f32[60,160]{1,0:T(8,128)}, u32[]{:S(2)}) copy-start(f32[60,160]{1,0:T(8,128)} %two_ref.1) | copy-start | bytes 115204

commit v10 on v7

--- a/solution.py
+++ b/solution.py
@@ -110,7 +110,7 @@
         mine = jnp.where(quarter == q, weight_ref[15 * q : 15 * q + 16], mine)
     tail = mine[:, 128:160]
     lane = lax.broadcasted_iota(jnp.int32, (16, 128), 1) // 32
-    tail = jnp.where(lane == lax.axis_index("x"), jnp.concatenate([tail] * 4, axis=1), 0.0)
+    tail = jnp.where(lane == 2 * lax.axis_index("xhi") + lax.axis_index("xlo"), jnp.concatenate([tail] * 4, axis=1), 0.0)
     rows_ref[...] = jnp.concatenate([mine[:, 0:128], tail], axis=0).astype(BF16)
 
 
@@ -202,8 +202,8 @@
                 halves = [edge_sum_ref[start + 30 * c : start + 30 * c + 32] for c in range(2)]
                 part = part + pack(choose(*halves))
             parts.append(part)
-        send_ref[x, 0:GRAD_ROWS] = jnp.concatenate(parts, axis=0).astype(BF16)
-        send_ref[x, GRAD_ROWS:SEND_ONE] = rows_ref[...]
+        send_ref[2 * (x % 2) + x // 2, 0:GRAD_ROWS] = jnp.concatenate(parts, axis=0).astype(BF16)
+        send_ref[2 * (x % 2) + x // 2, GRAD_ROWS:SEND_ONE] = rows_ref[...]
 
 
 def first_sum_kernel(got_ref, send_ref):
@@ -214,7 +214,7 @@
         tail = tail + got_ref[x, GRAD_ROWS + 16 : SEND_ONE].astype(F32)
     total = total.astype(BF16)
     tail = tail.astype(BF16)
-    heads = [got_ref[x, GRAD_ROWS : GRAD_ROWS + 16] for x in range(4)]
+    heads = [got_ref[2 * (x % 2) + x // 2, GRAD_ROWS : GRAD_ROWS + 16] for x in range(4)]
     for low in range(6):
         for high in range(2):
             n = 2 * low + high
@@ -366,7 +366,7 @@
         [shape((4, SEND_ONE, 128), BF16), shape((32, C), BF16), shape((2, 32, C), BF16)],
         [pltpu.VMEM((512, C), F32)],
     )(keep, given, rows, edge, traded)
-    got_one = lax.all_to_all(send_one, "x", 0, 0, tiled=True)
+    got_one = lax.all_to_all(send_one, ("xlo", "xhi"), 0, 0, tiled=True)
     send_two = call(first_sum_kernel, shape((12, SEND_TWO, 128), BF16))(got_one)
     got_two = lax.all_to_all(send_two, ("zlo", "zhi"), 0, 0, tiled=True)
     other = lax.ppermute(got_two, "core", [(0, 1), (1, 0)])
@@ -388,8 +388,8 @@
 
 
 def solution(mesh):
-    fine = Mesh(mesh.devices.reshape(4, 6, 2, 8, 2), ("x", "zlo", "zhi", "y", "core"))
-    dp, space = ("x", "zlo"), ("zhi", "y", "core")
+    fine = Mesh(mesh.devices.reshape(2, 2, 6, 2, 8, 2), ("xhi", "xlo", "zlo", "zhi", "y", "core"))
+    dp, space = ("xhi", "xlo", "zlo"), ("zhi", "y", "core")
     specs = (P(dp, space, None), P(dp, space, None), P(dp, None), P(dp, None), P(dp, None))
 
     return jax.shard_map(body, mesh=fine, in_specs=specs, out_specs=specs, check_vma=False)

time: 77.1 us -> 76.9 us (level)
  no operation moved by 1% of the time
where the time goes in v10:
time: 76.9 us; the launch traced here: 76.5 us
  blocking collectives  40 us (52%)
  starting transfers between devices  27.3 us (36%)
  Pallas kernels  5.4 us (7%)
  waiting for transfers between devices  3.18 us (4%)
    all_to_all x1, blocking collectives, body(): got_two = lax.all_to_all(send_two, ('zlo', 'zhi'), 0, 0, tiled=True)  18.1 us
    all_to_all x1, blocking collectives, body(): got_three = lax.all_to_all(send_three, ('y', 'core'), 0, 0, tiled=True)  14 us
    ppermute x1, starting transfers between devices, body(): other = lax.ppermute(got_two, 'core', [(0, 1), (1, 0)])  13 us
    ppermute x1, starting transfers between devices, body(): given = lax.ppermute(give, 'core', [(0, 1), (1, 0)])  12.4 us
    all_to_all x1, blocking collectives, body(): got_one = lax.all_to_all(send_one, ('xlo', 'xhi'), 0, 0, tiled=True)  7.93 us
    ppermute x1, waiting for transfers between devices, body(): traded = lax.ppermute(trade, ('zhi', 'y', 'core'), route)  3.17 us
    pallas_call x1, Pallas kernels, body(): call(conv_kernel, [shape((4, 32 * C), BF16), shape((8, 64 * C), BF16)], [...  1.98 us
    ppermute x1, starting transfers between devices, body(): traded = lax.ppermute(trade, ('zhi', 'y', 'core'), route)  1.92 us
  transfers between devices with their start and end apart: 3, of which 1 were waited for; matrix products, arithmetic and copies ran while one was open for 0% of the time, Pallas kernels for 1%

profile of v10, /device:TPU:1, one launch (start us, length us, event | category | flops | bytes accessed | tf_op | source)
XLA Modules:
  0.0 76.5 jit_solution(3816607884171675798)
XLA Ops:
  0.6 1.3 %shard_map.92 = (bf16[256,160]{1,0:T(8,128)(2,1)S(1)}, bf16[256,160]{1,0:T(8,128)(2,1)S(1)}, bf16[4,5120]{1,0:T(4,128)(2,1)S(1)}, bf16[32,128]{1,0:T(8,128)(2,1)...) custom-call(bf16[8,10240]{1,0:T(8,128)(2,1)} %bitcast.4, bf16[4,5120]{1,0:T(4,128)(2,1)} %bitcast.5, ...), custom_call_target="tpu_custom_call" | custom-call | tf_op jit(solution)/shard_map/pallas_call | solution.py:330
  2.0 0.8 %shard_map.93 = (bf16[4,240,128]{2,1,0:T(8,128)(2,1)S(1)}, bf16[4,280,128]{2,1,0:T(8,128)(2,1)S(1)}, bf16[3,256,160]{2,1,0:T(8,128)(2,1)S(1)}) custom-call(bf16[256,160]{1,0:T(8,128)(2,1)S(1)} %get-tuple-element.22.even_ref, bf16[256,160]{1,0:T(8,128)(2,1)S(1)} %get-tuple-element.23.odd_ref, bf16[4,5120]{1,0:T(4,128)(2,1)S(1)} %get-tuple-element.24.cotan_ref, ...), custom_call_target="tpu_custom_call" | custom-call | tf_op jit(solution)/shard_map/pallas_call | solution.py:350
  2.8 12.4 %collective-permute-start = (bf16[4,280,128]{2,1,0:T(8,128)(2,1)S(1)}, bf16[4,280,128]{2,1,0:T(8,128)(2,1)S(1)}, u32[]{:S(2)}, u32[]{:S(2)}) collective-permute-start(bf16[4,280,128]{2,1,0:T(8,128)(2,1)S(1)} %get-tuple-element.28), channel_id=1, source_target_pairs={{0,1},{1,0},{2,3},{3,2},{4,5},{5,4},{6,7},{7,6},{8,9},{9,8},{10,11... | collective-permute-start | bytes 860168 | tf_op jit(solution)/shard_map/ppermute | solution.py:363
  15.2 1.9 %collective-permute-start.1 = (bf16[2,40,128]{2,1,0:T(8,128)(2,1)S(1)}, bf16[2,40,128]{2,1,0:T(8,128)(2,1)S(1)}, u32[]{:S(2)}, u32[]{:S(2)}) collective-permute-start(bf16[2,40,128]{2,1,0:T(8,128)(2,1)S(1)} %get-tuple-element.30), channel_id=1, source_target_pairs={{1,2},{2,1},{3,4},{4,3},{5,6},{6,5},{7,8},{8,7},{9,10},{10,9},{11,... | collective-permute-start | bytes 61448 | tf_op jit(solution)/shard_map/ppermute | solution.py:349
  17.1 3.2 %collective-permute-done.1.trade_ref = bf16[2,40,128]{2,1,0:T(8,128)(2,1)S(1)} collective-permute-done((bf16[2,40,128]{2,1,0:T(8,128)(2,1)S(1)}, bf16[2,40,128]{2,1,0:T(8,128)(2,1)S(1)}, u32[]{:S(2)}, u32[]{:S(2)}) %collective-permute-start.1) | collective-permute-done | bytes 20512 | tf_op jit(solution)/shard_map/ppermute | solution.py:349
  20.3 0.0 collective-permute-done.got_ref
  20.3 0.4 shard_map.94
  20.7 7.9 %all_to_all.15.got_ref = bf16[4,272,128]{2,1,0:T(8,128)(2,1)S(1)} all-to-all(bf16[4,272,128]{2,1,0:T(8,128)(2,1)S(1)} %get-tuple-element.33), channel_id=1, replica_groups=mesh['xhi'=2,'xlo'=2,'zlo'=6,'zhi'=2,'y'=8,'core'=2] {'xlo','xhi'}, dimensions={0} | all-to-all | bytes 557056 | tf_op jit(solution)/shard_map/all_to_all | solution.py:369
  28.6 0.1 shard_map.95
  28.7 18.1 %all_to_all.16.own_ref.got_ref = bf16[12,120,128]{2,1,0:T(8,128)(2,1)S(1)} all-to-all(bf16[12,120,128]{2,1,0:T(8,128)(2,1)S(1)} %shard_map.95), channel_id=1, replica_groups=mesh['xhi'=2,'xlo'=2,'zlo'=6,'zhi'=2,'y'=8,'core'=2] {'zlo','zhi'}, dimensions={0} | all-to-all | bytes 737280 | tf_op jit(solution)/shard_map/all_to_all | solution.py:371
  46.7 13.0 %collective-permute-start.2 = (bf16[12,120,128]{2,1,0:T(8,128)(2,1)S(1)}, bf16[12,120,128]{2,1,0:T(8,128)(2,1)S(1)}, u32[]{:S(2)}, u32[]{:S(2)}) collective-permute-start(bf16[12,120,128]{2,1,0:T(8,128)(2,1)S(1)} %all_to_all.16.own_ref.got_ref), channel_id=1, source_target_pairs={{0,1},{1,0},{2,3},{3,2},{4,5},{5,4},{6,7},{7,6},{8,9},{9,8},{10,11... | collective-permute-start | bytes 1105928 | tf_op jit(solution)/shard_map/ppermute | solution.py:372
  59.7 0.0 copy-start
  59.8 0.0 copy-start.1
  59.8 0.0 copy-start.2
  59.8 14.0 %all_to_all.17.got_ref = bf16[16,40,128]{2,1,0:T(8,128)(2,1)S(1)} all-to-all(bf16[16,40,128]{2,1,0:T(8,128)(2,1)S(1)} %shard_map.97), channel_id=1, replica_groups=mesh['xhi'=2,'xlo'=2,'zlo'=6,'zhi'=2,'y'=8,'core'=2] {'y','core'}, dimensions={0} | all-to-all | bytes 327680 | tf_op jit(solution)/shard_map/all_to_all | solution.py:374
  73.8 0.0 copy-done
  73.8 0.0 copy-done.1
  73.8 0.0 copy-done.2
  73.8 0.8 %shard_map.98 = (f32[60,160]{1,0:T(8,128)}, f32[60,160]{1,0:T(8,128)}, f32[60,160]{1,0:T(8,128)}) custom-call(bf16[16,40,128]{2,1,0:T(8,128)(2,1)S(1)} %all_to_all.17.got_ref, f32[60,160]{1,0:T(8,128)S(1)} %copy-done, f32[60,160]{1,0:T(8,128)S(1)} %copy-done.1, f32[60,160]{1,0:T(8,128)S(1)} %copy-done.2), custom_call_target="tpu_custom_call" | custom-call | tf_op jit(solution)/shard_map/pallas_call | solution.py:384
  74.6 0.0 collective-permute-done.2.other_ref
  74.6 2.0 %shard_map.96 = (bf16[4,5120]{1,0:T(4,128)(2,1)}, bf16[8,10240]{1,0:T(8,128)(2,1)}) custom-call(bf16[256,160]{1,0:T(8,128)(2,1)S(1)} %get-tuple-element.22.even_ref, bf16[256,160]{1,0:T(8,128)(2,1)S(1)} %get-tuple-element.23.odd_ref, bf16[3,256,160]{2,1,0:T(8,128)(2,1)S(1)} %get-tuple-element.26.taps_ref, bf16[32,160]{1,0:T(8,128)(2,1)S(1)} %get-tuple-element.31.below_ref, ...), custom_call_target="tpu_custom_call" | custom-call | tf_op jit(solution)/shard_map/pallas_call | solution.py:375
  (1 shorter events, 0.0 us)
Async XLA Ops:
  2.8 17.5 %collective-permute-start = (bf16[4,280,128]{2,1,0:T(8,128)(2,1)S(1)}, bf16[4,280,128]{2,1,0:T(8,128)(2,1)S(1)}, u32[]{:S(2)}, u32[]{:S(2)}) collective-permute-start(bf16[4,280,128]{2,1,0:T(8,128)(2,1)S(1)} %get-tuple-element.28), channel_id=1, source_target_pairs={{0,1},{1,0},{2,3},{3,2},{4,5},{5,4},{6,7},{7,6},{8,9},{9,8},{10,11... | collective-permute-start | bytes 860168 | tf_op jit(solution)/shard_map/ppermute | solution.py:363
  15.2 5.1 %collective-permute-start.1 = (bf16[2,40,128]{2,1,0:T(8,128)(2,1)S(1)}, bf16[2,40,128]{2,1,0:T(8,128)(2,1)S(1)}, u32[]{:S(2)}, u32[]{:S(2)}) collective-permute-start(bf16[2,40,128]{2,1,0:T(8,128)(2,1)S(1)} %get-tuple-element.30), channel_id=1, source_target_pairs={{1,2},{2,1},{3,4},{4,3},{5,6},{6,5},{7,8},{8,7},{9,10},{10,9},{11,... | collective-permute-start | bytes 61448 | tf_op jit(solution)/shard_map/ppermute | solution.py:349
  46.7 27.8 %collective-permute-start.2 = (bf16[12,120,128]{2,1,0:T(8,128)(2,1)S(1)}, bf16[12,120,128]{2,1,0:T(8,128)(2,1)S(1)}, u32[]{:S(2)}, u32[]{:S(2)}) collective-permute-start(bf16[12,120,128]{2,1,0:T(8,128)(2,1)S(1)} %all_to_all.16.own_ref.got_ref), channel_id=1, source_target_pairs={{0,1},{1,0},{2,3},{3,2},{4,5},{5,4},{6,7},{7,6},{8,9},{9,8},{10,11... | collective-permute-start | bytes 1105928 | tf_op jit(solution)/shard_map/ppermute | solution.py:372
  59.7 14.0 %copy-start = (f32[60,160]{1,0:T(8,128)S(1)}, f32[60,160]{1,0:T(8,128)}, u32[]{:S(2)}) copy-start(f32[60,160]{1,0:T(8,128)} %weight_ref.1) | copy-start | bytes 115204
  59.8 14.0 %copy-start.1 = (f32[60,160]{1,0:T(8,128)S(1)}, f32[60,160]{1,0:T(8,128)}, u32[]{:S(2)}) copy-start(f32[60,160]{1,0:T(8,128)} %one_ref.1) | copy-start | bytes 115204
  59.8 14.0 %copy-start.2 = (f32[60,160]{1,0:T(8,128)S(1)}, f32[60,160]{1,0:T(8,128)}, u32[]{:S(2)}) copy-start(f32[60,160]{1,0:T(8,128)} %two_ref.1) | copy-start | bytes 115204
